TPU v7x, 512 devices: a whole 4x4x16 slice. The times are simulated.
512 devices in a mesh: dp: 32 (over y_lo, z), tensor: 16 (over y_hi, x, core).
Axes of the slice: x: 4, y: 4 (y_hi: 2, y_lo: 2; y = y_hi * 2 + y_lo), z: 16, core: 2. Of those that a mesh axis runs over, the one named last changes fastest.
Arguments:
- inputs: bfloat16 [8192, 6144], P('dp', 'tensor'), may hold values from -250 to 250
- upstream: bfloat16 [8192, 4096], P('dp', 'tensor'), may hold values from -6 to 6
- proj_weight: bfloat16 [6144, 4096], P(None, 'tensor'), may hold values from -0.078125 to 0.078125
- proj_bias: float32 [4096], P('tensor'), may hold values from -4 to 4
- norm_gain: float32 [6144], replicated, may hold values from 0.1 to 1.9
- home_rows: int32 [8192], P('dp'), may hold values from 0 to 8191, as said below
Outputs:
- home_grad: bfloat16 [8192, 6144], P('dp', 'tensor')
Inputs may be any that keep to these rules, and one draw needn't show every extreme that they name: `home_rows`: A permutation of 0 to 8191. The balanced row at position i * 256 + k goes to a home row j * 256 + s (0 <= s < 256); of the 256 rows of one dp index, at most 16 have the same owner j, and in every draw some do.
All inputs are finite; a program needn't handle non-finite values.
Results may differ from a plain program's by a relative error of at most 0.018.
Values may be sent and summed in bfloat16 or wider, within the bound.
No kernel may reach another device: no remote copies, remote signals or barrier semaphores. Data moves between devices by JAX's collectives and lax.ppermute only.
A program may use at most 64 MiB of HBM per device.

v0:
```python
import jax
import jax.numpy as jnp
from jax import lax
from jax.sharding import PartitionSpec as P

epsilon = 1e-05


def contract_cols(left, right):
    return lax.dot_general(
        left, right, (((1,), (1,)), ((), ())), preferred_element_type=jnp.float32
    )


def per_device(inputs, upstream, proj_weight, proj_bias, norm_gain, home_rows):
    gathered = lax.all_gather(inputs, "tensor", axis=1, tiled=True).astype(jnp.float32)
    row_mean = jnp.mean(gathered, axis=1, keepdims=True)
    centred = gathered - row_mean
    inv_std = lax.rsqrt(jnp.mean(centred * centred, axis=1, keepdims=True) + epsilon)
    unit_rows = centred * inv_std
    normed = (unit_rows * norm_gain[None, :]).astype(jnp.bfloat16)
    preact = jnp.dot(normed, proj_weight, preferred_element_type=jnp.float32) + proj_bias[None, :]
    gate_value = jax.nn.sigmoid(preact)
    pre_grad = (
        upstream.astype(jnp.float32) * gate_value * (1.0 + preact * (1.0 - gate_value))
    ).astype(jnp.bfloat16)
    row_total = upstream.shape[0]
    block_rows = row_total // lax.axis_size("tensor")
    first_row = lax.axis_index("tensor") * block_rows
    summed = lax.psum(contract_cols(pre_grad, proj_weight).astype(jnp.bfloat16), "tensor").astype(
        jnp.float32
    )
    mine = lax.dynamic_slice_in_dim(summed, first_row, block_rows, 0)
    own_unit = lax.dynamic_slice_in_dim(unit_rows, first_row, block_rows, 0)
    own_scale = lax.dynamic_slice_in_dim(inv_std, first_row, block_rows, 0)
    scaled = mine * norm_gain[None, :]
    input_grad = (
        own_scale
        * (
            scaled
            - jnp.mean(scaled, axis=1, keepdims=True)
            - own_unit * jnp.mean(scaled * own_unit, axis=1, keepdims=True)
        )
    ).astype(jnp.bfloat16)
    column_rows = lax.all_to_all(input_grad, "tensor", split_axis=1, concat_axis=0, tiled=True)
    owners = lax.axis_size("dp")
    capacity = max(2, 2 * row_total // owners)
    owner_of = home_rows // row_total
    home_slot = home_rows % row_total
    order_ids = jnp.arange(row_total, dtype=jnp.int32)
    earlier = jnp.sum(
        (
            (owner_of[:, None] == owner_of[None, :]) & (order_ids[:, None] > order_ids[None, :])
        ).astype(jnp.int32),
        axis=1,
    )
    target = owner_of * capacity + earlier
    placing = jnp.arange(owners * capacity, dtype=jnp.int32)[:, None] == target[None, :]
    send_rows = jnp.dot(
        placing.astype(jnp.bfloat16), column_rows, preferred_element_type=jnp.float32
    ).astype(jnp.bfloat16)
    send_slots = (jnp.sum(jnp.where(placing, home_slot[None, :] + 1, 0), axis=1) - 1)[:, None]
    arrived, arrived_slots = (
        lax.all_to_all(send_rows, "dp", split_axis=0, concat_axis=0, tiled=True),
        lax.all_to_all(send_slots, "dp", split_axis=0, concat_axis=0, tiled=True),
    )
    landing = order_ids[:, None] == arrived_slots[None, :, 0]
    return jnp.dot(
        landing.astype(jnp.bfloat16), arrived, preferred_element_type=jnp.float32
    ).astype(jnp.bfloat16)


def solution(mesh):
    return jax.shard_map(
        per_device,
        mesh=mesh,
        in_specs=(
            P("dp", "tensor"),
            P("dp", "tensor"),
            P(None, "tensor"),
            P("tensor"),
            P(),
            P("dp"),
        ),
        out_specs=P("dp", "tensor"),
        check_vma=False,
    )
```

profile of v0, /device:TPU:1, one launch (start us, length us, event | category | flops | bytes accessed | tf_op | source)
XLA Modules:
  0.0 337.9 jit_solution(17952135256464665378)
XLA Ops:
  6.5 0.0 copy-start
  6.5 0.0 copy-start.1
  6.5 0.0 copy-start.3
  6.5 0.0 copy-start.4
  6.5 0.0 all-gather.2.cloned.1.call-start
  6.6 0.7 all-gather.2.cloned.1.call-update
  7.3 0.0 all-reduce.2.cloned.1.call-start
  7.3 78.1 %all-gather.2.cloned.1.call-done = bf16[256,6144]{1,0:T(8,128)(2,1)} async-done(((bf16[256,384]{1,0:T(8,128)(2,1)}), bf16[256,6144]{1,0:T(8,128)(2,1)}) %all-gather.2.cloned.1.call-update) | async-done | bytes 3145744 | tf_op jit(solution)/shard_map/all_gather | solution.py:16
  85.4 2.4 convert_reduce_fusion
  87.8 2.9 fusion.2
  90.7 0.0 copy-done
  90.7 0.0 copy-done.1
  90.7 0.0 copy-done.3
  90.7 0.0 copy-done.4
  90.8 0.0 copy-start.2
  90.8 7.1 %convolution_convert_fusion = bf16[256,6144]{1,0:T(8,128)(2,1)} fusion(bf16[6144,256]{1,0:T(8,128)(2,1)S(1)} %copy-done, f32[6144]{0:T(1024)S(1)} %copy-done.1, bf16[256,256]{1,0:T(8,128)(2,1)S(1)} %copy-done.3, f32[256]{0:T(256)S(1)} %copy-done.4, bf16[256,6144]{1,0:T(8,128)(2,1)} %all-gather.2.cloned.1.call-done, f32[256]{0:T(256)S(1)} %add_rsqrt_fusion, ...), kind=kOutput, calls=%fused_computation.2 | convolution fusion | flops 1620770816 | bytes 9595904 | tf_op jit(solution)/shard_map/dot_general | solution.py:10
  97.9 0.0 all-reduce.2.cloned.1.call-update
  97.9 0.0 copy-done.2
  97.9 0.2 convert_reduce_fusion.1
  98.1 0.2 select_reduce_fusion
  98.3 0.1 dynamic-slice.3
  98.3 5.7 %fusion = f32[256,6144]{1,0:T(8,128)} fusion(bf16[256,6144]{1,0:T(8,128)(2,1)} %all-gather.2.cloned.1.call-done, f32[256]{0:T(256)S(1)} %add_rsqrt_fusion, f32[256]{0:T(256)S(1)} %broadcast_multiply_fusion), kind=kLoop, calls=%fused_computation.3 | loop fusion | flops 4718592 | bytes 9439232 | tf_op jit(solution)/shard_map/mul | solution.py:20
  104.0 154.8 %all-reduce.2.cloned.1.call-done = bf16[256,6144]{1,0:T(8,128)(2,1)} async-done(((bf16[256,6144]{1,0:T(8,128)(2,1)}), bf16[256,6144]{1,0:T(8,128)(2,1)}) %all-reduce.2.cloned.1.call-update) | async-done | bytes 3145744 | tf_op jit(solution)/shard_map/psum | solution.py:30
  258.8 1.3 fusion.6
  260.1 1.2 multiply_convert_fusion.4
  261.2 0.7 copy.14
  261.9 7.5 %all-to-all-start.1 = ((bf16[16,16,384]{2,0,1:T(8,128)(2,1)}), bf16[16,16,384]{2,0,1:T(8,128)(2,1)S(1)}, u32[]{:S(2)}, u32[]{:S(2)}) async-start(bf16[16,16,384]{2,0,1:T(8,128)(2,1)} %bitcast.14), calls=%async_computation.1 | async-start | bytes 393216 | tf_op jit(solution)/shard_map/all_to_all | solution.py:45
  269.4 0.7 sub.36
  270.1 7.4 %all-to-all-done.1 = bf16[16,16,384]{2,0,1:T(8,128)(2,1)S(1)} async-done(((bf16[16,16,384]{2,0,1:T(8,128)(2,1)}), bf16[16,16,384]{2,0,1:T(8,128)(2,1)S(1)}, u32[]{:S(2)}, u32[]{:S(2)}) %all-to-all-start.1) | async-done | bytes 196640 | tf_op jit(solution)/shard_map/all_to_all | solution.py:45
  277.5 12.3 %all-to-all-start = ((s32[32,16,1]{1,2,0:T(1,128)}), s32[32,16,1]{1,2,0:T(1,128)S(1)}, u32[]{:S(2)}, u32[]{:S(2)}) async-start(s32[32,16,1]{1,2,0:T(1,128)} %bitcast), calls=%async_computation | async-start | bytes 32768 | tf_op jit(solution)/shard_map/all_to_all | solution.py:65
  289.9 1.0 convolution_convert_fusion.1
  290.9 11.1 %all-to-all-done = s32[32,16,1]{1,2,0:T(1,128)S(1)} async-done(((s32[32,16,1]{1,2,0:T(1,128)}), s32[32,16,1]{1,2,0:T(1,128)S(1)}, u32[]{:S(2)}, u32[]{:S(2)}) %all-to-all-start) | async-done | bytes 2080 | tf_op jit(solution)/shard_map/all_to_all | solution.py:65
  302.1 3.9 %all-to-all-start.2 = ((bf16[32,16,384]{2,1,0:T(8,128)(2,1)}), bf16[32,16,384]{2,1,0:T(8,128)(2,1)S(1)}, u32[]{:S(2)}, u32[]{:S(2)}) async-start(bf16[32,16,384]{2,1,0:T(8,128)(2,1)} %bitcast.3), calls=%async_computation.2 | async-start | bytes 786432 | tf_op jit(solution)/shard_map/all_to_all | solution.py:64
  305.9 0.6 broadcast.124
  306.5 1.3 reduce.3
  307.8 0.8 eq.50
  308.6 21.5 %all-to-all-done.2 = bf16[32,16,384]{2,1,0:T(8,128)(2,1)S(1)} async-done(((bf16[32,16,384]{2,1,0:T(8,128)(2,1)}), bf16[32,16,384]{2,1,0:T(8,128)(2,1)S(1)}, u32[]{:S(2)}, u32[]{:S(2)}) %all-to-all-start.2) | async-done | bytes 393248 | tf_op jit(solution)/shard_map/all_to_all | solution.py:64
  330.1 1.0 convolution_convert_fusion.2
  (6 shorter events, 0.0 us)
Async XLA Ops:
  6.5 84.2 %copy-start = (bf16[6144,256]{1,0:T(8,128)(2,1)S(1)}, bf16[6144,256]{1,0:T(8,128)(2,1)}, u32[]{:S(2)}) copy-start(bf16[6144,256]{1,0:T(8,128)(2,1)} %param.8) | copy-start | bytes 9437188
  6.5 84.2 %copy-start.1 = (f32[6144]{0:T(1024)S(1)}, f32[6144]{0:T(1024)}, u32[]{:S(2)}) copy-start(f32[6144]{0:T(1024)} %param.10) | copy-start | bytes 73732
  6.5 84.2 %copy-start.3 = (bf16[256,256]{1,0:T(8,128)(2,1)S(1)}, bf16[256,256]{1,0:T(8,128)(2,1)}, u32[]{:S(2)}) copy-start(bf16[256,256]{1,0:T(8,128)(2,1)} %param.7) | copy-start | bytes 393220
  6.5 84.2 %copy-start.4 = (f32[256]{0:T(256)S(1)}, f32[256]{0:T(256)}, u32[]{:S(2)}) copy-start(f32[256]{0:T(256)} %param.9) | copy-start | bytes 3076
  6.5 78.9 %all-gather.2.cloned.1.call-start = ((), (), s32[]{:S(2)}) async-start(), calls=%async_computation.3 | async-start | bytes 3342336 | tf_op jit(solution)/shard_map/all_gather | solution.py:16
  7.3 251.5 %all-reduce.2.cloned.1.call-start = ((), (), s32[]{:S(2)}) async-start(), calls=%async_computation.4 | async-start | bytes 6291456 | tf_op jit(solution)/shard_map/psum | solution.py:30
  90.8 7.1 %copy-start.2 = (s32[256]{0:T(256)S(1)}, s32[256]{0:T(256)}, u32[]{:S(2)}) copy-start(s32[256]{0:T(256)} %param.11) | copy-start | bytes 3076
  261.9 15.6 %all-to-all-start.1 = ((bf16[16,16,384]{2,0,1:T(8,128)(2,1)}), bf16[16,16,384]{2,0,1:T(8,128)(2,1)S(1)}, u32[]{:S(2)}, u32[]{:S(2)}) async-start(bf16[16,16,384]{2,0,1:T(8,128)(2,1)} %bitcast.14), calls=%async_computation.1 | async-start | bytes 393216 | tf_op jit(solution)/shard_map/all_to_all | solution.py:45
  277.5 24.5 %all-to-all-start = ((s32[32,16,1]{1,2,0:T(1,128)}), s32[32,16,1]{1,2,0:T(1,128)S(1)}, u32[]{:S(2)}, u32[]{:S(2)}) async-start(s32[32,16,1]{1,2,0:T(1,128)} %bitcast), calls=%async_computation | async-start | bytes 32768 | tf_op jit(solution)/shard_map/all_to_all | solution.py:65
  302.1 28.0 %all-to-all-start.2 = ((bf16[32,16,384]{2,1,0:T(8,128)(2,1)}), bf16[32,16,384]{2,1,0:T(8,128)(2,1)S(1)}, u32[]{:S(2)}, u32[]{:S(2)}) async-start(bf16[32,16,384]{2,1,0:T(8,128)(2,1)} %bitcast.3), calls=%async_computation.2 | async-start | bytes 786432 | tf_op jit(solution)/shard_map/all_to_all | solution.py:64
Sparse Core Ops, SparseCore 0:
  10.5 74.9 all-gather.1
  98.0 160.7 all-reduce.1
where the time goes:
time: 340 us; the launch traced here: 338 us
  waiting for transfers between devices  274 us (81%)
  starting transfers between devices  23.7 us (7%)
  other arithmetic  15 us (4%)
  between operations  13.5 us (4%)
  matrix products  9.13 us (3%)
    psum x1, waiting for transfers between devices, per_device(): lax.psum(contract_cols(pre_grad, proj_weight).astype(jnp.bfloat16), 'tens...  155 us
    all_gather x1, waiting for transfers between devices, per_device(): lax.all_gather(inputs, 'tensor', axis=1, tiled=True).astype(jnp.float32)  78.1 us
    all_to_all x1, waiting for transfers between devices, per_device(): lax.all_to_all(send_rows, 'dp', split_axis=0, concat_axis=0, tiled=True)  21.5 us
    all_to_all x1, starting transfers between devices, per_device(): lax.all_to_all(send_slots, 'dp', split_axis=0, concat_axis=0, tiled=True)  12.3 us
    all_to_all x1, waiting for transfers between devices, per_device(): lax.all_to_all(send_slots, 'dp', split_axis=0, concat_axis=0, tiled=True)  11.1 us
    all_to_all x1, starting transfers between devices, per_device(): lax.all_to_all(input_grad, 'tensor', split_axis=1, concat_axis=0, tiled=T...  7.48 us
    all_to_all x1, waiting for transfers between devices, per_device(): lax.all_to_all(input_grad, 'tensor', split_axis=1, concat_axis=0, tiled=T...  7.44 us
    dot_general x1, matrix products, contract_cols(): lax.dot_general(left, right, (((1,), (1,)), ((), ())), preferred_element_...  7.1 us
  transfers between devices with their start and end apart: 5, of which 5 were waited for; matrix products, arithmetic and copies ran while one was open for 3% of the time, Pallas kernels for 0%

commit v1 on v0

v1 whole, which is shorter than its diff:
```python
import jax
import jax.numpy as jnp
from jax import lax
from jax.experimental import pallas as pl
from jax.experimental.pallas import tpu as pltpu
from jax.sharding import PartitionSpec as P

epsilon = 1e-05
f32, bf16 = jnp.float32, jnp.bfloat16
PAD = 16
NT = (((1,), (1,)), ((), ()))


def in_vmem(n):
    return [pl.BlockSpec(memory_space=pltpu.VMEM) for _ in range(n)]


SCALAR = pl.BlockSpec(memory_space=pltpu.SMEM)


def forward_kernel(core_ref, x_ref, gain_ref, weight_ref, other_ref, q_ref):
    blocks, rows, feats = x_ref.shape
    width = other_ref.shape[2]
    core = core_ref[0]
    total = jnp.zeros((rows, 1), f32)
    for b in range(blocks):
        total += jnp.sum(x_ref[b].astype(f32), axis=1, keepdims=True)
    mean = total / (blocks * feats)
    spread = jnp.zeros((rows, 1), f32)
    own = jnp.zeros((rows, width), f32)
    other = jnp.zeros((rows, width), f32)
    for b in range(blocks):
        centred = x_ref[b].astype(f32) - mean
        spread += jnp.sum(centred * centred, axis=1, keepdims=True)
        scaled = (centred * gain_ref[b, core]).astype(bf16)
        own += jnp.dot(scaled, weight_ref[b, core], preferred_element_type=f32)
        other += jnp.dot(scaled, other_ref[b], preferred_element_type=f32)
    q_ref[:, :width] = own
    q_ref[:, width : 2 * width] = other
    lane = lax.broadcasted_iota(jnp.int32, (rows, 128), 1)
    q_ref[:, 2 * width :] = jnp.where(lane == 0, mean, spread / (blocks * feats))


def forward(core, x, gain, weight, other):
    blocks, rows, feats = x.shape
    width = other.shape[2]
    return pl.pallas_call(
        forward_kernel,
        in_specs=[SCALAR] + in_vmem(4),
        out_specs=in_vmem(1)[0],
        out_shape=jax.ShapeDtypeStruct((rows, 2 * width + 128), f32),
        name="forward",
    )(core, x, gain, weight, other)


def backward_kernel(
    core_ref, q_ref, got_ref, up_ref, upo_ref, vec_ref, veco_ref, weight_ref, other_ref, p_ref, st_ref
):
    blocks, feats, width = other_ref.shape
    rows = q_ref.shape[0]
    core = core_ref[0]
    mine, theirs = q_ref[:, 2 * width :], got_ref[:, 2 * width :]
    mean_here, mean_there = mine[:, 0:1], theirs[:, 0:1]
    gap = 0.5 * (mean_here - mean_there)
    mean = 0.5 * (mean_here + mean_there)
    variance = 0.5 * (mine[:, 1:2] + theirs[:, 1:2]) + gap * gap
    inv_std = lax.rsqrt(variance + epsilon)
    lane = lax.broadcasted_iota(jnp.int32, (rows, 128), 1)
    st_ref[...] = jnp.where(lane == 0, mean, inv_std)
    side = jnp.where(core == 0, 1.0, -1.0)

    def grad(summed, up, vec):
        raw = inv_std * (summed + gap * (side * (vec[1:2, :] - vec[2:3, :])))
        preact = raw + vec[0:1, :]
        gate = 1.0 / (1.0 + jnp.exp(-preact))
        pg = (up.astype(f32) * gate * (1.0 + preact * (1.0 - gate))).astype(bf16)
        wide = pg.astype(f32)
        scale = jnp.broadcast_to(vec[1:2, :] + vec[2:3, :], (8, width))
        first = lax.dot_general(scale, wide, NT, precision=lax.Precision.HIGHEST)
        second = lax.dot_general(
            jnp.ones((8, width), f32), wide * raw, NT, precision=lax.Precision.HIGHEST
        )
        return pg, first, second

    pg, first, second = grad(q_ref[:, :width] + got_ref[:, width : 2 * width], up_ref[...], vec_ref[...])
    pgo, firsto, secondo = grad(
        q_ref[:, width : 2 * width] + got_ref[:, :width], upo_ref[...], veco_ref[...]
    )
    first, second = first + firsto, second + secondo
    row = lax.broadcasted_iota(jnp.int32, (8, rows), 0)
    value = jnp.where(row < 2, first, second)
    high = value.astype(bf16).astype(f32)
    tail = jnp.where(row % 2 == 0, high, value - high)
    tail = jnp.concatenate([tail, jnp.zeros_like(tail)], axis=0).astype(bf16)
    tail = jnp.concatenate([tail, jnp.zeros((PAD, feats - rows), bf16)], axis=1)
    for b in range(blocks):
        p_ref[b, :rows] = (
            lax.dot_general(pg, weight_ref[b, core], NT, preferred_element_type=f32)
            + lax.dot_general(pgo, other_ref[b], NT, preferred_element_type=f32)
        ).astype(bf16)
        p_ref[b, rows:] = tail


def backward(core, q, got, up, upo, vec, veco, weight, other):
    blocks, feats, width = other.shape
    rows = q.shape[0]
    return pl.pallas_call(
        backward_kernel,
        in_specs=[SCALAR] + in_vmem(8),
        out_specs=in_vmem(2),
        out_shape=[
            jax.ShapeDtypeStruct((blocks, rows + PAD, feats), bf16),
            jax.ShapeDtypeStruct((rows, 128), f32),
        ],
        name="backward",
    )(core, q, got, up, upo, vec, veco, weight, other)


def finish_kernel(back_ref, x_ref, st_ref, gain_ref, target_ref, send_ref):
    blocks = back_ref.shape[0]
    rows, feats = x_ref.shape
    slots = send_ref.shape[0]
    total = back_ref[0].astype(f32)
    for b in range(1, blocks):
        total += back_ref[b].astype(f32)
    tail = total[rows : rows + 8, :rows]
    sums = tail.T / (2 * blocks * feats)
    first = sums[:, 0:1] + sums[:, 1:2]
    second = sums[:, 2:3] + sums[:, 3:4]
    mean, inv_std = st_ref[:, 0:1], st_ref[:, 1:2]
    unit = (x_ref[...].astype(f32) - mean) * inv_std
    grad = (inv_std * (total[:rows] * gain_ref[...] - first - unit * second)).astype(bf16)
    placing = lax.broadcasted_iota(jnp.int32, (slots, rows), 0) == target_ref[...]
    send_ref[...] = jnp.dot(
        jnp.where(placing, 1.0, 0.0).astype(bf16), grad, preferred_element_type=f32
    ).astype(bf16)


def finish(back, x, st, gain, target, slots):
    return pl.pallas_call(
        finish_kernel,
        in_specs=in_vmem(5),
        out_specs=in_vmem(1)[0],
        out_shape=jax.ShapeDtypeStruct((slots, x.shape[1]), bf16),
        name="finish",
    )(back, x, st, gain, target)


def landing_kernel(got_ref, slot_ref, o_ref):
    rows = o_ref.shape[0]
    slots = got_ref.shape[0]
    landing = lax.broadcasted_iota(jnp.int32, (rows, slots), 0) == slot_ref[...]
    o_ref[...] = jnp.dot(
        jnp.where(landing, 1.0, 0.0).astype(bf16), got_ref[...], preferred_element_type=f32
    ).astype(bf16)


def land(got, slot, rows):
    return pl.pallas_call(
        landing_kernel,
        in_specs=in_vmem(2),
        out_specs=in_vmem(1)[0],
        out_shape=jax.ShapeDtypeStruct((rows, got.shape[1]), bf16),
        name="land",
    )(got, slot)


def per_device(inputs, upstream, proj_weight, proj_bias, norm_gain, home_rows):
    rows, feats = inputs.shape
    width = upstream.shape[1]
    n_tensor, owners = lax.axis_size("tensor"), lax.axis_size("dp")
    chips = n_tensor // 2
    me = lax.axis_index("tensor")
    core = me % 2
    swap = [(t, t ^ 1) for t in range(n_tensor)]
    classes = [[2 * k + c for k in range(chips)] for c in range(2)]
    core_arr = core.reshape(1).astype(jnp.int32)

    sent = jnp.broadcast_to(inputs[None], (chips, rows, feats))
    half = lax.all_to_all(sent, "tensor", 0, 0, axis_index_groups=classes, tiled=True)

    pairs = proj_weight.reshape(chips, 2, feats, width)
    other = lax.ppermute(lax.dynamic_index_in_dim(pairs, 1 - core, 1, False), "tensor", swap)
    upo = lax.ppermute(upstream, "tensor", swap)
    gains = norm_gain.reshape(chips, 2, 1, feats)
    scales = jnp.sum(norm_gain.reshape(chips, 2, feats, 1) * pairs.astype(f32), axis=(0, 2))
    vec = jnp.concatenate([proj_bias[None], scales], axis=0)
    veco = lax.ppermute(vec, "tensor", swap)

    capacity = max(2, 2 * rows // owners)
    owner_of = home_rows // rows
    home_slot = home_rows % rows
    order_ids = jnp.arange(rows, dtype=jnp.int32)
    earlier = jnp.sum(
        ((owner_of[:, None] == owner_of[None, :]) & (order_ids[:, None] > order_ids[None, :])).astype(
            jnp.int32
        ),
        axis=1,
    )
    target = owner_of * capacity + earlier
    placing = jnp.arange(owners * capacity, dtype=jnp.int32)[:, None] == target[None, :]
    send_slots = jnp.sum(jnp.where(placing, home_slot[None, :] + 1, 0), axis=1) - 1
    arrived_slots = lax.all_to_all(
        send_slots.reshape(owners, 1, capacity), "dp", split_axis=0, concat_axis=0, tiled=True
    ).reshape(1, -1)

    half, other, upo, veco, arrived_slots, target = lax.optimization_barrier(
        (half, other, upo, veco, arrived_slots, target)
    )
    q = forward(core_arr, half, gains, pairs, other)
    got = lax.ppermute(q, "tensor", swap)
    parts, st = backward(core_arr, q, got, upstream, upo, vec, veco, pairs, other)
    back = lax.all_to_all(parts, "tensor", 0, 0, axis_index_groups=classes, tiled=True)
    own_gain = lax.dynamic_index_in_dim(norm_gain.reshape(n_tensor, 1, feats), me, 0, False)
    send_rows = finish(back, inputs, st, own_gain, target[None, :], owners * capacity)
    arrived = lax.all_to_all(send_rows, "dp", split_axis=0, concat_axis=0, tiled=True)
    return land(arrived, arrived_slots, rows)


def solution(mesh):
    return jax.shard_map(
        per_device,
        mesh=mesh,
        in_specs=(
            P("dp", "tensor"),
            P("dp", "tensor"),
            P(None, "tensor"),
            P("tensor"),
            P(),
            P("dp"),
        ),
        out_specs=P("dp", "tensor"),
        check_vma=False,
    )
```

time: 340 us -> 148 us (0.44)
  waiting for transfers between devices: 274 us -> 39.2 us
  blocking collectives: 0 us -> 53.3 us
  Pallas kernels: 0 us -> 17.1 us
  between operations: 13.5 us -> 0.17 us
  other arithmetic: 15 us -> 2.04 us
  matrix products: 9.13 us -> 0 us
  local copies, waits for them, and re-layouts: 2.85 us -> 8.62 us
  starting transfers between devices: 23.7 us -> 27.2 us
    psum x1 -> x0, waiting for transfers between devices: 155 us -> none  [per_device(): lax.psum(contract_cols(pre_grad, proj_weight).astype(jnp.bfloat16), 'tens...]
    all_gather x1 -> x0, waiting for transfers between devices: 78.1 us -> none  [per_device(): lax.all_gather(inputs, 'tensor', axis=1, tiled=True).astype(jnp.float32)]
    all_to_all x0 -> x2, blocking collectives: none -> 53.3 us  [the longest x1 30.4 us: per_device(): lax.all_to_all(send_rows, 'dp', split_axis=0, concat_axis=0, tiled=True)]
    pallas_call x0 -> x4, Pallas kernels: none -> 17.1 us  [the longest x1 6.56 us: backward(): pl.pallas_call(backward_kernel, in_specs=[SCALAR] + in_vmem(8), out_specs...]
    ppermute x0 -> x4, starting transfers between devices: none -> 17 us  [the longest x1 8.74 us: per_device(): lax.ppermute(lax.dynamic_index_in_dim(pairs, 1 - core, 1, False), 'tensor...]
    all_to_all x3 -> x2, starting transfers between devices: 23.7 us -> 10.2 us  [the longest x1 6.62 us: per_device(): lax.all_to_all(sent, 'tensor', 0, 0, axis_index_groups=classes, tiled=True)]
    dot_general x3 -> x0, matrix products: 9.13 us -> none  [the longest x1 7.1 us: contract_cols(): lax.dot_general(left, right, (((1,), (1,)), ((), ())), preferred_element_...]
    mul x1 -> x0, other arithmetic: 5.68 us -> none  [per_device(): unit_rows = centred * inv_std]
  transfers between devices with their start and end apart: 5 -> 6, of which waited for: 5 -> 3; matrix products, arithmetic and copies ran while one was open for 3% -> 4% of each run, Pallas kernels for 0% -> 0%
where the time goes in v1:
time: 148 us
  blocking collectives  53.3 us (36%)
  waiting for transfers between devices  39.2 us (26%)
  starting transfers between devices  27.2 us (18%)
  Pallas kernels  17.1 us (12%)
  local copies, waits for them, and re-layouts  8.62 us (6%)
  other arithmetic  2.04 us (1%)
    all_to_all x1, blocking collectives, per_device(): lax.all_to_all(send_rows, 'dp', split_axis=0, concat_axis=0, tiled=True)  30.4 us
    all_to_all x1, blocking collectives, per_device(): lax.all_to_all(send_slots.reshape(owners, 1, capacity), 'dp', split_axis=...  22.9 us
    all_to_all x1, waiting for transfers between devices, per_device(): lax.all_to_all(parts, 'tensor', 0, 0, axis_index_groups=classes, tiled=True)  22.7 us
    all_to_all x1, waiting for transfers between devices, per_device(): lax.all_to_all(sent, 'tensor', 0, 0, axis_index_groups=classes, tiled=True)  14.6 us
    ppermute x1, starting transfers between devices, per_device(): lax.ppermute(lax.dynamic_index_in_dim(pairs, 1 - core, 1, False), 'tensor...  8.74 us
    all_to_all x1, starting transfers between devices, per_device(): lax.all_to_all(sent, 'tensor', 0, 0, axis_index_groups=classes, tiled=True)  6.62 us
    pallas_call x1, Pallas kernels, backward(): pl.pallas_call(backward_kernel, in_specs=[SCALAR] + in_vmem(8), out_specs...  6.56 us
    pallas_call x1, Pallas kernels, forward(): pl.pallas_call(forward_kernel, in_specs=[SCALAR] + in_vmem(4), out_specs=...  5.49 us
  transfers between devices with their start and end apart: 6, of which 3 were waited for; matrix products, arithmetic and copies ran while one was open for 4% of the time, Pallas kernels for 0%

profile of v1, /device:TPU:1, one launch (start us, length us, event | category | flops | bytes accessed | tf_op | source)
XLA Modules:
  0.0 147.7 jit_solution(7653252739623599484)
XLA Ops:
  0.0 0.0 copy-start.10
  0.0 0.0 copy-start.2
  0.0 2.7 %dynamic-slice_bitcast_fusion = bf16[8,384,256]{2,1,0:T(8,128)(2,1)} fusion(bf16[8,2,384,256]{3,2,1,0:T(8,128)(2,1)} %bitcast.13, s32[]{:T(128)S(6)} %select_n.31), kind=kLoop, calls=%fused_computation.1 | loop fusion | bytes 3145732 | tf_op jit(solution)/shard_map/jit(dynamic_index_in_dim)/squeeze | solution.py:183
  2.7 8.7 %collective-permute-start = (bf16[8,384,256]{2,1,0:T(8,128)(2,1)}, bf16[8,384,256]{2,1,0:T(8,128)(2,1)}, u32[]{:S(2)}, u32[]{:S(2)}) collective-permute-start(bf16[8,384,256]{2,1,0:T(8,128)(2,1)} %dynamic-slice_bitcast_fusion), channel_id=1, source_target_pairs={{0,1},{1,0},{2,3},{3,2},{4,5},{5,4},{6,7},{7,6},{8,9},{9,8},{10,11... | collective-permute-start | bytes 4718600 | tf_op jit(solution)/shard_map/ppermute | solution.py:183
  11.4 0.0 copy-done.10
  11.5 0.2 convert_reduce_fusion
  11.7 0.0 copy-start.8
  11.7 0.1 select_reduce_fusion
  11.8 0.1 sub.18
  11.9 22.9 %all_to_all.26 = s32[32,1,16]{2,1,0:T(1,128)S(1)} all-to-all(s32[32,1,16]{2,1,0:T(1,128)S(1)} %bitcast.21), channel_id=1, replica_groups=mesh['dp'=32,'tensor'=16] {'dp'}, dimensions={0} | all-to-all | bytes 4096 | tf_op jit(solution)/shard_map/all_to_all | solution.py:203
  34.8 0.0 copy-done.2
  34.8 0.0 copy-start.4
  34.8 0.0 copy-start.6
  34.8 1.3 broadcast_in_dim.14
  36.1 0.0 copy-start
  36.1 0.0 copy-done.8
  36.1 6.6 %all-to-all-start = ((bf16[8,256,384]{2,1,0:T(8,128)(2,1)}), bf16[8,256,384]{2,1,0:T(8,128)(2,1)}, u32[]{:S(2)}, u32[]{:S(2)}) async-start(bf16[8,256,384]{2,1,0:T(8,128)(2,1)} %broadcast_in_dim.14), calls=%async_computation | async-start | bytes 3145728 | tf_op jit(solution)/shard_map/all_to_all | solution.py:180
  42.8 0.0 copy-done.4
  42.8 0.0 copy-start.11
  42.8 3.7 %collective-permute-start.1 = (bf16[256,256]{1,0:T(8,128)(2,1)S(1)}, bf16[256,256]{1,0:T(8,128)(2,1)S(1)}, u32[]{:S(2)}, u32[]{:S(2)}) collective-permute-start(bf16[256,256]{1,0:T(8,128)(2,1)S(1)} %copy-done.4), channel_id=1, source_target_pairs={{0,1},{1,0},{2,3},{3,2},{4,5},{5,4},{6,7},{7,6},{8,9},{9,8},{10,11... | collective-permute-start | bytes 393224 | tf_op jit(solution)/shard_map/ppermute | solution.py:184
  46.4 0.0 copy-done.6
  46.5 0.0 copy-done
  46.5 1.0 multiply_reduce_fusion
  47.5 0.0 copy-done.11
  47.5 0.0 copy-start.7
  47.5 1.9 %collective-permute-start.2 = (f32[3,256]{1,0:T(4,128)S(1)}, f32[3,256]{1,0:T(4,128)S(1)}, u32[]{:S(2)}, u32[]{:S(2)}) collective-permute-start(f32[3,256]{1,0:T(4,128)S(1)} %pad_maximum_fusion.vec_ref), channel_id=1, source_target_pairs={{0,1},{1,0},{2,3},{3,2},{4,5},{5,4},{6,7},{7,6},{8,9},{9,8},{10,11... | collective-permute-start | bytes 9224 | tf_op jit(solution)/shard_map/ppermute | solution.py:188
  49.4 0.5 broadcast.61
  49.9 0.7 reduce.3
  50.6 0.6 reshape.40.slot_ref
  51.3 0.0 collective-permute-done.2.veco_ref
  51.3 0.0 copy-start.9
  51.3 0.0 collective-permute-done.1.upo_ref
  51.3 0.0 copy-start.5
  51.3 14.6 %all-to-all-done.x_ref = bf16[8,256,384]{2,1,0:T(8,128)(2,1)} async-done(((bf16[8,256,384]{2,1,0:T(8,128)(2,1)}), bf16[8,256,384]{2,1,0:T(8,128)(2,1)}, u32[]{:S(2)}, u32[]{:S(2)}) %all-to-all-start) | async-done | bytes 1572896 | tf_op jit(solution)/shard_map/all_to_all | solution.py:180
  65.8 0.0 collective-permute-done.other_ref
  65.9 5.5 %forward.1.q_ref = f32[256,640]{1,0:T(8,128)} custom-call(s32[1]{0:T(128)} %bitcast.core_ref, bf16[8,256,384]{2,1,0:T(8,128)(2,1)} %all-to-all-done.x_ref, f32[8,2,1,384]{3,2,1,0:T(1,128)} %bitcast.19, bf16[8,2,384,256]{3,2,1,0:T(8,128)(2,1)} %bitcast.14, bf16[8,384,256]{2,1,0:T(8,128)(2,1)} %collective-permute-done.other_ref), custom_call_target="tpu_custom_call" | custom-call | tf_op jit(solution)/shard_map/forward/pallas_call | solution.py:47
  71.3 0.0 copy-done.7
  71.3 0.0 copy-done.9
  71.4 0.0 copy-done.5
  71.4 2.7 %collective-permute-start.3 = (f32[256,640]{1,0:T(8,128)}, f32[256,640]{1,0:T(8,128)S(1)}, u32[]{:S(2)}, u32[]{:S(2)}) collective-permute-start(f32[256,640]{1,0:T(8,128)} %forward.1.q_ref), channel_id=1, source_target_pairs={{0,1},{1,0},{2,3},{3,2},{4,5},{5,4},{6,7},{7,6},{8,9},{9,8},{10,11... | collective-permute-start | bytes 1966088 | tf_op jit(solution)/shard_map/ppermute | solution.py:211
  74.1 1.9 %collective-permute-done.3.got_ref = f32[256,640]{1,0:T(8,128)S(1)} collective-permute-done((f32[256,640]{1,0:T(8,128)}, f32[256,640]{1,0:T(8,128)S(1)}, u32[]{:S(2)}, u32[]{:S(2)}) %collective-permute-start.3) | collective-permute-done | bytes 655392 | tf_op jit(solution)/shard_map/ppermute | solution.py:211
  76.0 0.0 copy-start.3
  76.0 0.8 copy-done.3
  76.8 6.6 %backward.1 = (bf16[8,272,384]{2,1,0:T(8,128)(2,1)}, f32[256,128]{1,0:T(8,128)}) custom-call(s32[1]{0:T(128)} %bitcast.core_ref, f32[256,640]{1,0:T(8,128)} %forward.1.q_ref, f32[256,640]{1,0:T(8,128)} %copy-done.3, bf16[256,256]{1,0:T(8,128)(2,1)} %up_ref.1, bf16[256,256]{1,0:T(8,128)(2,1)} %copy-done.5, f32[3,256]{1,0:T(4,128)} %copy-done.7, ...), custom_call_target="tpu_custom_call" | custom-call | tf_op jit(solution)/shard_map/backward/pallas_call | solution.py:107
  83.4 3.6 %all-to-all-start.2 = ((bf16[8,272,384]{2,1,0:T(8,128)(2,1)}), bf16[8,272,384]{2,1,0:T(8,128)(2,1)S(1)}, u32[]{:S(2)}, u32[]{:S(2)}) async-start(bf16[8,272,384]{2,1,0:T(8,128)(2,1)} %get-tuple-element.17), calls=%async_computation.2 | async-start | bytes 3342336 | tf_op jit(solution)/shard_map/all_to_all | solution.py:213
  87.0 1.2 dynamic-slice_bitcast_fusion.1.gain_ref
  88.2 22.7 %all-to-all-done.2.back_ref = bf16[8,272,384]{2,1,0:T(8,128)(2,1)S(1)} async-done(((bf16[8,272,384]{2,1,0:T(8,128)(2,1)}), bf16[8,272,384]{2,1,0:T(8,128)(2,1)S(1)}, u32[]{:S(2)}, u32[]{:S(2)}) %all-to-all-start.2) | async-done | bytes 1671200 | tf_op jit(solution)/shard_map/all_to_all | solution.py:213
  111.0 0.0 copy-start.1
  111.0 1.2 copy-done.1
  112.2 3.1 %finish.1 = bf16[512,384]{1,0:T(8,128)(2,1)} custom-call(bf16[8,272,384]{2,1,0:T(8,128)(2,1)} %copy-done.1, bf16[256,384]{1,0:T(8,128)(2,1)} %x_ref.1, f32[256,128]{1,0:T(8,128)} %get-tuple-element.18.st_ref, f32[1,384]{1,0:T(1,128)} %dynamic-slice_bitcast_fusion.1.gain_ref, s32[1,256]{1,0:T(1,128)} %bitcast.22), custom_call_target="tpu_custom_call" | custom-call | tf_op jit(solution)/shard_map/finish/pallas_call | solution.py:140
  115.3 30.4 %all_to_all.27 = bf16[32,16,384]{2,1,0:T(8,128)(2,1)} all-to-all(bf16[32,16,384]{2,1,0:T(8,128)(2,1)} %bitcast.17), channel_id=1, replica_groups=mesh['dp'=32,'tensor'=16] {'dp'}, dimensions={0} | all-to-all | bytes 786432 | tf_op jit(solution)/shard_map/all_to_all | solution.py:216
  145.7 2.0 %land.1 = bf16[256,384]{1,0:T(8,128)(2,1)} custom-call(bf16[512,384]{1,0:T(8,128)(2,1)} %bitcast.18, s32[1,512]{1,0:T(1,128)} %reshape.40.slot_ref), custom_call_target="tpu_custom_call" | custom-call | tf_op jit(solution)/shard_map/land/pallas_call | solution.py:159
  (5 shorter events, 0.1 us)
Async XLA Ops:
  0.0 11.5 %copy-start.10 = (s32[256]{0:T(256)S(1)}, s32[256]{0:T(256)}, u32[]{:S(2)}) copy-start(s32[256]{0:T(256)} %param.11) | copy-start | bytes 3076
  0.0 34.8 %copy-start.2 = (bf16[256,384]{1,0:T(8,128)(2,1)S(1)}, bf16[256,384]{1,0:T(8,128)(2,1)}, u32[]{:S(2)}) copy-start(bf16[256,384]{1,0:T(8,128)(2,1)} %x_ref.1) | copy-start | bytes 589828
  2.7 63.1 %collective-permute-start = (bf16[8,384,256]{2,1,0:T(8,128)(2,1)}, bf16[8,384,256]{2,1,0:T(8,128)(2,1)}, u32[]{:S(2)}, u32[]{:S(2)}) collective-permute-start(bf16[8,384,256]{2,1,0:T(8,128)(2,1)} %dynamic-slice_bitcast_fusion), channel_id=1, source_target_pairs={{0,1},{1,0},{2,3},{3,2},{4,5},{5,4},{6,7},{7,6},{8,9},{9,8},{10,11... | collective-permute-start | bytes 4718600 | tf_op jit(solution)/shard_map/ppermute | solution.py:183
  11.7 24.5 %copy-start.8 = (s32[256]{0:T(256)}, s32[256]{0:T(256)S(1)}, u32[]{:S(2)}) copy-start(s32[256]{0:T(256)S(1)} %multiply_add_fusion) | copy-start | bytes 3076
  34.8 8.0 %copy-start.4 = (bf16[256,256]{1,0:T(8,128)(2,1)S(1)}, bf16[256,256]{1,0:T(8,128)(2,1)}, u32[]{:S(2)}) copy-start(bf16[256,256]{1,0:T(8,128)(2,1)} %up_ref.1) | copy-start | bytes 393220
  34.8 11.6 %copy-start.6 = (f32[6144]{0:T(1024)S(1)}, f32[6144]{0:T(1024)}, u32[]{:S(2)}) copy-start(f32[6144]{0:T(1024)} %param.10) | copy-start | bytes 73732
  36.1 10.3 %copy-start = (bf16[6144,256]{1,0:T(8,128)(2,1)S(1)}, bf16[6144,256]{1,0:T(8,128)(2,1)}, u32[]{:S(2)}) copy-start(bf16[6144,256]{1,0:T(8,128)(2,1)} %param.8) | copy-start | bytes 9437188
  36.1 29.7 %all-to-all-start = ((bf16[8,256,384]{2,1,0:T(8,128)(2,1)}), bf16[8,256,384]{2,1,0:T(8,128)(2,1)}, u32[]{:S(2)}, u32[]{:S(2)}) async-start(bf16[8,256,384]{2,1,0:T(8,128)(2,1)} %broadcast_in_dim.14), calls=%async_computation | async-start | bytes 3145728 | tf_op jit(solution)/shard_map/all_to_all | solution.py:180
  42.8 4.7 %copy-start.11 = (f32[256]{0:T(256)S(1)}, f32[256]{0:T(256)}, u32[]{:S(2)}) copy-start(f32[256]{0:T(256)} %param.9) | copy-start | bytes 3076
  42.8 8.5 %collective-permute-start.1 = (bf16[256,256]{1,0:T(8,128)(2,1)S(1)}, bf16[256,256]{1,0:T(8,128)(2,1)S(1)}, u32[]{:S(2)}, u32[]{:S(2)}) collective-permute-start(bf16[256,256]{1,0:T(8,128)(2,1)S(1)} %copy-done.4), channel_id=1, source_target_pairs={{0,1},{1,0},{2,3},{3,2},{4,5},{5,4},{6,7},{7,6},{8,9},{9,8},{10,11... | collective-permute-start | bytes 393224 | tf_op jit(solution)/shard_map/ppermute | solution.py:184
  47.5 23.9 %copy-start.7 = (f32[3,256]{1,0:T(4,128)}, f32[3,256]{1,0:T(4,128)S(1)}, u32[]{:S(2)}) copy-start(f32[3,256]{1,0:T(4,128)S(1)} %pad_maximum_fusion.vec_ref) | copy-start | bytes 9220
  47.5 3.8 %collective-permute-start.2 = (f32[3,256]{1,0:T(4,128)S(1)}, f32[3,256]{1,0:T(4,128)S(1)}, u32[]{:S(2)}, u32[]{:S(2)}) collective-permute-start(f32[3,256]{1,0:T(4,128)S(1)} %pad_maximum_fusion.vec_ref), channel_id=1, source_target_pairs={{0,1},{1,0},{2,3},{3,2},{4,5},{5,4},{6,7},{7,6},{8,9},{9,8},{10,11... | collective-permute-start | bytes 9224 | tf_op jit(solution)/shard_map/ppermute | solution.py:188
  51.3 20.1 %copy-start.9 = (f32[3,256]{1,0:T(4,128)}, f32[3,256]{1,0:T(4,128)S(1)}, u32[]{:S(2)}) copy-start(f32[3,256]{1,0:T(4,128)S(1)} %collective-permute-done.2.veco_ref) | copy-start | bytes 9220
  51.3 20.1 %copy-start.5 = (bf16[256,256]{1,0:T(8,128)(2,1)}, bf16[256,256]{1,0:T(8,128)(2,1)S(1)}, u32[]{:S(2)}) copy-start(bf16[256,256]{1,0:T(8,128)(2,1)S(1)} %collective-permute-done.1.upo_ref) | copy-start | bytes 393220
  71.4 4.6 %collective-permute-start.3 = (f32[256,640]{1,0:T(8,128)}, f32[256,640]{1,0:T(8,128)S(1)}, u32[]{:S(2)}, u32[]{:S(2)}) collective-permute-start(f32[256,640]{1,0:T(8,128)} %forward.1.q_ref), channel_id=1, source_target_pairs={{0,1},{1,0},{2,3},{3,2},{4,5},{5,4},{6,7},{7,6},{8,9},{9,8},{10,11... | collective-permute-start | bytes 1966088 | tf_op jit(solution)/shard_map/ppermute | solution.py:211
  76.0 0.8 copy-start.3
  83.4 27.6 %all-to-all-start.2 = ((bf16[8,272,384]{2,1,0:T(8,128)(2,1)}), bf16[8,272,384]{2,1,0:T(8,128)(2,1)S(1)}, u32[]{:S(2)}, u32[]{:S(2)}) async-start(bf16[8,272,384]{2,1,0:T(8,128)(2,1)} %get-tuple-element.17), calls=%async_computation.2 | async-start | bytes 3342336 | tf_op jit(solution)/shard_map/all_to_all | solution.py:213
  111.0 1.2 copy-start.1

commit v2 on v1

v2 whole, which is shorter than its diff:
```python
import jax
import jax.numpy as jnp
from jax import lax
from jax.experimental import pallas as pl
from jax.experimental.pallas import tpu as pltpu
from jax.sharding import PartitionSpec as P


epsilon = 1e-05
f32, bf16 = jnp.float32, jnp.bfloat16
PAD = 16
CAPACITY = 16
NT = (((1,), (1,)), ((), ()))


def in_vmem(n):
    return [pl.BlockSpec(memory_space=pltpu.VMEM) for _ in range(n)]


def held(*arrays):
    return [pltpu.with_memory_space_constraint(a, pltpu.VMEM) for a in arrays]


PARAMS = pltpu.CompilerParams(vmem_limit_bytes=16 * 1024 * 1024)


ANYWHERE = pl.BlockSpec(memory_space=pl.ANY)
SCALAR = pl.BlockSpec(memory_space=pltpu.SMEM)


def forward_kernel(
    core_ref, x_any, gain_ref, weight_any, other_any, q_ref, x_ref, weight_ref, other_ref, x_sem, w_sem, o_sem
):
    blocks, rows, feats = x_ref.shape
    width = other_ref.shape[2]
    core = core_ref[0]
    x_copies = [pltpu.make_async_copy(x_any.at[b], x_ref.at[b], x_sem.at[b]) for b in range(blocks)]
    w_copies = [
        pltpu.make_async_copy(weight_any.at[b, core], weight_ref.at[b], w_sem.at[b]) for b in range(blocks)
    ]
    o_copies = [
        pltpu.make_async_copy(other_any.at[b], other_ref.at[b], o_sem.at[b]) for b in range(blocks)
    ]
    for copy in x_copies:
        copy.start()
    for b in range(blocks):
        w_copies[b].start()
        o_copies[b].start()
    total = jnp.zeros((rows, feats), f32)
    for b in range(blocks):
        x_copies[b].wait()
        total += x_ref[b].astype(f32)
    mean = jnp.sum(total, axis=1, keepdims=True) / (blocks * feats)
    spread = jnp.zeros((rows, feats), f32)
    for b in range(blocks):
        centred = x_ref[b].astype(f32) - mean
        spread += centred * centred
        scaled = (centred * gain_ref[b, core]).astype(bf16)
        w_copies[b].wait()
        o_copies[b].wait()
        own = jnp.dot(scaled, weight_ref[b], preferred_element_type=f32)
        other = jnp.dot(scaled, other_ref[b], preferred_element_type=f32)
        if b == 0:
            q_ref[:, :width] = own
            q_ref[:, width : 2 * width] = other
        else:
            q_ref[:, :width] += own
            q_ref[:, width : 2 * width] += other
    spread = jnp.sum(spread, axis=1, keepdims=True) / (blocks * feats)
    lane = lax.broadcasted_iota(jnp.int32, (rows, 128), 1)
    q_ref[:, 2 * width :] = jnp.where(lane == 0, mean, spread)


def forward(core, x, gain, weight, other):
    blocks, rows, _ = x.shape
    width = other.shape[2]
    return pl.pallas_call(
        forward_kernel,
        in_specs=[SCALAR, ANYWHERE] + in_vmem(1) + [ANYWHERE, ANYWHERE],
        out_specs=in_vmem(1)[0],
        out_shape=jax.ShapeDtypeStruct((rows, 2 * width + 128), f32),
        scratch_shapes=[
            pltpu.VMEM(x.shape, bf16),
            pltpu.VMEM(other.shape, bf16),
            pltpu.VMEM(other.shape, bf16),
            pltpu.SemaphoreType.DMA((blocks,)),
            pltpu.SemaphoreType.DMA((blocks,)),
            pltpu.SemaphoreType.DMA((blocks,)),
        ],
        compiler_params=PARAMS,
        name="forward",
    )(core, x, gain, weight, other)


def backward_kernel(
    core_ref,
    q_ref,
    got_ref,
    up_ref,
    upo_ref,
    vec_ref,
    veco_ref,
    weight_any,
    other_any,
    p_any,
    st_ref,
    weight_ref,
    other_ref,
    p_ref,
    w_sem,
    o_sem,
    p_sem,
):
    blocks, feats, width = other_ref.shape
    rows = q_ref.shape[0]
    core = core_ref[0]
    w_copies = [
        pltpu.make_async_copy(weight_any.at[b, core], weight_ref.at[b], w_sem.at[b]) for b in range(blocks)
    ]
    o_copies = [
        pltpu.make_async_copy(other_any.at[b], other_ref.at[b], o_sem.at[b]) for b in range(blocks)
    ]
    p_copies = [pltpu.make_async_copy(p_ref.at[b], p_any.at[b], p_sem.at[b]) for b in range(blocks)]
    for b in range(blocks):
        w_copies[b].start()
        o_copies[b].start()
    mine, theirs = q_ref[:, 2 * width :], got_ref[:, 2 * width :]
    mean_here, mean_there = mine[:, 0:1], theirs[:, 0:1]
    gap = 0.5 * (mean_here - mean_there)
    mean = 0.5 * (mean_here + mean_there)
    variance = 0.5 * (mine[:, 1:2] + theirs[:, 1:2]) + gap * gap
    inv_std = lax.rsqrt(variance + epsilon)
    lane = lax.broadcasted_iota(jnp.int32, (rows, 128), 1)
    st_ref[...] = jnp.where(lane == 0, mean, inv_std)
    side = jnp.where(core == 0, 1.0, -1.0)

    def grad(summed, up, vec):
        raw = inv_std * (summed + gap * (side * (vec[1:2, :] - vec[2:3, :])))
        preact = raw + vec[0:1, :]
        gate = 1.0 / (1.0 + jnp.exp(-preact))
        pg = (up.astype(f32) * gate * (1.0 + preact * (1.0 - gate))).astype(bf16)
        wide = pg.astype(f32)
        scale = jnp.broadcast_to(vec[1:2, :] + vec[2:3, :], (8, width))
        first = lax.dot_general(scale, wide, NT, precision=lax.Precision.HIGHEST)
        second = lax.dot_general(
            jnp.ones((8, width), f32), wide * raw, NT, precision=lax.Precision.HIGHEST
        )
        return pg, first, second

    pg, first, second = grad(q_ref[:, :width] + got_ref[:, width : 2 * width], up_ref[...], vec_ref[...])
    pgo, firsto, secondo = grad(
        q_ref[:, width : 2 * width] + got_ref[:, :width], upo_ref[...], veco_ref[...]
    )
    first, second = first + firsto, second + secondo
    row = lax.broadcasted_iota(jnp.int32, (8, rows), 0)
    value = jnp.where(row < 2, first, second)
    high = value.astype(bf16).astype(f32)
    tail = jnp.where(row % 2 == 0, high, value - high)
    tail = jnp.concatenate([tail, jnp.zeros_like(tail)], axis=0).astype(bf16)
    tail = jnp.concatenate([tail, jnp.zeros((PAD, feats - rows), bf16)], axis=1)
    for b in range(blocks):
        w_copies[b].wait()
        o_copies[b].wait()
        p_ref[b, :rows] = (
            lax.dot_general(pg, weight_ref[b], NT, preferred_element_type=f32)
            + lax.dot_general(pgo, other_ref[b], NT, preferred_element_type=f32)
        ).astype(bf16)
        p_ref[b, rows:] = tail
        p_copies[b].start()
    for copy in p_copies:
        copy.wait()


def backward(core, q, got, up, upo, vec, veco, weight, other):
    blocks, feats, _ = other.shape
    rows = q.shape[0]
    return pl.pallas_call(
        backward_kernel,
        in_specs=[SCALAR] + in_vmem(6) + [ANYWHERE, ANYWHERE],
        out_specs=[ANYWHERE] + in_vmem(1),
        out_shape=[
            jax.ShapeDtypeStruct((blocks, rows + PAD, feats), bf16),
            jax.ShapeDtypeStruct((rows, 128), f32),
        ],
        scratch_shapes=[
            pltpu.VMEM(other.shape, bf16),
            pltpu.VMEM(other.shape, bf16),
            pltpu.VMEM((blocks, rows + PAD, feats), bf16),
            pltpu.SemaphoreType.DMA((blocks,)),
            pltpu.SemaphoreType.DMA((blocks,)),
            pltpu.SemaphoreType.DMA((blocks,)),
        ],
        compiler_params=PARAMS,
        name="backward",
    )(core, q, got, up, upo, vec, veco, weight, other)


def finish_kernel(back_ref, x_ref, st_ref, gain_ref, target_ref, slot_ref, send_ref):
    blocks = back_ref.shape[0]
    rows, feats = x_ref.shape
    owners = send_ref.shape[0]
    total = back_ref[0].astype(f32)
    for b in range(1, blocks):
        total += back_ref[b].astype(f32)
    tail = total[rows : rows + 8, :rows]
    sums = tail.T / (2 * blocks * feats)
    first = sums[:, 0:1] + sums[:, 1:2]
    second = sums[:, 2:3] + sums[:, 3:4]
    mean, inv_std = st_ref[:, 0:1], st_ref[:, 1:2]
    unit = (x_ref[...].astype(f32) - mean) * inv_std
    grad = (inv_std * (total[:rows] * gain_ref[...] - first - unit * second)).astype(bf16)
    slots = owners * CAPACITY
    placing = lax.broadcasted_iota(jnp.int32, (slots, rows), 0) == target_ref[...]
    placed = jnp.dot(
        jnp.where(placing, 1.0, 0.0).astype(bf16), grad, preferred_element_type=f32
    ).astype(bf16)
    placed = placed.reshape(owners, CAPACITY, feats)
    for k in range(feats // 128):
        send_ref[:, k * CAPACITY : (k + 1) * CAPACITY, :] = placed[:, :, k * 128 : (k + 1) * 128]
    send_ref[:, feats // 128 * CAPACITY :, :] = jnp.broadcast_to(slot_ref[...][:, None, :], (owners, 8, 128))


def finish(back, x, st, gain, target, slot):
    owners = slot.shape[0]
    return pl.pallas_call(
        finish_kernel,
        in_specs=in_vmem(6),
        out_specs=in_vmem(1)[0],
        out_shape=pltpu.VMEM((owners, x.shape[1] // 128 * CAPACITY + 8, 128), bf16),
        compiler_params=PARAMS,
        name="finish",
    )(*held(back, x, st, gain, target, slot))


def landing_kernel(got_ref, o_ref):
    rows, feats = o_ref.shape
    owners = got_ref.shape[0]
    slots = owners * CAPACITY
    pieces = feats // 128
    held_slots = got_ref[:, pieces * CAPACITY, :].astype(bf16)
    spread = lax.broadcasted_iota(jnp.int32, (128, slots), 0) == (
        lax.broadcasted_iota(jnp.int32, (128, slots), 1) % CAPACITY
    )
    every = jnp.dot(held_slots, jnp.where(spread, 1.0, 0.0).astype(bf16), preferred_element_type=f32)
    own = lax.broadcasted_iota(jnp.int32, (owners, slots), 0) == (
        lax.broadcasted_iota(jnp.int32, (owners, slots), 1) // CAPACITY
    )
    slot = jnp.sum(jnp.where(own, every, 0.0), axis=0, keepdims=True).astype(jnp.int32)
    landing = lax.broadcasted_iota(jnp.int32, (rows, slots), 0) == slot
    landing = jnp.where(landing, 1.0, 0.0).astype(bf16)
    for k in range(pieces):
        piece = got_ref[:, k * CAPACITY : (k + 1) * CAPACITY, :].reshape(slots, 128)
        o_ref[:, k * 128 : (k + 1) * 128] = jnp.dot(
            landing, piece, preferred_element_type=f32
        ).astype(bf16)


def land(got, rows, feats):
    return pl.pallas_call(
        landing_kernel,
        in_specs=in_vmem(1),
        out_specs=in_vmem(1)[0],
        out_shape=jax.ShapeDtypeStruct((rows, feats), bf16),
        compiler_params=PARAMS,
        name="land",
    )(*held(got))


def per_device(inputs, upstream, proj_weight, proj_bias, norm_gain, home_rows):
    rows, feats = inputs.shape
    width = upstream.shape[1]
    n_tensor, owners = lax.axis_size("tensor"), lax.axis_size("dp")
    chips = n_tensor // 2
    me = lax.axis_index("tensor")
    core = me % 2
    swap = [(t, t ^ 1) for t in range(n_tensor)]
    classes = [[2 * k + c for k in range(chips)] for c in range(2)]
    core_arr = core.reshape(1).astype(jnp.int32)

    sent = jnp.broadcast_to(inputs[None], (chips, rows, feats))
    half = lax.all_to_all(sent, "tensor", 0, 0, axis_index_groups=classes, tiled=True)

    pairs = proj_weight.reshape(chips, 2, feats, width)
    cut = lax.dynamic_index_in_dim(pairs, 1 - core, 1, False)
    other = lax.ppermute(cut, "tensor", swap)
    upo = lax.ppermute(upstream, "tensor", swap)
    gains = norm_gain.reshape(chips, 2, 1, feats)
    scales = jnp.sum(norm_gain.reshape(chips, 2, feats, 1) * pairs.astype(f32), axis=(0, 2))
    vec = jnp.concatenate([proj_bias[None], scales], axis=0)
    veco = lax.ppermute(vec, "tensor", swap)

    owner_of = home_rows // rows
    home_slot = home_rows % rows
    order_ids = jnp.arange(rows, dtype=jnp.int32)
    earlier = jnp.sum(
        ((owner_of[:, None] == owner_of[None, :]) & (order_ids[:, None] > order_ids[None, :])).astype(
            jnp.int32
        ),
        axis=1,
    )
    target = owner_of * CAPACITY + earlier
    lanes = jnp.arange(128, dtype=jnp.int32)
    held_at = (jnp.arange(owners, dtype=jnp.int32)[:, None] * CAPACITY + lanes[None, :])[:, :, None]
    match = (held_at == target[None, None, :]) & (lanes < CAPACITY)[None, :, None]
    slot = jnp.sum(jnp.where(match, home_slot[None, None, :] + 1, 0), axis=2) - 1
    slot = slot.astype(f32).astype(bf16)

    own_gain = lax.dynamic_index_in_dim(norm_gain.reshape(n_tensor, 1, feats), me, 0, False)
    half, other, upo, veco, slot, target, own_gain = lax.optimization_barrier(
        (half, other, upo, veco, slot, target, own_gain)
    )
    q = forward(core_arr, half, gains, pairs, other)
    got = lax.ppermute(q, "tensor", swap)
    parts, st = backward(core_arr, q, got, upstream, upo, vec, veco, pairs, other)
    back = lax.all_to_all(parts, "tensor", 0, 0, axis_index_groups=classes, tiled=True)
    send = finish(back, inputs, st, own_gain, target[None, :], slot)
    arrived = lax.all_to_all(send, "dp", split_axis=0, concat_axis=0, tiled=True)
    return land(arrived, rows, feats)


def solution(mesh):
    return jax.shard_map(
        per_device,
        mesh=mesh,
        in_specs=(
            P("dp", "tensor"),
            P("dp", "tensor"),
            P(None, "tensor"),
            P("tensor"),
            P(),
            P("dp"),
        ),
        out_specs=P("dp", "tensor"),
        check_vma=False,
    )
```

time: 148 us -> 132 us (0.89); the launches traced: 148 us -> 130 us
  waiting for transfers between devices: 39.2 us -> 20.4 us
  blocking collectives: 53.3 us -> 66 us
  starting transfers between devices: 27.2 us -> 20.2 us
  local copies, waits for them, and re-layouts: 8.62 us -> 4.17 us
    all_to_all x1 -> x0, waiting for transfers between devices: 22.7 us -> none  [per_device(): lax.all_to_all(parts, 'tensor', 0, 0, axis_index_groups=classes, tiled=True)]
    all_to_all x2, blocking collectives: 53.3 us -> 66 us  [the longest x1 38.3 us: per_device(): lax.all_to_all(send, 'dp', split_axis=0, concat_axis=0, tiled=True)]
    all_to_all x1, waiting for transfers between devices: 14.6 us -> 18.7 us  [per_device(): lax.all_to_all(sent, 'tensor', 0, 0, axis_index_groups=classes, tiled=True)]
    all_to_all x1 -> x0, starting transfers between devices: 3.59 us -> none  [per_device(): lax.all_to_all(parts, 'tensor', 0, 0, axis_index_groups=classes, tiled=True)]
    all_to_all x1, starting transfers between devices: 6.62 us -> 4.29 us  [per_device(): lax.all_to_all(sent, 'tensor', 0, 0, axis_index_groups=classes, tiled=True)]
    unnamed x24 -> x12, local copies, waits for them, and re-layouts: 2.1 us -> 0.03 us
  transfers between devices with their start and end apart: 6 -> 5, of which waited for: 3 -> 2; matrix products, arithmetic and copies ran while one was open for 4% -> 3% of each run, Pallas kernels for 0% -> 0%
where the time goes in v2:
time: 132 us; the launch traced here: 130 us
  blocking collectives  66 us (50%)
  waiting for transfers between devices  20.4 us (15%)
  starting transfers between devices  20.2 us (15%)
  Pallas kernels  16 us (12%)
  local copies, waits for them, and re-layouts  4.17 us (3%)
  other arithmetic  2.79 us (2%)
    all_to_all x1, blocking collectives, per_device(): lax.all_to_all(send, 'dp', split_axis=0, concat_axis=0, tiled=True)  38.3 us
    all_to_all x1, blocking collectives, per_device(): lax.all_to_all(parts, 'tensor', 0, 0, axis_index_groups=classes, tiled=True)  27.7 us
    all_to_all x1, waiting for transfers between devices, per_device(): lax.all_to_all(sent, 'tensor', 0, 0, axis_index_groups=classes, tiled=True)  18.7 us
    pallas_call x1, Pallas kernels, backward(): pl.pallas_call(backward_kernel, in_specs=[SCALAR] + in_vmem(6) + [ANYWHER...  9.18 us
    ppermute x1, starting transfers between devices, per_device(): other = lax.ppermute(cut, 'tensor', swap)  8.73 us
    pallas_call x1, Pallas kernels, forward(): pl.pallas_call(forward_kernel, in_specs=[SCALAR, ANYWHERE] + in_vmem(1) +...  4.86 us
    all_to_all x1, starting transfers between devices, per_device(): lax.all_to_all(sent, 'tensor', 0, 0, axis_index_groups=classes, tiled=True)  4.29 us
    squeeze x1, local copies, waits for them, and re-layouts, per_device(): cut = lax.dynamic_index_in_dim(pairs, 1 - core, 1, False)  2.82 us
  transfers between devices with their start and end apart: 5, of which 2 were waited for; matrix products, arithmetic and copies ran while one was open for 3% of the time, Pallas kernels for 0%

profile of v2, /device:TPU:1, one launch (start us, length us, event | category | flops | bytes accessed | tf_op | source)
XLA Modules:
  0.0 129.8 jit_solution(651115833881045739)
XLA Ops:
  0.0 0.0 copy-start
  0.0 0.0 copy-start.3
  0.0 0.0 copy-start.4
  0.0 0.0 copy-start.1
  0.0 2.8 %dynamic-slice_bitcast_fusion = bf16[8,384,256]{2,1,0:T(8,128)(2,1)} fusion(bf16[8,2,384,256]{3,2,1,0:T(8,128)(2,1)} %bitcast.10, s32[]{:T(128)S(6)} %select_n.31), kind=kLoop, calls=%fused_computation.2 | loop fusion | bytes 3145732 | tf_op jit(solution)/shard_map/jit(dynamic_index_in_dim)/squeeze | solution.py:284
  2.8 8.7 %collective-permute-start = (bf16[8,384,256]{2,1,0:T(8,128)(2,1)}, bf16[8,384,256]{2,1,0:T(8,128)(2,1)}, u32[]{:S(2)}, u32[]{:S(2)}) collective-permute-start(bf16[8,384,256]{2,1,0:T(8,128)(2,1)} %dynamic-slice_bitcast_fusion), channel_id=1, source_target_pairs={{0,1},{1,0},{2,3},{3,2},{4,5},{5,4},{6,7},{7,6},{8,9},{9,8},{10,11... | collective-permute-start | bytes 4718600 | tf_op jit(solution)/shard_map/ppermute | solution.py:285
  11.6 0.0 copy-done.3
  11.6 0.0 copy-done
  11.6 1.0 multiply_reduce_fusion
  12.6 0.0 copy-start.2
  12.6 0.0 copy-start.5
  12.6 0.0 copy-done.4
  12.7 2.1 %collective-permute-start.2 = (f32[3,256]{1,0:T(4,128)S(1)}, f32[3,256]{1,0:T(4,128)S(1)}, u32[]{:S(2)}, u32[]{:S(2)}) collective-permute-start(f32[3,256]{1,0:T(4,128)S(1)} %pad_maximum_fusion.vec_ref), channel_id=1, source_target_pairs={{0,1},{1,0},{2,3},{3,2},{4,5},{5,4},{6,7},{7,6},{8,9},{9,8},{10,11... | collective-permute-start | bytes 9224 | tf_op jit(solution)/shard_map/ppermute | solution.py:290
  14.7 0.0 copy-done.1
  14.7 1.3 %broadcast_in_dim.14 = bf16[8,256,384]{2,1,0:T(8,128)(2,1)} broadcast(bf16[256,384]{1,0:T(8,128)(2,1)S(1)} %copy-done.1), dimensions={1,2} | broadcast | bytes 1769472 | tf_op jit(solution)/shard_map/broadcast_in_dim | solution.py:280
  16.0 4.3 %all-to-all-start = ((bf16[8,256,384]{2,1,0:T(8,128)(2,1)}), bf16[8,256,384]{2,1,0:T(8,128)(2,1)}, u32[]{:S(2)}, u32[]{:S(2)}) async-start(bf16[8,256,384]{2,1,0:T(8,128)(2,1)} %broadcast_in_dim.14), calls=%async_computation | async-start | bytes 3145728 | tf_op jit(solution)/shard_map/all_to_all | solution.py:281
  20.3 0.0 copy-done.2
  20.3 2.4 %collective-permute-start.1 = (bf16[256,256]{1,0:T(8,128)(2,1)S(1)}, bf16[256,256]{1,0:T(8,128)(2,1)}, u32[]{:S(2)}, u32[]{:S(2)}) collective-permute-start(bf16[256,256]{1,0:T(8,128)(2,1)S(1)} %copy-done.2), channel_id=1, source_target_pairs={{0,1},{1,0},{2,3},{3,2},{4,5},{5,4},{6,7},{7,6},{8,9},{9,8},{10,11... | collective-permute-start | bytes 393224 | tf_op jit(solution)/shard_map/ppermute | solution.py:286
  22.8 0.0 copy-done.5
  22.8 0.2 convert_reduce_fusion
  23.0 0.1 iota_add_fusion
  23.1 1.5 %select_reduce_fusion = s32[32,128]{1,0:T(8,128)S(1)} fusion(s32[256]{0:T(256)S(1)} %get-tuple-element.24, s32[256]{0:T(256)S(1)} %multiply_add_fusion, s32[32,128]{1,0:T(8,128)S(1)} %iota_add_fusion, pred[128]{0:T(512)(128)(4,1)S(1)} %iota_compare_fusion.1), kind=kLoop, calls=%fused_computation.1 | loop fusion | flops 4190208 | bytes 34944 | tf_op jit(solution)/shard_map/reduce_sum | solution.py:305
  24.6 0.0 collective-permute-done.2.veco_ref
  24.6 0.0 collective-permute-done.1.upo_ref
  24.6 18.7 %all-to-all-done.x_any = bf16[8,256,384]{2,1,0:T(8,128)(2,1)} async-done(((bf16[8,256,384]{2,1,0:T(8,128)(2,1)}), bf16[8,256,384]{2,1,0:T(8,128)(2,1)}, u32[]{:S(2)}, u32[]{:S(2)}) %all-to-all-start) | async-done | bytes 1572896 | tf_op jit(solution)/shard_map/all_to_all | solution.py:281
  43.3 0.0 collective-permute-done.other_any
  43.3 4.9 %forward.1.q_ref = f32[256,640]{1,0:T(8,128)S(1)} custom-call(s32[1]{0:T(128)} %bitcast.core_ref, bf16[8,256,384]{2,1,0:T(8,128)(2,1)} %all-to-all-done.x_any, f32[8,2,1,384]{3,2,1,0:T(1,128)S(1)} %bitcast.15, bf16[8,2,384,256]{3,2,1,0:T(8,128)(2,1)S(1)} %bitcast.12, bf16[8,384,256]{2,1,0:T(8,128)(2,1)} %collective-permute-done.other_any), custom_call_target="tpu_custom_call" | custom-call | tf_op jit(solution)/shard_map/forward/pallas_call | solution.py:77
  48.2 2.7 %collective-permute-start.3 = (f32[256,640]{1,0:T(8,128)S(1)}, f32[256,640]{1,0:T(8,128)S(1)}, u32[]{:S(2)}, u32[]{:S(2)}) collective-permute-start(f32[256,640]{1,0:T(8,128)S(1)} %forward.1.q_ref), channel_id=1, source_target_pairs={{0,1},{1,0},{2,3},{3,2},{4,5},{5,4},{6,7},{7,6},{8,9},{9,8},{10,11... | collective-permute-start | bytes 1966088 | tf_op jit(solution)/shard_map/ppermute | solution.py:313
  50.9 1.7 %collective-permute-done.3.got_ref = f32[256,640]{1,0:T(8,128)S(1)} collective-permute-done((f32[256,640]{1,0:T(8,128)S(1)}, f32[256,640]{1,0:T(8,128)S(1)}, u32[]{:S(2)}, u32[]{:S(2)}) %collective-permute-start.3) | collective-permute-done | bytes 655392 | tf_op jit(solution)/shard_map/ppermute | solution.py:313
  52.6 9.2 %backward.1 = (bf16[8,272,384]{2,1,0:T(8,128)(2,1)S(1)}, f32[256,128]{1,0:T(8,128)S(1)}) custom-call(s32[1]{0:T(128)} %bitcast.core_ref, f32[256,640]{1,0:T(8,128)S(1)} %forward.1.q_ref, f32[256,640]{1,0:T(8,128)S(1)} %collective-permute-done.3.got_ref, bf16[256,256]{1,0:T(8,128)(2,1)S(1)} %copy-done.2, bf16[256,256]{1,0:T(8,128)(2,1)} %collective-permute-done.1.upo_ref, ...), custom_call_target="tpu_custom_call" | custom-call | tf_op jit(solution)/shard_map/backward/pallas_call | solution.py:177
  61.8 27.7 %all_to_all.15.back_ref = bf16[8,272,384]{2,1,0:T(8,128)(2,1)S(1)} all-to-all(bf16[8,272,384]{2,1,0:T(8,128)(2,1)S(1)} %get-tuple-element.18), channel_id=1, replica_groups={{0,2,4,6,8,10,12,14},{1,3,5,7,9,11,13,15},{16,18,20,22,24,26,28,30},{17..., dimensions={0} | all-to-all | bytes 3342336 | tf_op jit(solution)/shard_map/all_to_all | solution.py:315
  89.5 0.8 finish.1
  90.3 38.3 %all_to_all.16.got_ref = bf16[32,56,128]{2,1,0:T(8,128)(2,1)S(1)} all-to-all(bf16[32,56,128]{2,1,0:T(8,128)(2,1)S(1)} %finish.1), channel_id=1, replica_groups=mesh['dp'=32,'tensor'=16] {'dp'}, dimensions={0} | all-to-all | bytes 917504 | tf_op jit(solution)/shard_map/all_to_all | solution.py:317
  128.6 1.2 land.1
  (8 shorter events, 0.1 us)
Async XLA Ops:
  0.0 11.6 %copy-start = (bf16[6144,256]{1,0:T(8,128)(2,1)S(1)}, bf16[6144,256]{1,0:T(8,128)(2,1)}, u32[]{:S(2)}) copy-start(bf16[6144,256]{1,0:T(8,128)(2,1)} %param.8) | copy-start | bytes 9437188
  0.0 11.6 %copy-start.3 = (f32[6144]{0:T(1024)S(1)}, f32[6144]{0:T(1024)}, u32[]{:S(2)}) copy-start(f32[6144]{0:T(1024)} %param.10) | copy-start | bytes 73732
  0.0 12.6 %copy-start.4 = (f32[256]{0:T(256)S(1)}, f32[256]{0:T(256)}, u32[]{:S(2)}) copy-start(f32[256]{0:T(256)} %param.9) | copy-start | bytes 3076
  0.0 14.7 %copy-start.1 = (bf16[256,384]{1,0:T(8,128)(2,1)S(1)}, bf16[256,384]{1,0:T(8,128)(2,1)}, u32[]{:S(2)}) copy-start(bf16[256,384]{1,0:T(8,128)(2,1)} %x_ref.1) | copy-start | bytes 589828
  2.8 40.5 %collective-permute-start = (bf16[8,384,256]{2,1,0:T(8,128)(2,1)}, bf16[8,384,256]{2,1,0:T(8,128)(2,1)}, u32[]{:S(2)}, u32[]{:S(2)}) collective-permute-start(bf16[8,384,256]{2,1,0:T(8,128)(2,1)} %dynamic-slice_bitcast_fusion), channel_id=1, source_target_pairs={{0,1},{1,0},{2,3},{3,2},{4,5},{5,4},{6,7},{7,6},{8,9},{9,8},{10,11... | collective-permute-start | bytes 4718600 | tf_op jit(solution)/shard_map/ppermute | solution.py:285
  12.6 7.7 %copy-start.2 = (bf16[256,256]{1,0:T(8,128)(2,1)S(1)}, bf16[256,256]{1,0:T(8,128)(2,1)}, u32[]{:S(2)}) copy-start(bf16[256,256]{1,0:T(8,128)(2,1)} %up_ref.1) | copy-start | bytes 393220
  12.6 10.2 %copy-start.5 = (s32[256]{0:T(256)S(1)}, s32[256]{0:T(256)}, u32[]{:S(2)}) copy-start(s32[256]{0:T(256)} %param.11) | copy-start | bytes 3076
  12.7 12.0 %collective-permute-start.2 = (f32[3,256]{1,0:T(4,128)S(1)}, f32[3,256]{1,0:T(4,128)S(1)}, u32[]{:S(2)}, u32[]{:S(2)}) collective-permute-start(f32[3,256]{1,0:T(4,128)S(1)} %pad_maximum_fusion.vec_ref), channel_id=1, source_target_pairs={{0,1},{1,0},{2,3},{3,2},{4,5},{5,4},{6,7},{7,6},{8,9},{9,8},{10,11... | collective-permute-start | bytes 9224 | tf_op jit(solution)/shard_map/ppermute | solution.py:290
  16.0 27.3 %all-to-all-start = ((bf16[8,256,384]{2,1,0:T(8,128)(2,1)}), bf16[8,256,384]{2,1,0:T(8,128)(2,1)}, u32[]{:S(2)}, u32[]{:S(2)}) async-start(bf16[8,256,384]{2,1,0:T(8,128)(2,1)} %broadcast_in_dim.14), calls=%async_computation | async-start | bytes 3145728 | tf_op jit(solution)/shard_map/all_to_all | solution.py:281
  20.3 4.3 %collective-permute-start.1 = (bf16[256,256]{1,0:T(8,128)(2,1)S(1)}, bf16[256,256]{1,0:T(8,128)(2,1)}, u32[]{:S(2)}, u32[]{:S(2)}) collective-permute-start(bf16[256,256]{1,0:T(8,128)(2,1)S(1)} %copy-done.2), channel_id=1, source_target_pairs={{0,1},{1,0},{2,3},{3,2},{4,5},{5,4},{6,7},{7,6},{8,9},{9,8},{10,11... | collective-permute-start | bytes 393224 | tf_op jit(solution)/shard_map/ppermute | solution.py:286
  48.2 4.4 %collective-permute-start.3 = (f32[256,640]{1,0:T(8,128)S(1)}, f32[256,640]{1,0:T(8,128)S(1)}, u32[]{:S(2)}, u32[]{:S(2)}) collective-permute-start(f32[256,640]{1,0:T(8,128)S(1)} %forward.1.q_ref), channel_id=1, source_target_pairs={{0,1},{1,0},{2,3},{3,2},{4,5},{5,4},{6,7},{7,6},{8,9},{9,8},{10,11... | collective-permute-start | bytes 1966088 | tf_op jit(solution)/shard_map/ppermute | solution.py:313

commit v3 on v2

v3 whole, which is shorter than its diff:
```python
import jax
import jax.numpy as jnp
from jax import lax
from jax.experimental import pallas as pl
from jax.experimental.pallas import tpu as pltpu
from jax.sharding import PartitionSpec as P


epsilon = 1e-05
f32, bf16 = jnp.float32, jnp.bfloat16
PAD = 16
CAPACITY = 16
NT = (((1,), (1,)), ((), ()))


def in_vmem(n):
    return [pl.BlockSpec(memory_space=pltpu.VMEM) for _ in range(n)]


def held(*arrays):
    return [pltpu.with_memory_space_constraint(a, pltpu.VMEM) for a in arrays]


PARAMS = pltpu.CompilerParams(vmem_limit_bytes=16 * 1024 * 1024)


ANYWHERE = pl.BlockSpec(memory_space=pl.ANY)
SCALAR = pl.BlockSpec(memory_space=pltpu.SMEM)


def weight_copies(core, first, weight_any, other_any, weight_ref, w_sem, o_sem):
    slots, _, width = weight_ref.shape
    blocks = other_any.shape[0]
    copies = []
    for p in range(slots):
        k = (first + p) % blocks
        copies.append(
            (
                pltpu.make_async_copy(
                    weight_any.at[k, core], weight_ref.at[p, :, : width // 2], w_sem.at[p]
                ),
                pltpu.make_async_copy(other_any.at[k], weight_ref.at[p, :, width // 2 :], o_sem.at[p]),
            )
        )
    return copies


def forward_kernel(
    place_ref, near_any, far_any, gain_ref, weight_any, other_any, q_ref, x_ref, weight_ref, x_sem, w_sem, o_sem
):
    blocks, rows, feats = x_ref.shape
    width = weight_ref.shape[2]
    half = blocks // 2
    core, first = place_ref[0], place_ref[1]
    x_copies = [
        pltpu.make_async_copy((near_any if p < half else far_any).at[p % half], x_ref.at[p], x_sem.at[p])
        for p in range(blocks)
    ]
    w_copies = weight_copies(core, first, weight_any, other_any, weight_ref, w_sem, o_sem)
    for copy in x_copies:
        copy.start()
    for pair in w_copies:
        for copy in pair:
            copy.start()
    total = jnp.zeros((rows, 128), f32)
    for p in range(blocks):
        x_copies[p].wait()
        for j in range(0, feats, 128):
            total += x_ref[p, :, j : j + 128].astype(f32)
    mean = jnp.sum(total, axis=1, keepdims=True) / (blocks * feats)
    spread = jnp.zeros((rows, 128), f32)
    for p in range(blocks):
        centred = x_ref[p].astype(f32) - mean
        square = centred * centred
        for j in range(0, feats, 128):
            spread += square[:, j : j + 128]
        scaled = (centred * gain_ref[(first + p) % blocks, core]).astype(bf16)
        for copy in w_copies[p]:
            copy.wait()
        term = jnp.dot(scaled, weight_ref[p], preferred_element_type=f32)
        if p == 0:
            q_ref[:, :width] = term
        else:
            q_ref[:, :width] += term
    spread = jnp.sum(spread, axis=1, keepdims=True) / (blocks * feats)
    lane = lax.broadcasted_iota(jnp.int32, (rows, 128), 1)
    q_ref[:, width:] = jnp.where(lane == 0, mean, spread)


def forward(place, near, far, gain, weight, other):
    _, rows, feats = near.shape
    blocks, _, width = other.shape
    return pl.pallas_call(
        forward_kernel,
        in_specs=[SCALAR, ANYWHERE, ANYWHERE] + in_vmem(1) + [ANYWHERE, ANYWHERE],
        out_specs=in_vmem(1)[0],
        out_shape=jax.ShapeDtypeStruct((rows, 2 * width + 128), f32),
        scratch_shapes=[
            pltpu.VMEM((blocks, rows, feats), bf16),
            pltpu.VMEM((blocks, feats, 2 * width), bf16),
            pltpu.SemaphoreType.DMA((blocks,)),
            pltpu.SemaphoreType.DMA((blocks,)),
            pltpu.SemaphoreType.DMA((blocks,)),
        ],
        compiler_params=PARAMS,
        name="forward",
    )(place, near, far, gain, weight, other)


def split_sums(first, second):
    rows = first.shape[0]
    lane = lax.broadcasted_iota(jnp.int32, (rows, 128), 1)
    value = jnp.where(lane < 2, first, second)
    high = value.astype(bf16).astype(f32)
    return jnp.where(lane % 2 == 0, high, value - high).T[:PAD]


def backward_kernel(
    place_ref,
    q_ref,
    got_ref,
    up_ref,
    upo_ref,
    vec_ref,
    veco_ref,
    weight_any,
    other_any,
    p_any,
    pg_ref,
    st_ref,
    weight_ref,
    p_ref,
    w_sem,
    o_sem,
    p_sem,
):
    half, feats, width = weight_ref.shape
    width = width // 2
    rows = q_ref.shape[0]
    core, first = place_ref[0], place_ref[1]
    w_copies = weight_copies(core, first + half, weight_any, other_any, weight_ref, w_sem, o_sem)
    p_copies = [pltpu.make_async_copy(p_ref.at[p], p_any.at[p], p_sem.at[p]) for p in range(half)]
    for pair in w_copies:
        for copy in pair:
            copy.start()
    mine, theirs = q_ref[:, 2 * width :], got_ref[:, 2 * width :]
    mean_here, mean_there = mine[:, 0:1], theirs[:, 0:1]
    gap = 0.5 * (mean_here - mean_there)
    mean = 0.5 * (mean_here + mean_there)
    variance = 0.5 * (mine[:, 1:2] + theirs[:, 1:2]) + gap * gap
    inv_std = lax.rsqrt(variance + epsilon)
    lane = lax.broadcasted_iota(jnp.int32, (rows, 128), 1)
    st_ref[...] = jnp.where(lane == 0, mean, inv_std)
    gap = gap * jnp.where(core == 0, 1.0, -1.0)

    def grad(summed, up, vec):
        raw = inv_std * (summed + gap * (vec[1:2, :] - vec[2:3, :]))
        preact = raw + vec[0:1, :]
        gate = 1.0 / (1.0 + jnp.exp(-preact))
        pg = (up.astype(f32) * gate * (1.0 + preact * (1.0 - gate))).astype(bf16)
        wide = pg.astype(f32)
        scale = vec[1:2, :] + vec[2:3, :]
        return (
            pg,
            jnp.sum(wide * scale, axis=1, keepdims=True),
            jnp.sum(wide * raw, axis=1, keepdims=True),
        )

    pg, sum_g, sum_gu = grad(q_ref[:, :width] + got_ref[:, width : 2 * width], up_ref[...], vec_ref[...])
    pgo, sum_go, sum_guo = grad(
        q_ref[:, width : 2 * width] + got_ref[:, :width], upo_ref[...], veco_ref[...]
    )
    both = jnp.concatenate([pg, pgo], axis=1)
    pg_ref[...] = both
    tail = split_sums(sum_g + sum_go, sum_gu + sum_guo).astype(bf16)
    tail = jnp.concatenate([tail, jnp.zeros((PAD, feats - rows), bf16)], axis=1)
    for p in range(half):
        for copy in w_copies[p]:
            copy.wait()
        p_ref[p, :rows] = lax.dot_general(both, weight_ref[p], NT, preferred_element_type=f32).astype(bf16)
        p_ref[p, rows:] = tail
        p_copies[p].start()
    for copy in p_copies:
        copy.wait()


def backward(place, q, got, up, upo, vec, veco, weight, other):
    blocks, feats, width = other.shape
    rows, half = q.shape[0], blocks // 2
    return pl.pallas_call(
        backward_kernel,
        in_specs=[SCALAR] + in_vmem(6) + [ANYWHERE, ANYWHERE],
        out_specs=[ANYWHERE] + in_vmem(2),
        out_shape=[
            pltpu.HBM((half, rows + PAD, feats), bf16),
            pltpu.HBM((rows, 2 * width), bf16),
            jax.ShapeDtypeStruct((rows, 128), f32),
        ],
        scratch_shapes=[
            pltpu.VMEM((half, feats, 2 * width), bf16),
            pltpu.VMEM((half, rows + PAD, feats), bf16),
            pltpu.SemaphoreType.DMA((half,)),
            pltpu.SemaphoreType.DMA((half,)),
            pltpu.SemaphoreType.DMA((half,)),
        ],
        compiler_params=PARAMS,
        name="backward",
    )(place, q, got, up, upo, vec, veco, weight, other)


def second_kernel(place_ref, pg_ref, weight_any, other_any, p_any, weight_ref, p_ref, w_sem, o_sem, p_sem):
    half = p_ref.shape[0]
    core, first = place_ref[0], place_ref[1]
    w_copies = weight_copies(core, first, weight_any, other_any, weight_ref, w_sem, o_sem)
    p_copies = [pltpu.make_async_copy(p_ref.at[p], p_any.at[p], p_sem.at[p]) for p in range(half)]
    for pair in w_copies:
        for copy in pair:
            copy.start()
    both = pg_ref[...]
    for p in range(half):
        for copy in w_copies[p]:
            copy.wait()
        p_ref[p] = lax.dot_general(both, weight_ref[p], NT, preferred_element_type=f32).astype(bf16)
        p_copies[p].start()
    for copy in p_copies:
        copy.wait()


def second(place, pg, weight, other):
    blocks, feats, width = other.shape
    rows, half = pg.shape[0], blocks // 2
    return pl.pallas_call(
        second_kernel,
        in_specs=[SCALAR] + in_vmem(1) + [ANYWHERE, ANYWHERE],
        out_specs=ANYWHERE,
        out_shape=pltpu.HBM((half, rows, feats), bf16),
        scratch_shapes=[
            pltpu.VMEM((half, feats, 2 * width), bf16),
            pltpu.VMEM((half, rows, feats), bf16),
            pltpu.SemaphoreType.DMA((half,)),
            pltpu.SemaphoreType.DMA((half,)),
            pltpu.SemaphoreType.DMA((half,)),
        ],
        compiler_params=PARAMS,
        name="second",
    )(place, pg, weight, other)


def gather_sums(tail):
    sums = tail.T
    return sums[:, 0:1] + sums[:, 1:2], sums[:, 2:3] + sums[:, 3:4]


def meet_kernel(part_any, sum_ref, own_ref, part_ref, sem):
    blocks, padded, feats = part_ref.shape
    rows = padded - PAD
    copies = [pltpu.make_async_copy(part_any.at[p], part_ref.at[p], sem.at[p]) for p in range(blocks)]
    for copy in copies:
        copy.start()
    copies[0].wait()
    total = part_ref[0].astype(f32)
    for p in range(1, blocks):
        copies[p].wait()
        total += part_ref[p].astype(f32)
    sum_g, sum_gu = gather_sums(total[rows : rows + 8, :rows])
    lane = lax.broadcasted_iota(jnp.int32, (rows, 128), 1)
    own_ref[...] = jnp.where(lane == 0, sum_g, sum_gu)
    sum_ref[:rows] = total[:rows].astype(bf16)
    tail = split_sums(sum_g, sum_gu).astype(bf16)
    sum_ref[rows:] = jnp.concatenate([tail, jnp.zeros((PAD, feats - rows), bf16)], axis=1)


def meet(part):
    blocks, padded, feats = part.shape
    return pl.pallas_call(
        meet_kernel,
        in_specs=[ANYWHERE],
        out_specs=in_vmem(2),
        out_shape=[pltpu.VMEM((padded, feats), bf16), pltpu.VMEM((padded - PAD, 128), f32)],
        scratch_shapes=[pltpu.VMEM(part.shape, bf16), pltpu.SemaphoreType.DMA((blocks,))],
        compiler_params=PARAMS,
        name="meet",
    )(part)


def finish_kernel(back_ref, across_ref, own_ref, x_ref, st_ref, gain_ref, target_ref, slot_ref, send_ref):
    blocks, rows, feats = back_ref.shape
    owners = send_ref.shape[0]
    total = across_ref[:rows].astype(f32)
    for p in range(blocks):
        total += back_ref[p].astype(f32)
    sum_g, sum_gu = gather_sums(across_ref[rows:, :rows].astype(f32)[:8])
    count = 4 * blocks * feats
    mean_g = (sum_g + own_ref[:, 0:1]) / count
    mean_gu = (sum_gu + own_ref[:, 1:2]) / count
    mean, inv_std = st_ref[:, 0:1], st_ref[:, 1:2]
    unit = (x_ref[...].astype(f32) - mean) * inv_std
    grad = (inv_std * (total * gain_ref[...] - mean_g - unit * mean_gu)).astype(bf16)
    slots = owners * CAPACITY
    placing = lax.broadcasted_iota(jnp.int32, (slots, rows), 0) == target_ref[...]
    placed = jnp.dot(
        jnp.where(placing, 1.0, 0.0).astype(bf16), grad, preferred_element_type=f32
    ).astype(bf16)
    placed = placed.reshape(owners, CAPACITY, feats)
    for k in range(feats // 128):
        send_ref[:, k * CAPACITY : (k + 1) * CAPACITY, :] = placed[:, :, k * 128 : (k + 1) * 128]
    send_ref[:, feats // 128 * CAPACITY :, :] = jnp.broadcast_to(
        slot_ref[...][:, None, :], (owners, 8, 128)
    )


def finish(back, across, own, x, st, gain, target, slot):
    owners = slot.shape[0]
    return pl.pallas_call(
        finish_kernel,
        in_specs=in_vmem(8),
        out_specs=in_vmem(1)[0],
        out_shape=pltpu.VMEM((owners, x.shape[1] // 128 * CAPACITY + 8, 128), bf16),
        compiler_params=PARAMS,
        name="finish",
    )(*held(back, across, own, x, st, gain, target, slot))


def landing_kernel(got_ref, o_ref):
    rows, feats = o_ref.shape
    owners = got_ref.shape[0]
    slots = owners * CAPACITY
    pieces = feats // 128
    held_slots = got_ref[:, pieces * CAPACITY, :].astype(bf16)
    spread = lax.broadcasted_iota(jnp.int32, (128, slots), 0) == (
        lax.broadcasted_iota(jnp.int32, (128, slots), 1) % CAPACITY
    )
    every = jnp.dot(held_slots, jnp.where(spread, 1.0, 0.0).astype(bf16), preferred_element_type=f32)
    own = lax.broadcasted_iota(jnp.int32, (owners, slots), 0) == (
        lax.broadcasted_iota(jnp.int32, (owners, slots), 1) // CAPACITY
    )
    slot = jnp.sum(jnp.where(own, every, 0.0), axis=0, keepdims=True).astype(jnp.int32)
    landing = lax.broadcasted_iota(jnp.int32, (rows, slots), 0) == slot
    landing = jnp.where(landing, 1.0, 0.0).astype(bf16)
    for k in range(pieces):
        piece = got_ref[:, k * CAPACITY : (k + 1) * CAPACITY, :].reshape(slots, 128)
        o_ref[:, k * 128 : (k + 1) * 128] = jnp.dot(
            landing, piece, preferred_element_type=f32
        ).astype(bf16)


def land(got, rows, feats):
    return pl.pallas_call(
        landing_kernel,
        in_specs=in_vmem(1),
        out_specs=in_vmem(1)[0],
        out_shape=jax.ShapeDtypeStruct((rows, feats), bf16),
        compiler_params=PARAMS,
        name="land",
    )(*held(got))


def per_device(inputs, upstream, proj_weight, proj_bias, norm_gain, home_rows):
    rows, feats = inputs.shape
    width = upstream.shape[1]
    n_tensor, owners = lax.axis_size("tensor"), lax.axis_size("dp")
    chips = n_tensor // 2
    side = chips // 2
    me = lax.axis_index("tensor")
    core, first = me % 2, me // (2 * side) * side
    swap = [(t, t ^ 1) for t in range(n_tensor)]
    cross = [(t, (t + 2 * side) % n_tensor) for t in range(n_tensor)]
    lines = [[2 * side * h + 2 * k + c for k in range(side)] for h in range(2) for c in range(2)]
    place = jnp.stack([core, first]).astype(jnp.int32)

    def exchange(blocks):
        return lax.all_to_all(blocks, "tensor", 0, 0, axis_index_groups=lines, tiled=True)

    facing = lax.ppermute(inputs, "tensor", cross)
    near = exchange(jnp.broadcast_to(inputs[None], (side, rows, feats)))
    far = exchange(jnp.broadcast_to(facing[None], (side, rows, feats)))

    pairs = proj_weight.reshape(chips, 2, feats, width)
    cut = lax.dynamic_index_in_dim(pairs, 1 - core, 1, False)
    other = lax.ppermute(cut, "tensor", swap)
    upo = lax.ppermute(upstream, "tensor", swap)
    gains = norm_gain.reshape(chips, 2, 1, feats)
    scales = jnp.sum(norm_gain.reshape(chips, 2, feats, 1) * pairs.astype(f32), axis=(0, 2))
    vec = jnp.concatenate([proj_bias[None], scales], axis=0)
    veco = lax.ppermute(vec, "tensor", swap)

    owner_of = home_rows // rows
    home_slot = home_rows % rows
    order_ids = jnp.arange(rows, dtype=jnp.int32)
    earlier = jnp.sum(
        ((owner_of[:, None] == owner_of[None, :]) & (order_ids[:, None] > order_ids[None, :])).astype(
            jnp.int32
        ),
        axis=1,
    )
    target = owner_of * CAPACITY + earlier
    lanes = jnp.arange(128, dtype=jnp.int32)
    held_at = (jnp.arange(owners, dtype=jnp.int32)[:, None] * CAPACITY + lanes[None, :])[:, :, None]
    match = (held_at == target[None, None, :]) & (lanes < CAPACITY)[None, :, None]
    slot = jnp.sum(jnp.where(match, home_slot[None, None, :] + 1, 0), axis=2) - 1
    slot = slot.astype(f32).astype(bf16)

    own_gain = lax.dynamic_index_in_dim(norm_gain.reshape(n_tensor, 1, feats), me, 0, False)
    near, far, other, upo, veco, slot, target, own_gain = lax.optimization_barrier(
        (near, far, other, upo, veco, slot, target, own_gain)
    )
    q = forward(place, near, far, gains, pairs, other)
    got = lax.ppermute(q, "tensor", swap)
    away, pg, st = backward(place, q, got, upstream, upo, vec, veco, pairs, other)
    met = exchange(away)
    home = second(place, pg, pairs, other)
    summed, own = meet(met)
    across = lax.ppermute(summed, "tensor", cross)
    back = exchange(home)
    send = finish(back, across, own, inputs, st, own_gain, target[None, :], slot)
    arrived = lax.all_to_all(send, "dp", split_axis=0, concat_axis=0, tiled=True)
    return land(arrived, rows, feats)


def solution(mesh):
    return jax.shard_map(
        per_device,
        mesh=mesh,
        in_specs=(
            P("dp", "tensor"),
            P("dp", "tensor"),
            P(None, "tensor"),
            P("tensor"),
            P(),
            P("dp"),
        ),
        out_specs=P("dp", "tensor"),
        check_vma=False,
    )
```

time: 132 us -> 142 us (1.076)
  the two profiles are of different devices: /device:TPU:1 before, /device:TPU:32 now
where the time goes in v3:
time: 142 us; the launch traced here: 141 us
  blocking collectives  43.4 us (31%)
  waiting for transfers between devices  39 us (27%)
  starting transfers between devices  31.8 us (22%)
  Pallas kernels  16.3 us (11%)
  local copies, waits for them, and re-layouts  7.31 us (5%)
  other arithmetic  2.87 us (2%)
    all_to_all x1, blocking collectives, per_device(): lax.all_to_all(send, 'dp', split_axis=0, concat_axis=0, tiled=True)  43.4 us
    all_to_all x4, waiting for transfers between devices, exchange(): lax.all_to_all(blocks, 'tensor', 0, 0, axis_index_groups=lines, tiled=True)  37 us
    all_to_all x4, starting transfers between devices, exchange(): lax.all_to_all(blocks, 'tensor', 0, 0, axis_index_groups=lines, tiled=True)  16.2 us
    ppermute x1, starting transfers between devices, per_device(): facing = lax.ppermute(inputs, 'tensor', cross)  5.1 us
    pallas_call x1, Pallas kernels, backward(): pl.pallas_call(backward_kernel, in_specs=[SCALAR] + in_vmem(6) + [ANYWHER...  4.65 us
    pallas_call x1, Pallas kernels, forward(): pl.pallas_call(forward_kernel, in_specs=[SCALAR, ANYWHERE, ANYWHERE] + in...  4.46 us
    pallas_call x1, Pallas kernels, second(): pl.pallas_call(second_kernel, in_specs=[SCALAR] + in_vmem(1) + [ANYWHERE,...  3.58 us
  transfers between devices with their start and end apart: 10, of which 5 were waited for; matrix products, arithmetic and copies ran while one was open for 4% of the time, Pallas kernels for 4%

profile of v3, /device:TPU:32, one launch (start us, length us, event | category | flops | bytes accessed | tf_op | source)
XLA Modules:
  0.0 141.0 jit_solution(3659450596547267777)
XLA Ops:
  0.0 0.0 copy-start
  0.0 0.0 copy-start.6
  0.0 0.0 copy-start.7
  0.0 0.0 copy-start.1
  0.0 2.8 %dynamic-slice_bitcast_fusion = bf16[8,384,256]{2,1,0:T(8,128)(2,1)} fusion(bf16[8,2,384,256]{3,2,1,0:T(8,128)(2,1)} %bitcast.11, s32[]{:T(128)S(6)} %select_n.36), kind=kLoop, calls=%fused_computation.2 | loop fusion | bytes 3145732 | tf_op jit(solution)/shard_map/jit(dynamic_index_in_dim)/squeeze | solution.py:379
  2.8 0.0 copy-start.3
  2.8 0.0 copy-start.8
  2.8 2.0 %collective-permute-start.1 = (bf16[8,384,256]{2,1,0:T(8,128)(2,1)}, bf16[8,384,256]{2,1,0:T(8,128)(2,1)}, u32[]{:S(2)}, u32[]{:S(2)}) collective-permute-start(bf16[8,384,256]{2,1,0:T(8,128)(2,1)} %dynamic-slice_bitcast_fusion), channel_id=1, source_target_pairs={{0,1},{1,0},{2,3},{3,2},{4,5},{5,4},{6,7},{7,6},{8,9},{9,8},{10,11... | collective-permute-start | bytes 4718600 | tf_op jit(solution)/shard_map/ppermute | solution.py:380
  4.9 0.0 copy-done.6
  4.9 0.0 copy-done
  4.9 1.0 multiply_reduce_fusion
  5.9 0.0 copy-done.7
  6.0 2.4 %collective-permute-start.3 = (f32[3,256]{1,0:T(4,128)S(1)}, f32[3,256]{1,0:T(4,128)S(1)}, u32[]{:S(2)}, u32[]{:S(2)}) collective-permute-start(f32[3,256]{1,0:T(4,128)S(1)} %pad_maximum_fusion.vec_ref), channel_id=1, source_target_pairs={{0,1},{1,0},{2,3},{3,2},{4,5},{5,4},{6,7},{7,6},{8,9},{9,8},{10,11... | collective-permute-start | bytes 9224 | tf_op jit(solution)/shard_map/ppermute | solution.py:385
  8.4 0.0 copy-done.1
  8.4 5.1 %collective-permute-start = (bf16[256,384]{1,0:T(8,128)(2,1)S(1)}, bf16[256,384]{1,0:T(8,128)(2,1)}, u32[]{:S(2)}, u32[]{:S(2)}) collective-permute-start(bf16[256,384]{1,0:T(8,128)(2,1)S(1)} %copy-done.1), channel_id=1, source_target_pairs={{0,8},{1,9},{2,10},{3,11},{4,12},{5,13},{6,14},{7,15},{8,0},{9,1},... | collective-permute-start | bytes 589832 | tf_op jit(solution)/shard_map/ppermute | solution.py:374
  13.5 0.9 broadcast_in_dim.16
  14.4 4.3 %all-to-all-start = ((bf16[4,256,384]{2,1,0:T(8,128)(2,1)}), bf16[4,256,384]{2,1,0:T(8,128)(2,1)}, u32[]{:S(2)}, u32[]{:S(2)}) async-start(bf16[4,256,384]{2,1,0:T(8,128)(2,1)} %broadcast_in_dim.16), calls=%async_computation | async-start | bytes 1572864 | tf_op jit(solution)/shard_map/all_to_all | solution.py:372
  18.7 0.0 copy-done.3
  18.7 1.9 %collective-permute-start.2 = (bf16[256,256]{1,0:T(8,128)(2,1)S(1)}, bf16[256,256]{1,0:T(8,128)(2,1)}, u32[]{:S(2)}, u32[]{:S(2)}) collective-permute-start(bf16[256,256]{1,0:T(8,128)(2,1)S(1)} %copy-done.3), channel_id=1, source_target_pairs={{0,1},{1,0},{2,3},{3,2},{4,5},{5,4},{6,7},{7,6},{8,9},{9,8},{10,11... | collective-permute-start | bytes 393224 | tf_op jit(solution)/shard_map/ppermute | solution.py:381
  20.7 0.0 copy-done.8
  20.7 0.2 convert_reduce_fusion
  20.9 0.1 iota_add_fusion
  21.0 0.0 collective-permute-done
  21.0 10.2 %all-to-all-done.near_any = bf16[4,256,384]{2,1,0:T(8,128)(2,1)} async-done(((bf16[4,256,384]{2,1,0:T(8,128)(2,1)}), bf16[4,256,384]{2,1,0:T(8,128)(2,1)}, u32[]{:S(2)}, u32[]{:S(2)}) %all-to-all-start) | async-done | bytes 786464 | tf_op jit(solution)/shard_map/all_to_all | solution.py:372
  31.1 1.9 %broadcast_in_dim.17 = bf16[4,256,384]{2,1,0:T(8,128)(2,1)} broadcast(bf16[256,384]{1,0:T(8,128)(2,1)} %collective-permute-done), dimensions={1,2} | broadcast | bytes 983040 | tf_op jit(solution)/shard_map/broadcast_in_dim | solution.py:376
  33.1 4.2 %all-to-all-start.1 = ((bf16[4,256,384]{2,1,0:T(8,128)(2,1)}), bf16[4,256,384]{2,1,0:T(8,128)(2,1)}, u32[]{:S(2)}, u32[]{:S(2)}) async-start(bf16[4,256,384]{2,1,0:T(8,128)(2,1)} %broadcast_in_dim.17), calls=%async_computation.1 | async-start | bytes 1572864 | tf_op jit(solution)/shard_map/all_to_all | solution.py:372
  37.3 1.5 %select_reduce_fusion = s32[32,128]{1,0:T(8,128)S(1)} fusion(s32[256]{0:T(256)S(1)} %get-tuple-element.32, s32[256]{0:T(256)S(1)} %multiply_add_fusion, s32[32,128]{1,0:T(8,128)S(1)} %iota_add_fusion, pred[128]{0:T(512)(128)(4,1)S(1)} %iota_compare_fusion.1), kind=kLoop, calls=%fused_computation.1 | loop fusion | flops 4190208 | bytes 34944 | tf_op jit(solution)/shard_map/reduce_sum | solution.py:400
  38.8 0.1 pad_add_fusion.place_ref
  38.9 0.0 collective-permute-done.3.veco_ref
  38.9 0.0 collective-permute-done.2.upo_ref
  38.9 9.9 %all-to-all-done.1.far_any = bf16[4,256,384]{2,1,0:T(8,128)(2,1)} async-done(((bf16[4,256,384]{2,1,0:T(8,128)(2,1)}), bf16[4,256,384]{2,1,0:T(8,128)(2,1)}, u32[]{:S(2)}, u32[]{:S(2)}) %all-to-all-start.1) | async-done | bytes 786464 | tf_op jit(solution)/shard_map/all_to_all | solution.py:372
  48.8 0.0 collective-permute-done.1.other_any
  48.8 4.5 %forward.1.q_ref = f32[256,640]{1,0:T(8,128)S(1)} custom-call(s32[2]{0:T(128)S(1)} %pad_add_fusion.place_ref, bf16[4,256,384]{2,1,0:T(8,128)(2,1)} %all-to-all-done.near_any, bf16[4,256,384]{2,1,0:T(8,128)(2,1)} %all-to-all-done.1.far_any, f32[8,2,1,384]{3,2,1,0:T(1,128)S(1)} %bitcast.17, bf16[8,2,384,256]{3,2,1,0:T(8,128)(2,1)S(1)} %bitcast.13, ...), custom_call_target="tpu_custom_call" | custom-call | tf_op jit(solution)/shard_map/forward/pallas_call | solution.py:93
  53.2 1.9 %collective-permute-start.4 = (f32[256,640]{1,0:T(8,128)S(1)}, f32[256,640]{1,0:T(8,128)S(1)}, u32[]{:S(2)}, u32[]{:S(2)}) collective-permute-start(f32[256,640]{1,0:T(8,128)S(1)} %forward.1.q_ref), channel_id=1, source_target_pairs={{0,1},{1,0},{2,3},{3,2},{4,5},{5,4},{6,7},{7,6},{8,9},{9,8},{10,11... | collective-permute-start | bytes 1966088 | tf_op jit(solution)/shard_map/ppermute | solution.py:408
  55.2 2.1 %collective-permute-done.4.got_ref = f32[256,640]{1,0:T(8,128)S(1)} collective-permute-done((f32[256,640]{1,0:T(8,128)S(1)}, f32[256,640]{1,0:T(8,128)S(1)}, u32[]{:S(2)}, u32[]{:S(2)}) %collective-permute-start.4) | collective-permute-done | bytes 655392 | tf_op jit(solution)/shard_map/ppermute | solution.py:408
  57.2 4.7 %backward.1 = (bf16[4,272,384]{2,1,0:T(8,128)(2,1)}, bf16[256,512]{1,0:T(8,128)(2,1)}, f32[256,128]{1,0:T(8,128)S(1)}) custom-call(s32[2]{0:T(128)S(1)} %pad_add_fusion.place_ref, f32[256,640]{1,0:T(8,128)S(1)} %forward.1.q_ref, f32[256,640]{1,0:T(8,128)S(1)} %collective-permute-done.4.got_ref, bf16[256,256]{1,0:T(8,128)(2,1)S(1)} %copy-done.3, ...), custom_call_target="tpu_custom_call" | custom-call | tf_op jit(solution)/shard_map/backward/pallas_call | solution.py:190
  61.9 0.0 copy-start.4
  61.9 0.6 copy-done.4
  62.5 4.2 %all-to-all-start.3 = ((bf16[4,272,384]{2,1,0:T(8,128)(2,1)}), bf16[4,272,384]{2,1,0:T(8,128)(2,1)}, u32[]{:S(2)}, u32[]{:S(2)}) async-start(bf16[4,272,384]{2,1,0:T(8,128)(2,1)} %get-tuple-element.24), calls=%async_computation.3 | async-start | bytes 1671168 | tf_op jit(solution)/shard_map/all_to_all | solution.py:372
  66.8 0.0 copy-start.2
  66.8 0.9 copy-done.2
  67.7 0.0 copy-start.5
  67.7 3.6 %second.1 = bf16[4,256,384]{2,1,0:T(8,128)(2,1)} custom-call(s32[2]{0:T(128)S(1)} %pad_add_fusion.place_ref, bf16[256,512]{1,0:T(8,128)(2,1)S(1)} %copy-done.2, bf16[8,2,384,256]{3,2,1,0:T(8,128)(2,1)S(1)} %bitcast.15, bf16[8,384,256]{2,1,0:T(8,128)(2,1)} %collective-permute-done.1.other_any), custom_call_target="tpu_custom_call" | custom-call | tf_op jit(solution)/shard_map/second/pallas_call | solution.py:232
  71.3 8.9 %all-to-all-done.3.part_any = bf16[4,272,384]{2,1,0:T(8,128)(2,1)} async-done(((bf16[4,272,384]{2,1,0:T(8,128)(2,1)}), bf16[4,272,384]{2,1,0:T(8,128)(2,1)}, u32[]{:S(2)}, u32[]{:S(2)}) %all-to-all-start.3) | async-done | bytes 835616 | tf_op jit(solution)/shard_map/all_to_all | solution.py:372
  80.2 3.5 %all-to-all-start.2 = ((bf16[4,256,384]{2,1,0:T(8,128)(2,1)}), bf16[4,256,384]{2,1,0:T(8,128)(2,1)S(1)}, u32[]{:S(2)}, u32[]{:S(2)}) async-start(bf16[4,256,384]{2,1,0:T(8,128)(2,1)} %second.1), calls=%async_computation.2 | async-start | bytes 1572864 | tf_op jit(solution)/shard_map/all_to_all | solution.py:372
  83.7 1.7 %meet.1 = (bf16[272,384]{1,0:T(8,128)(2,1)S(1)}, f32[256,128]{1,0:T(8,128)S(1)}) custom-call(bf16[4,272,384]{2,1,0:T(8,128)(2,1)} %all-to-all-done.3.part_any), custom_call_target="tpu_custom_call" | custom-call | tf_op jit(solution)/shard_map/meet/pallas_call | solution.py:275
  85.5 2.2 %collective-permute-start.5 = (bf16[272,384]{1,0:T(8,128)(2,1)S(1)}, bf16[272,384]{1,0:T(8,128)(2,1)S(1)}, u32[]{:S(2)}, u32[]{:S(2)}) collective-permute-start(bf16[272,384]{1,0:T(8,128)(2,1)S(1)} %get-tuple-element.25), channel_id=1, source_target_pairs={{0,8},{1,9},{2,10},{3,11},{4,12},{5,13},{6,14},{7,15},{8,0},{9,1},... | collective-permute-start | bytes 626696 | tf_op jit(solution)/shard_map/ppermute | solution.py:413
  87.7 8.0 %all-to-all-done.2.back_ref = bf16[4,256,384]{2,1,0:T(8,128)(2,1)S(1)} async-done(((bf16[4,256,384]{2,1,0:T(8,128)(2,1)}), bf16[4,256,384]{2,1,0:T(8,128)(2,1)S(1)}, u32[]{:S(2)}, u32[]{:S(2)}) %all-to-all-start.2) | async-done | bytes 786464 | tf_op jit(solution)/shard_map/all_to_all | solution.py:372
  95.7 0.0 collective-permute-done.5.across_ref
  95.7 0.0 copy-done.5
  95.7 0.7 finish.1
  96.4 43.4 %all_to_all.25.got_ref = bf16[32,56,128]{2,1,0:T(8,128)(2,1)S(1)} all-to-all(bf16[32,56,128]{2,1,0:T(8,128)(2,1)S(1)} %finish.1), channel_id=1, replica_groups=mesh['dp'=32,'tensor'=16] {'dp'}, dimensions={0} | all-to-all | bytes 917504 | tf_op jit(solution)/shard_map/all_to_all | solution.py:416
  139.9 1.2 land.1
  (8 shorter events, 0.1 us)
Async XLA Ops:
  0.0 4.9 %copy-start = (bf16[6144,256]{1,0:T(8,128)(2,1)S(1)}, bf16[6144,256]{1,0:T(8,128)(2,1)}, u32[]{:S(2)}) copy-start(bf16[6144,256]{1,0:T(8,128)(2,1)} %param.8) | copy-start | bytes 9437188
  0.0 4.9 %copy-start.6 = (f32[6144]{0:T(1024)S(1)}, f32[6144]{0:T(1024)}, u32[]{:S(2)}) copy-start(f32[6144]{0:T(1024)} %param.10) | copy-start | bytes 73732
  0.0 5.9 %copy-start.7 = (f32[256]{0:T(256)S(1)}, f32[256]{0:T(256)}, u32[]{:S(2)}) copy-start(f32[256]{0:T(256)} %param.9) | copy-start | bytes 3076
  0.0 8.4 %copy-start.1 = (bf16[256,384]{1,0:T(8,128)(2,1)S(1)}, bf16[256,384]{1,0:T(8,128)(2,1)}, u32[]{:S(2)}) copy-start(bf16[256,384]{1,0:T(8,128)(2,1)} %x_ref.1) | copy-start | bytes 589828
  2.8 15.9 %copy-start.3 = (bf16[256,256]{1,0:T(8,128)(2,1)S(1)}, bf16[256,256]{1,0:T(8,128)(2,1)}, u32[]{:S(2)}) copy-start(bf16[256,256]{1,0:T(8,128)(2,1)} %up_ref.1) | copy-start | bytes 393220
  2.8 17.8 %copy-start.8 = (s32[256]{0:T(256)S(1)}, s32[256]{0:T(256)}, u32[]{:S(2)}) copy-start(s32[256]{0:T(256)} %param.11) | copy-start | bytes 3076
  2.8 45.9 %collective-permute-start.1 = (bf16[8,384,256]{2,1,0:T(8,128)(2,1)}, bf16[8,384,256]{2,1,0:T(8,128)(2,1)}, u32[]{:S(2)}, u32[]{:S(2)}) collective-permute-start(bf16[8,384,256]{2,1,0:T(8,128)(2,1)} %dynamic-slice_bitcast_fusion), channel_id=1, source_target_pairs={{0,1},{1,0},{2,3},{3,2},{4,5},{5,4},{6,7},{7,6},{8,9},{9,8},{10,11... | collective-permute-start | bytes 4718600 | tf_op jit(solution)/shard_map/ppermute | solution.py:380
  6.0 33.0 %collective-permute-start.3 = (f32[3,256]{1,0:T(4,128)S(1)}, f32[3,256]{1,0:T(4,128)S(1)}, u32[]{:S(2)}, u32[]{:S(2)}) collective-permute-start(f32[3,256]{1,0:T(4,128)S(1)} %pad_maximum_fusion.vec_ref), channel_id=1, source_target_pairs={{0,1},{1,0},{2,3},{3,2},{4,5},{5,4},{6,7},{7,6},{8,9},{9,8},{10,11... | collective-permute-start | bytes 9224 | tf_op jit(solution)/shard_map/ppermute | solution.py:385
  8.4 12.6 %collective-permute-start = (bf16[256,384]{1,0:T(8,128)(2,1)S(1)}, bf16[256,384]{1,0:T(8,128)(2,1)}, u32[]{:S(2)}, u32[]{:S(2)}) collective-permute-start(bf16[256,384]{1,0:T(8,128)(2,1)S(1)} %copy-done.1), channel_id=1, source_target_pairs={{0,8},{1,9},{2,10},{3,11},{4,12},{5,13},{6,14},{7,15},{8,0},{9,1},... | collective-permute-start | bytes 589832 | tf_op jit(solution)/shard_map/ppermute | solution.py:374
  14.4 16.7 %all-to-all-start = ((bf16[4,256,384]{2,1,0:T(8,128)(2,1)}), bf16[4,256,384]{2,1,0:T(8,128)(2,1)}, u32[]{:S(2)}, u32[]{:S(2)}) async-start(bf16[4,256,384]{2,1,0:T(8,128)(2,1)} %broadcast_in_dim.16), calls=%async_computation | async-start | bytes 1572864 | tf_op jit(solution)/shard_map/all_to_all | solution.py:372
  18.7 20.2 %collective-permute-start.2 = (bf16[256,256]{1,0:T(8,128)(2,1)S(1)}, bf16[256,256]{1,0:T(8,128)(2,1)}, u32[]{:S(2)}, u32[]{:S(2)}) collective-permute-start(bf16[256,256]{1,0:T(8,128)(2,1)S(1)} %copy-done.3), channel_id=1, source_target_pairs={{0,1},{1,0},{2,3},{3,2},{4,5},{5,4},{6,7},{7,6},{8,9},{9,8},{10,11... | collective-permute-start | bytes 393224 | tf_op jit(solution)/shard_map/ppermute | solution.py:381
  33.1 15.7 %all-to-all-start.1 = ((bf16[4,256,384]{2,1,0:T(8,128)(2,1)}), bf16[4,256,384]{2,1,0:T(8,128)(2,1)}, u32[]{:S(2)}, u32[]{:S(2)}) async-start(bf16[4,256,384]{2,1,0:T(8,128)(2,1)} %broadcast_in_dim.17), calls=%async_computation.1 | async-start | bytes 1572864 | tf_op jit(solution)/shard_map/all_to_all | solution.py:372
  53.2 4.0 %collective-permute-start.4 = (f32[256,640]{1,0:T(8,128)S(1)}, f32[256,640]{1,0:T(8,128)S(1)}, u32[]{:S(2)}, u32[]{:S(2)}) collective-permute-start(f32[256,640]{1,0:T(8,128)S(1)} %forward.1.q_ref), channel_id=1, source_target_pairs={{0,1},{1,0},{2,3},{3,2},{4,5},{5,4},{6,7},{7,6},{8,9},{9,8},{10,11... | collective-permute-start | bytes 1966088 | tf_op jit(solution)/shard_map/ppermute | solution.py:408
  61.9 0.7 copy-start.4
  62.5 17.7 %all-to-all-start.3 = ((bf16[4,272,384]{2,1,0:T(8,128)(2,1)}), bf16[4,272,384]{2,1,0:T(8,128)(2,1)}, u32[]{:S(2)}, u32[]{:S(2)}) async-start(bf16[4,272,384]{2,1,0:T(8,128)(2,1)} %get-tuple-element.24), calls=%async_computation.3 | async-start | bytes 1671168 | tf_op jit(solution)/shard_map/all_to_all | solution.py:372
  66.8 1.0 copy-start.2
  67.7 28.0 %copy-start.5 = (f32[256,128]{1,0:T(8,128)S(1)}, f32[256,128]{1,0:T(8,128)}, u32[]{:S(2)}) copy-start(f32[256,128]{1,0:T(8,128)} %copy-done.4) | copy-start | bytes 393220
  80.2 15.5 %all-to-all-start.2 = ((bf16[4,256,384]{2,1,0:T(8,128)(2,1)}), bf16[4,256,384]{2,1,0:T(8,128)(2,1)S(1)}, u32[]{:S(2)}, u32[]{:S(2)}) async-start(bf16[4,256,384]{2,1,0:T(8,128)(2,1)} %second.1), calls=%async_computation.2 | async-start | bytes 1572864 | tf_op jit(solution)/shard_map/all_to_all | solution.py:372
  85.5 10.3 %collective-permute-start.5 = (bf16[272,384]{1,0:T(8,128)(2,1)S(1)}, bf16[272,384]{1,0:T(8,128)(2,1)S(1)}, u32[]{:S(2)}, u32[]{:S(2)}) collective-permute-start(bf16[272,384]{1,0:T(8,128)(2,1)S(1)} %get-tuple-element.25), channel_id=1, source_target_pairs={{0,8},{1,9},{2,10},{3,11},{4,12},{5,13},{6,14},{7,15},{8,0},{9,1},... | collective-permute-start | bytes 626696 | tf_op jit(solution)/shard_map/ppermute | solution.py:413

commit v4 on v2

--- a/solution.py
+++ b/solution.py
@@ -28,51 +28,80 @@
 SCALAR = pl.BlockSpec(memory_space=pltpu.SMEM)
 
 
+def spread_kernel(x_ref, o_any, sem):
+    copies = [pltpu.make_async_copy(x_ref, o_any.at[b], sem.at[b]) for b in range(o_any.shape[0])]
+    for copy in copies:
+        copy.start()
+    for copy in copies:
+        copy.wait()
+
+
+def spread(x, blocks):
+    return pl.pallas_call(
+        spread_kernel,
+        in_specs=in_vmem(1),
+        out_specs=ANYWHERE,
+        out_shape=pltpu.HBM((blocks,) + x.shape, x.dtype),
+        scratch_shapes=[pltpu.SemaphoreType.DMA((blocks,))],
+        compiler_params=PARAMS,
+        name="spread",
+    )(x)
+
+
+def weight_copies(core, weight_any, other_any, weight_ref, w_sem, o_sem):
+    blocks, _, width = weight_ref.shape
+    half = width // 2
+    return [
+        (
+            pltpu.make_async_copy(weight_any.at[b, core], weight_ref.at[b, :, :half], w_sem.at[b]),
+            pltpu.make_async_copy(other_any.at[b], weight_ref.at[b, :, half:], o_sem.at[b]),
+        )
+        for b in range(blocks)
+    ]
+
+
 def forward_kernel(
-    core_ref, x_any, gain_ref, weight_any, other_any, q_ref, x_ref, weight_ref, other_ref, x_sem, w_sem, o_sem
+    core_ref, x_any, gain_ref, weight_any, other_any, q_ref, x_ref, weight_ref, x_sem, w_sem, o_sem
 ):
     blocks, rows, feats = x_ref.shape
-    width = other_ref.shape[2]
+    width = weight_ref.shape[2]
     core = core_ref[0]
     x_copies = [pltpu.make_async_copy(x_any.at[b], x_ref.at[b], x_sem.at[b]) for b in range(blocks)]
-    w_copies = [
-        pltpu.make_async_copy(weight_any.at[b, core], weight_ref.at[b], w_sem.at[b]) for b in range(blocks)
-    ]
-    o_copies = [
-        pltpu.make_async_copy(other_any.at[b], other_ref.at[b], o_sem.at[b]) for b in range(blocks)
-    ]
-    for copy in x_copies:
-        copy.start()
+    w_copies = weight_copies(core, weight_any, other_any, weight_ref, w_sem, o_sem)
     for b in range(blocks):
-        w_copies[b].start()
-        o_copies[b].start()
-    total = jnp.zeros((rows, feats), f32)
+        x_copies[b].start()
+        for copy in w_copies[b]:
+            copy.start()
+    x_copies[0].wait()
+    pivot = jnp.mean(x_ref[0].astype(f32), axis=1, keepdims=True)
+    total = jnp.zeros((rows, 128), f32)
+    square = jnp.zeros((rows, 128), f32)
     for b in range(blocks):
-        x_copies[b].wait()
-        total += x_ref[b].astype(f32)
-    mean = jnp.sum(total, axis=1, keepdims=True) / (blocks * feats)
-    spread = jnp.zeros((rows, feats), f32)
-    for b in range(blocks):
-        centred = x_ref[b].astype(f32) - mean
-        spread += centred * centred
-        scaled = (centred * gain_ref[b, core]).astype(bf16)
-        w_copies[b].wait()
-        o_copies[b].wait()
-        own = jnp.dot(scaled, weight_ref[b], preferred_element_type=f32)
-        other = jnp.dot(scaled, other_ref[b], preferred_element_type=f32)
+        if b > 0:
+            x_copies[b].wait()
+        moved = x_ref[b].astype(f32) - pivot
+        for j in range(0, feats, 128):
+            part = moved[:, j : j + 128]
+            total += part
+            square += part * part
+        scaled = (moved * gain_ref[b, core]).astype(bf16)
+        for copy in w_copies[b]:
+            copy.wait()
+        term = jnp.dot(scaled, weight_ref[b], preferred_element_type=f32)
         if b == 0:
-            q_ref[:, :width] = own
-            q_ref[:, width : 2 * width] = other
+            q_ref[:, :width] = term
         else:
-            q_ref[:, :width] += own
-            q_ref[:, width : 2 * width] += other
-    spread = jnp.sum(spread, axis=1, keepdims=True) / (blocks * feats)
+            q_ref[:, :width] += term
+    shift = jnp.sum(total, axis=1, keepdims=True) / (blocks * feats)
+    spread = jnp.sum(square, axis=1, keepdims=True) / (blocks * feats) - shift * shift
     lane = lax.broadcasted_iota(jnp.int32, (rows, 128), 1)
-    q_ref[:, 2 * width :] = jnp.where(lane == 0, mean, spread)
+    q_ref[:, width:] = jnp.where(
+        lane == 0, pivot, jnp.where(lane == 1, pivot + shift, jnp.maximum(spread, 0.0))
+    )
 
 
 def forward(core, x, gain, weight, other):
-    blocks, rows, _ = x.shape
+    blocks, rows, feats = x.shape
     width = other.shape[2]
     return pl.pallas_call(
         forward_kernel,
@@ -81,8 +110,7 @@
         out_shape=jax.ShapeDtypeStruct((rows, 2 * width + 128), f32),
         scratch_shapes=[
             pltpu.VMEM(x.shape, bf16),
-            pltpu.VMEM(other.shape, bf16),
-            pltpu.VMEM(other.shape, bf16),
+            pltpu.VMEM((blocks, feats, 2 * width), bf16),
             pltpu.SemaphoreType.DMA((blocks,)),
             pltpu.SemaphoreType.DMA((blocks,)),
             pltpu.SemaphoreType.DMA((blocks,)),
@@ -102,91 +130,72 @@
     veco_ref,
     weight_any,
     other_any,
-    p_any,
+    p_ref,
     st_ref,
     weight_ref,
-    other_ref,
-    p_ref,
     w_sem,
     o_sem,
-    p_sem,
 ):
-    blocks, feats, width = other_ref.shape
+    blocks, feats, width = weight_ref.shape
+    width = width // 2
     rows = q_ref.shape[0]
     core = core_ref[0]
-    w_copies = [
-        pltpu.make_async_copy(weight_any.at[b, core], weight_ref.at[b], w_sem.at[b]) for b in range(blocks)
-    ]
-    o_copies = [
-        pltpu.make_async_copy(other_any.at[b], other_ref.at[b], o_sem.at[b]) for b in range(blocks)
-    ]
-    p_copies = [pltpu.make_async_copy(p_ref.at[b], p_any.at[b], p_sem.at[b]) for b in range(blocks)]
-    for b in range(blocks):
-        w_copies[b].start()
-        o_copies[b].start()
+    w_copies = weight_copies(core, weight_any, other_any, weight_ref, w_sem, o_sem)
+    for pair in w_copies:
+        for copy in pair:
+            copy.start()
     mine, theirs = q_ref[:, 2 * width :], got_ref[:, 2 * width :]
-    mean_here, mean_there = mine[:, 0:1], theirs[:, 0:1]
-    gap = 0.5 * (mean_here - mean_there)
-    mean = 0.5 * (mean_here + mean_there)
-    variance = 0.5 * (mine[:, 1:2] + theirs[:, 1:2]) + gap * gap
+    gap = 0.5 * (mine[:, 1:2] - theirs[:, 1:2])
+    mean = 0.5 * (mine[:, 1:2] + theirs[:, 1:2])
+    variance = 0.5 * (mine[:, 2:3] + theirs[:, 2:3]) + gap * gap
     inv_std = lax.rsqrt(variance + epsilon)
     lane = lax.broadcasted_iota(jnp.int32, (rows, 128), 1)
     st_ref[...] = jnp.where(lane == 0, mean, inv_std)
-    side = jnp.where(core == 0, 1.0, -1.0)
+    even = jnp.where(core == 0, mine[:, 0:1], theirs[:, 0:1]) - mean
+    odd = jnp.where(core == 0, theirs[:, 0:1], mine[:, 0:1]) - mean
 
     def grad(summed, up, vec):
-        raw = inv_std * (summed + gap * (side * (vec[1:2, :] - vec[2:3, :])))
+        raw = inv_std * (summed + even * vec[1:2, :] + odd * vec[2:3, :])
         preact = raw + vec[0:1, :]
         gate = 1.0 / (1.0 + jnp.exp(-preact))
         pg = (up.astype(f32) * gate * (1.0 + preact * (1.0 - gate))).astype(bf16)
         wide = pg.astype(f32)
-        scale = jnp.broadcast_to(vec[1:2, :] + vec[2:3, :], (8, width))
-        first = lax.dot_general(scale, wide, NT, precision=lax.Precision.HIGHEST)
-        second = lax.dot_general(
-            jnp.ones((8, width), f32), wide * raw, NT, precision=lax.Precision.HIGHEST
+        scale = vec[1:2, :] + vec[2:3, :]
+        return (
+            pg,
+            jnp.sum(wide * scale, axis=1, keepdims=True),
+            jnp.sum(wide * raw, axis=1, keepdims=True),
         )
-        return pg, first, second
-
-    pg, first, second = grad(q_ref[:, :width] + got_ref[:, width : 2 * width], up_ref[...], vec_ref[...])
-    pgo, firsto, secondo = grad(
+
+    pg, sum_g, sum_gu = grad(q_ref[:, :width] + got_ref[:, width : 2 * width], up_ref[...], vec_ref[...])
+    pgo, sum_go, sum_guo = grad(
         q_ref[:, width : 2 * width] + got_ref[:, :width], upo_ref[...], veco_ref[...]
     )
-    first, second = first + firsto, second + secondo
-    row = lax.broadcasted_iota(jnp.int32, (8, rows), 0)
-    value = jnp.where(row < 2, first, second)
+    both = jnp.concatenate([pg, pgo], axis=1)
+    value = jnp.where(lane < 2, sum_g + sum_go, sum_gu + sum_guo)
     high = value.astype(bf16).astype(f32)
-    tail = jnp.where(row % 2 == 0, high, value - high)
-    tail = jnp.concatenate([tail, jnp.zeros_like(tail)], axis=0).astype(bf16)
+    tail = jnp.where(lane % 2 == 0, high, value - high).T[:PAD].astype(bf16)
     tail = jnp.concatenate([tail, jnp.zeros((PAD, feats - rows), bf16)], axis=1)
     for b in range(blocks):
-        w_copies[b].wait()
-        o_copies[b].wait()
-        p_ref[b, :rows] = (
-            lax.dot_general(pg, weight_ref[b], NT, preferred_element_type=f32)
-            + lax.dot_general(pgo, other_ref[b], NT, preferred_element_type=f32)
-        ).astype(bf16)
+        for copy in w_copies[b]:
+            copy.wait()
+        p_ref[b, :rows] = lax.dot_general(both, weight_ref[b], NT, preferred_element_type=f32).astype(bf16)
         p_ref[b, rows:] = tail
-        p_copies[b].start()
-    for copy in p_copies:
-        copy.wait()
 
 
 def backward(core, q, got, up, upo, vec, veco, weight, other):
-    blocks, feats, _ = other.shape
+    blocks, feats, width = other.shape
     rows = q.shape[0]
     return pl.pallas_call(
         backward_kernel,
         in_specs=[SCALAR] + in_vmem(6) + [ANYWHERE, ANYWHERE],
-        out_specs=[ANYWHERE] + in_vmem(1),
+        out_specs=in_vmem(2),
         out_shape=[
-            jax.ShapeDtypeStruct((blocks, rows + PAD, feats), bf16),
-            jax.ShapeDtypeStruct((rows, 128), f32),
+            pltpu.VMEM((blocks, rows + PAD, feats), bf16),
+            pltpu.VMEM((rows, 128), f32),
         ],
         scratch_shapes=[
-            pltpu.VMEM(other.shape, bf16),
-            pltpu.VMEM(other.shape, bf16),
-            pltpu.VMEM((blocks, rows + PAD, feats), bf16),
-            pltpu.SemaphoreType.DMA((blocks,)),
+            pltpu.VMEM((blocks, feats, 2 * width), bf16),
             pltpu.SemaphoreType.DMA((blocks,)),
             pltpu.SemaphoreType.DMA((blocks,)),
         ],
@@ -277,7 +286,7 @@
     classes = [[2 * k + c for k in range(chips)] for c in range(2)]
     core_arr = core.reshape(1).astype(jnp.int32)
 
-    sent = jnp.broadcast_to(inputs[None], (chips, rows, feats))
+    sent = spread(inputs, chips)
     half = lax.all_to_all(sent, "tensor", 0, 0, axis_index_groups=classes, tiled=True)
 
     pairs = proj_weight.reshape(chips, 2, feats, width)

time: 132 us -> 126 us (0.955)
  Pallas kernels: 16 us -> 11.6 us
    pallas_call x1, Pallas kernels: 9.18 us -> 4.58 us  [backward(): pl.pallas_call(backward_kernel, in_specs=[SCALAR] + in_vmem(6) + [ANYWHER...]
  transfers between devices with their start and end apart: 5 -> 5, of which waited for: 2 -> 2; matrix products, arithmetic and copies ran while one was open for 3% -> 2% of each run, Pallas kernels for 0% -> 1%
where the time goes in v4:
time: 126 us; the launch traced here: 124 us
  blocking collectives  66.1 us (52%)
  waiting for transfers between devices  20.4 us (16%)
  starting transfers between devices  20.2 us (16%)
  Pallas kernels  11.6 us (9%)
  local copies, waits for them, and re-layouts  2.87 us (2%)
  other arithmetic  2.79 us (2%)
    all_to_all x1, blocking collectives, per_device(): lax.all_to_all(send, 'dp', split_axis=0, concat_axis=0, tiled=True)  38.3 us
    all_to_all x1, blocking collectives, per_device(): lax.all_to_all(parts, 'tensor', 0, 0, axis_index_groups=classes, tiled=True)  27.8 us
    all_to_all x1, waiting for transfers between devices, per_device(): lax.all_to_all(sent, 'tensor', 0, 0, axis_index_groups=classes, tiled=True)  18.7 us
    ppermute x1, starting transfers between devices, per_device(): other = lax.ppermute(cut, 'tensor', swap)  8.73 us
    pallas_call x1, Pallas kernels, backward(): pl.pallas_call(backward_kernel, in_specs=[SCALAR] + in_vmem(6) + [ANYWHER...  4.58 us
    all_to_all x1, starting transfers between devices, per_device(): lax.all_to_all(sent, 'tensor', 0, 0, axis_index_groups=classes, tiled=True)  4.3 us
    pallas_call x1, Pallas kernels, forward(): pl.pallas_call(forward_kernel, in_specs=[SCALAR, ANYWHERE] + in_vmem(1) +...  3.86 us
    squeeze x1, local copies, waits for them, and re-layouts, per_device(): cut = lax.dynamic_index_in_dim(pairs, 1 - core, 1, False)  2.82 us
  transfers between devices with their start and end apart: 5, of which 2 were waited for; matrix products, arithmetic and copies ran while one was open for 2% of the time, Pallas kernels for 1%

profile of v4, /device:TPU:1, one launch (start us, length us, event | category | flops | bytes accessed | tf_op | source)
XLA Modules:
  0.0 124.2 jit_solution(1925891428150237406)
XLA Ops:
  0.0 0.0 copy-start
  0.0 0.0 copy-start.3
  0.0 0.0 copy-start.4
  0.0 0.0 copy-start.1
  0.0 2.8 %dynamic-slice_bitcast_fusion = bf16[8,384,256]{2,1,0:T(8,128)(2,1)} fusion(bf16[8,2,384,256]{3,2,1,0:T(8,128)(2,1)} %bitcast.10, s32[]{:T(128)S(6)} %select_n.31), kind=kLoop, calls=%fused_computation.2 | loop fusion | bytes 3145732 | tf_op jit(solution)/shard_map/jit(dynamic_index_in_dim)/squeeze | solution.py:293
  2.8 8.7 %collective-permute-start = (bf16[8,384,256]{2,1,0:T(8,128)(2,1)}, bf16[8,384,256]{2,1,0:T(8,128)(2,1)}, u32[]{:S(2)}, u32[]{:S(2)}) collective-permute-start(bf16[8,384,256]{2,1,0:T(8,128)(2,1)} %dynamic-slice_bitcast_fusion), channel_id=1, source_target_pairs={{0,1},{1,0},{2,3},{3,2},{4,5},{5,4},{6,7},{7,6},{8,9},{9,8},{10,11... | collective-permute-start | bytes 4718600 | tf_op jit(solution)/shard_map/ppermute | solution.py:294
  11.6 0.0 copy-done.3
  11.6 0.0 copy-done
  11.6 1.0 multiply_reduce_fusion
  12.6 0.0 copy-start.2
  12.6 0.0 copy-start.5
  12.6 0.0 copy-done.4
  12.7 2.1 %collective-permute-start.2 = (f32[3,256]{1,0:T(4,128)S(1)}, f32[3,256]{1,0:T(4,128)S(1)}, u32[]{:S(2)}, u32[]{:S(2)}) collective-permute-start(f32[3,256]{1,0:T(4,128)S(1)} %pad_maximum_fusion.vec_ref), channel_id=1, source_target_pairs={{0,1},{1,0},{2,3},{3,2},{4,5},{5,4},{6,7},{7,6},{8,9},{9,8},{10,11... | collective-permute-start | bytes 9224 | tf_op jit(solution)/shard_map/ppermute | solution.py:299
  14.7 0.0 copy-done.1
  14.7 1.2 spread.1
  16.0 4.3 %all-to-all-start = ((bf16[8,256,384]{2,1,0:T(8,128)(2,1)}), bf16[8,256,384]{2,1,0:T(8,128)(2,1)}, u32[]{:S(2)}, u32[]{:S(2)}) async-start(bf16[8,256,384]{2,1,0:T(8,128)(2,1)} %spread.1), calls=%async_computation | async-start | bytes 3145728 | tf_op jit(solution)/shard_map/all_to_all | solution.py:290
  20.3 0.0 copy-done.2
  20.3 2.4 %collective-permute-start.1 = (bf16[256,256]{1,0:T(8,128)(2,1)S(1)}, bf16[256,256]{1,0:T(8,128)(2,1)}, u32[]{:S(2)}, u32[]{:S(2)}) collective-permute-start(bf16[256,256]{1,0:T(8,128)(2,1)S(1)} %copy-done.2), channel_id=1, source_target_pairs={{0,1},{1,0},{2,3},{3,2},{4,5},{5,4},{6,7},{7,6},{8,9},{9,8},{10,11... | collective-permute-start | bytes 393224 | tf_op jit(solution)/shard_map/ppermute | solution.py:295
  22.7 0.0 copy-done.5
  22.8 0.2 convert_reduce_fusion
  22.9 0.1 iota_add_fusion
  23.0 1.5 %select_reduce_fusion = s32[32,128]{1,0:T(8,128)S(1)} fusion(s32[256]{0:T(256)S(1)} %get-tuple-element.24, s32[256]{0:T(256)S(1)} %multiply_add_fusion, s32[32,128]{1,0:T(8,128)S(1)} %iota_add_fusion, pred[128]{0:T(512)(128)(4,1)S(1)} %iota_compare_fusion.1), kind=kLoop, calls=%fused_computation.1 | loop fusion | flops 4190208 | bytes 34944 | tf_op jit(solution)/shard_map/reduce_sum | solution.py:314
  24.6 0.0 collective-permute-done.2.veco_ref
  24.6 0.0 collective-permute-done.1.upo_ref
  24.6 18.7 %all-to-all-done.x_any = bf16[8,256,384]{2,1,0:T(8,128)(2,1)} async-done(((bf16[8,256,384]{2,1,0:T(8,128)(2,1)}), bf16[8,256,384]{2,1,0:T(8,128)(2,1)}, u32[]{:S(2)}, u32[]{:S(2)}) %all-to-all-start) | async-done | bytes 1572896 | tf_op jit(solution)/shard_map/all_to_all | solution.py:290
  43.3 0.0 collective-permute-done.other_any
  43.3 3.9 %forward.1.q_ref = f32[256,640]{1,0:T(8,128)S(1)} custom-call(s32[1]{0:T(128)} %bitcast.core_ref, bf16[8,256,384]{2,1,0:T(8,128)(2,1)} %all-to-all-done.x_any, f32[8,2,1,384]{3,2,1,0:T(1,128)S(1)} %bitcast.15, bf16[8,2,384,256]{3,2,1,0:T(8,128)(2,1)S(1)} %bitcast.12, bf16[8,384,256]{2,1,0:T(8,128)(2,1)} %collective-permute-done.other_any), custom_call_target="tpu_custom_call" | custom-call | tf_op jit(solution)/shard_map/forward/pallas_call | solution.py:106
  47.2 2.7 %collective-permute-start.3 = (f32[256,640]{1,0:T(8,128)S(1)}, f32[256,640]{1,0:T(8,128)S(1)}, u32[]{:S(2)}, u32[]{:S(2)}) collective-permute-start(f32[256,640]{1,0:T(8,128)S(1)} %forward.1.q_ref), channel_id=1, source_target_pairs={{0,1},{1,0},{2,3},{3,2},{4,5},{5,4},{6,7},{7,6},{8,9},{9,8},{10,11... | collective-permute-start | bytes 1966088 | tf_op jit(solution)/shard_map/ppermute | solution.py:322
  49.9 1.7 %collective-permute-done.3.got_ref = f32[256,640]{1,0:T(8,128)S(1)} collective-permute-done((f32[256,640]{1,0:T(8,128)S(1)}, f32[256,640]{1,0:T(8,128)S(1)}, u32[]{:S(2)}, u32[]{:S(2)}) %collective-permute-start.3) | collective-permute-done | bytes 655392 | tf_op jit(solution)/shard_map/ppermute | solution.py:322
  51.6 4.6 %backward.1 = (bf16[8,272,384]{2,1,0:T(8,128)(2,1)S(1)}, f32[256,128]{1,0:T(8,128)S(1)}) custom-call(s32[1]{0:T(128)} %bitcast.core_ref, f32[256,640]{1,0:T(8,128)S(1)} %forward.1.q_ref, f32[256,640]{1,0:T(8,128)S(1)} %collective-permute-done.3.got_ref, bf16[256,256]{1,0:T(8,128)(2,1)S(1)} %copy-done.2, bf16[256,256]{1,0:T(8,128)(2,1)} %collective-permute-done.1.upo_ref, ...), custom_call_target="tpu_custom_call" | custom-call | tf_op jit(solution)/shard_map/backward/pallas_call | solution.py:189
  56.2 27.8 %all_to_all.15.back_ref = bf16[8,272,384]{2,1,0:T(8,128)(2,1)S(1)} all-to-all(bf16[8,272,384]{2,1,0:T(8,128)(2,1)S(1)} %get-tuple-element.18), channel_id=1, replica_groups={{0,2,4,6,8,10,12,14},{1,3,5,7,9,11,13,15},{16,18,20,22,24,26,28,30},{17..., dimensions={0} | all-to-all | bytes 3342336 | tf_op jit(solution)/shard_map/all_to_all | solution.py:324
  84.0 0.8 finish.1
  84.8 38.3 %all_to_all.16.got_ref = bf16[32,56,128]{2,1,0:T(8,128)(2,1)S(1)} all-to-all(bf16[32,56,128]{2,1,0:T(8,128)(2,1)S(1)} %finish.1), channel_id=1, replica_groups=mesh['dp'=32,'tensor'=16] {'dp'}, dimensions={0} | all-to-all | bytes 917504 | tf_op jit(solution)/shard_map/all_to_all | solution.py:326
  123.1 1.2 land.1
  (8 shorter events, 0.1 us)
Async XLA Ops:
  0.0 11.6 %copy-start = (bf16[6144,256]{1,0:T(8,128)(2,1)S(1)}, bf16[6144,256]{1,0:T(8,128)(2,1)}, u32[]{:S(2)}) copy-start(bf16[6144,256]{1,0:T(8,128)(2,1)} %param.8) | copy-start | bytes 9437188
  0.0 11.6 %copy-start.3 = (f32[6144]{0:T(1024)S(1)}, f32[6144]{0:T(1024)}, u32[]{:S(2)}) copy-start(f32[6144]{0:T(1024)} %param.10) | copy-start | bytes 73732
  0.0 12.6 %copy-start.4 = (f32[256]{0:T(256)S(1)}, f32[256]{0:T(256)}, u32[]{:S(2)}) copy-start(f32[256]{0:T(256)} %param.9) | copy-start | bytes 3076
  0.0 14.7 %copy-start.1 = (bf16[256,384]{1,0:T(8,128)(2,1)S(1)}, bf16[256,384]{1,0:T(8,128)(2,1)}, u32[]{:S(2)}) copy-start(bf16[256,384]{1,0:T(8,128)(2,1)} %x_ref.3) | copy-start | bytes 589828
  2.8 40.5 %collective-permute-start = (bf16[8,384,256]{2,1,0:T(8,128)(2,1)}, bf16[8,384,256]{2,1,0:T(8,128)(2,1)}, u32[]{:S(2)}, u32[]{:S(2)}) collective-permute-start(bf16[8,384,256]{2,1,0:T(8,128)(2,1)} %dynamic-slice_bitcast_fusion), channel_id=1, source_target_pairs={{0,1},{1,0},{2,3},{3,2},{4,5},{5,4},{6,7},{7,6},{8,9},{9,8},{10,11... | collective-permute-start | bytes 4718600 | tf_op jit(solution)/shard_map/ppermute | solution.py:294
  12.6 7.7 %copy-start.2 = (bf16[256,256]{1,0:T(8,128)(2,1)S(1)}, bf16[256,256]{1,0:T(8,128)(2,1)}, u32[]{:S(2)}) copy-start(bf16[256,256]{1,0:T(8,128)(2,1)} %up_ref.1) | copy-start | bytes 393220
  12.6 10.1 %copy-start.5 = (s32[256]{0:T(256)S(1)}, s32[256]{0:T(256)}, u32[]{:S(2)}) copy-start(s32[256]{0:T(256)} %param.11) | copy-start | bytes 3076
  12.7 11.9 %collective-permute-start.2 = (f32[3,256]{1,0:T(4,128)S(1)}, f32[3,256]{1,0:T(4,128)S(1)}, u32[]{:S(2)}, u32[]{:S(2)}) collective-permute-start(f32[3,256]{1,0:T(4,128)S(1)} %pad_maximum_fusion.vec_ref), channel_id=1, source_target_pairs={{0,1},{1,0},{2,3},{3,2},{4,5},{5,4},{6,7},{7,6},{8,9},{9,8},{10,11... | collective-permute-start | bytes 9224 | tf_op jit(solution)/shard_map/ppermute | solution.py:299
  16.0 27.3 %all-to-all-start = ((bf16[8,256,384]{2,1,0:T(8,128)(2,1)}), bf16[8,256,384]{2,1,0:T(8,128)(2,1)}, u32[]{:S(2)}, u32[]{:S(2)}) async-start(bf16[8,256,384]{2,1,0:T(8,128)(2,1)} %spread.1), calls=%async_computation | async-start | bytes 3145728 | tf_op jit(solution)/shard_map/all_to_all | solution.py:290
  20.3 4.3 %collective-permute-start.1 = (bf16[256,256]{1,0:T(8,128)(2,1)S(1)}, bf16[256,256]{1,0:T(8,128)(2,1)}, u32[]{:S(2)}, u32[]{:S(2)}) collective-permute-start(bf16[256,256]{1,0:T(8,128)(2,1)S(1)} %copy-done.2), channel_id=1, source_target_pairs={{0,1},{1,0},{2,3},{3,2},{4,5},{5,4},{6,7},{7,6},{8,9},{9,8},{10,11... | collective-permute-start | bytes 393224 | tf_op jit(solution)/shard_map/ppermute | solution.py:295
  47.2 4.4 %collective-permute-start.3 = (f32[256,640]{1,0:T(8,128)S(1)}, f32[256,640]{1,0:T(8,128)S(1)}, u32[]{:S(2)}, u32[]{:S(2)}) collective-permute-start(f32[256,640]{1,0:T(8,128)S(1)} %forward.1.q_ref), channel_id=1, source_target_pairs={{0,1},{1,0},{2,3},{3,2},{4,5},{5,4},{6,7},{7,6},{8,9},{9,8},{10,11... | collective-permute-start | bytes 1966088 | tf_op jit(solution)/shard_map/ppermute | solution.py:322

commit v5 on v4

--- a/solution.py
+++ b/solution.py
@@ -8,7 +8,7 @@
 
 epsilon = 1e-05
 f32, bf16 = jnp.float32, jnp.bfloat16
-PAD = 16
+PAD = 8
 CAPACITY = 16
 NT = (((1,), (1,)), ((), ()))
 
@@ -28,8 +28,8 @@
 SCALAR = pl.BlockSpec(memory_space=pltpu.SMEM)
 
 
-def spread_kernel(x_ref, o_any, sem):
-    copies = [pltpu.make_async_copy(x_ref, o_any.at[b], sem.at[b]) for b in range(o_any.shape[0])]
+def spread_kernel(x_any, o_any, sem):
+    copies = [pltpu.make_async_copy(x_any, o_any.at[b], sem.at[b]) for b in range(o_any.shape[0])]
     for copy in copies:
         copy.start()
     for copy in copies:
@@ -39,13 +39,13 @@
 def spread(x, blocks):
     return pl.pallas_call(
         spread_kernel,
-        in_specs=in_vmem(1),
+        in_specs=[ANYWHERE],
         out_specs=ANYWHERE,
         out_shape=pltpu.HBM((blocks,) + x.shape, x.dtype),
         scratch_shapes=[pltpu.SemaphoreType.DMA((blocks,))],
         compiler_params=PARAMS,
         name="spread",
-    )(x)
+    )(pltpu.with_memory_space_constraint(x, pltpu.HBM))
 
 
 def weight_copies(core, weight_any, other_any, weight_ref, w_sem, o_sem):
@@ -61,7 +61,7 @@
 
 
 def forward_kernel(
-    core_ref, x_any, gain_ref, weight_any, other_any, q_ref, x_ref, weight_ref, x_sem, w_sem, o_sem
+    core_ref, x_any, gain_ref, weight_any, other_any, q_ref, x_ref, weight_ref, rows_ref, x_sem, w_sem, o_sem
 ):
     blocks, rows, feats = x_ref.shape
     width = weight_ref.shape[2]
@@ -84,14 +84,12 @@
             part = moved[:, j : j + 128]
             total += part
             square += part * part
-        scaled = (moved * gain_ref[b, core]).astype(bf16)
+        rows_ref[:, b * feats : (b + 1) * feats] = (moved * gain_ref[b, core]).astype(bf16)
         for copy in w_copies[b]:
             copy.wait()
-        term = jnp.dot(scaled, weight_ref[b], preferred_element_type=f32)
-        if b == 0:
-            q_ref[:, :width] = term
-        else:
-            q_ref[:, :width] += term
+    q_ref[:, :width] = jnp.dot(
+        rows_ref[...], weight_ref[...].reshape(blocks * feats, width), preferred_element_type=f32
+    )
     shift = jnp.sum(total, axis=1, keepdims=True) / (blocks * feats)
     spread = jnp.sum(square, axis=1, keepdims=True) / (blocks * feats) - shift * shift
     lane = lax.broadcasted_iota(jnp.int32, (rows, 128), 1)
@@ -111,6 +109,7 @@
         scratch_shapes=[
             pltpu.VMEM(x.shape, bf16),
             pltpu.VMEM((blocks, feats, 2 * width), bf16),
+            pltpu.VMEM((rows, blocks * feats), bf16),
             pltpu.SemaphoreType.DMA((blocks,)),
             pltpu.SemaphoreType.DMA((blocks,)),
             pltpu.SemaphoreType.DMA((blocks,)),

time: 126 us -> 172 us (1.37)
  Pallas kernels: 11.6 us -> 57.7 us
    pallas_call x1, Pallas kernels: 1.23 us -> 48.8 us  [spread(): pl.pallas_call(spread_kernel, in_specs=[ANYWHERE], out_specs=ANYWHERE, ou...]
  transfers between devices with their start and end apart: 5 -> 5, of which waited for: 2 -> 2; matrix products, arithmetic and copies ran while one was open for 2% -> 2% of each run, Pallas kernels for 1% -> 29%
where the time goes in v5:
time: 172 us; the launch traced here: 170 us
  blocking collectives  65.7 us (38%)
  Pallas kernels  57.7 us (34%)
  waiting for transfers between devices  20.4 us (12%)
  starting transfers between devices  20.2 us (12%)
  local copies, waits for them, and re-layouts  2.87 us (2%)
  other arithmetic  2.79 us (2%)
    pallas_call x1, Pallas kernels, spread(): pl.pallas_call(spread_kernel, in_specs=[ANYWHERE], out_specs=ANYWHERE, ou...  48.8 us
    all_to_all x1, blocking collectives, per_device(): lax.all_to_all(send, 'dp', split_axis=0, concat_axis=0, tiled=True)  38.2 us
    all_to_all x1, blocking collectives, per_device(): lax.all_to_all(parts, 'tensor', 0, 0, axis_index_groups=classes, tiled=True)  27.5 us
    all_to_all x1, waiting for transfers between devices, per_device(): lax.all_to_all(sent, 'tensor', 0, 0, axis_index_groups=classes, tiled=True)  18.7 us
    ppermute x1, starting transfers between devices, per_device(): other = lax.ppermute(cut, 'tensor', swap)  8.74 us
    all_to_all x1, starting transfers between devices, per_device(): lax.all_to_all(sent, 'tensor', 0, 0, axis_index_groups=classes, tiled=True)  4.3 us
    pallas_call x1, Pallas kernels, backward(): pl.pallas_call(backward_kernel, in_specs=[SCALAR] + in_vmem(6) + [ANYWHER...  3.71 us
  transfers between devices with their start and end apart: 5, of which 2 were waited for; matrix products, arithmetic and copies ran while one was open for 2% of the time, Pallas kernels for 29%

profile of v5, /device:TPU:1, one launch (start us, length us, event | category | flops | bytes accessed | tf_op | source)
XLA Modules:
  0.0 169.8 jit_solution(14633879691102167584)
XLA Ops:
  0.0 0.0 copy-start
  0.0 0.0 copy-start.3
  0.0 0.0 copy-start.4
  0.0 2.8 %dynamic-slice_bitcast_fusion = bf16[8,384,256]{2,1,0:T(8,128)(2,1)} fusion(bf16[8,2,384,256]{3,2,1,0:T(8,128)(2,1)} %bitcast.10, s32[]{:T(128)S(6)} %select_n.31), kind=kLoop, calls=%fused_computation.2 | loop fusion | bytes 3145732 | tf_op jit(solution)/shard_map/jit(dynamic_index_in_dim)/squeeze | solution.py:292
  2.8 8.7 %collective-permute-start = (bf16[8,384,256]{2,1,0:T(8,128)(2,1)}, bf16[8,384,256]{2,1,0:T(8,128)(2,1)}, u32[]{:S(2)}, u32[]{:S(2)}) collective-permute-start(bf16[8,384,256]{2,1,0:T(8,128)(2,1)} %dynamic-slice_bitcast_fusion), channel_id=1, source_target_pairs={{0,1},{1,0},{2,3},{3,2},{4,5},{5,4},{6,7},{7,6},{8,9},{9,8},{10,11... | collective-permute-start | bytes 4718600 | tf_op jit(solution)/shard_map/ppermute | solution.py:293
  11.6 0.0 copy-done.3
  11.6 0.0 copy-done
  11.6 1.0 multiply_reduce_fusion
  12.6 0.0 copy-start.2
  12.6 0.0 copy-start.5
  12.6 0.0 copy-done.4
  12.7 2.1 %collective-permute-start.2 = (f32[3,256]{1,0:T(4,128)S(1)}, f32[3,256]{1,0:T(4,128)S(1)}, u32[]{:S(2)}, u32[]{:S(2)}) collective-permute-start(f32[3,256]{1,0:T(4,128)S(1)} %pad_maximum_fusion.vec_ref), channel_id=1, source_target_pairs={{0,1},{1,0},{2,3},{3,2},{4,5},{5,4},{6,7},{7,6},{8,9},{9,8},{10,11... | collective-permute-start | bytes 9224 | tf_op jit(solution)/shard_map/ppermute | solution.py:298
  14.7 48.8 %spread.1 = bf16[8,256,384]{2,1,0:T(8,128)(2,1)} custom-call(bf16[256,384]{1,0:T(8,128)(2,1)} %x_ref.1), custom_call_target="tpu_custom_call" | custom-call | tf_op jit(solution)/shard_map/spread/pallas_call | solution.py:40
  63.5 4.3 %all-to-all-start = ((bf16[8,256,384]{2,1,0:T(8,128)(2,1)}), bf16[8,256,384]{2,1,0:T(8,128)(2,1)}, u32[]{:S(2)}, u32[]{:S(2)}) async-start(bf16[8,256,384]{2,1,0:T(8,128)(2,1)} %spread.1), calls=%async_computation | async-start | bytes 3145728 | tf_op jit(solution)/shard_map/all_to_all | solution.py:289
  67.9 0.0 copy-done.2
  67.9 2.4 %collective-permute-start.1 = (bf16[256,256]{1,0:T(8,128)(2,1)S(1)}, bf16[256,256]{1,0:T(8,128)(2,1)S(1)}, u32[]{:S(2)}, u32[]{:S(2)}) collective-permute-start(bf16[256,256]{1,0:T(8,128)(2,1)S(1)} %copy-done.2), channel_id=1, source_target_pairs={{0,1},{1,0},{2,3},{3,2},{4,5},{5,4},{6,7},{7,6},{8,9},{9,8},{10,11... | collective-permute-start | bytes 393224 | tf_op jit(solution)/shard_map/ppermute | solution.py:294
  70.3 0.0 copy-done.5
  70.3 0.2 convert_reduce_fusion
  70.5 0.1 iota_add_fusion
  70.6 1.5 select_reduce_fusion
  72.1 0.0 collective-permute-done.2.veco_ref
  72.2 0.0 collective-permute-done.1.upo_ref
  72.2 18.7 %all-to-all-done.x_any = bf16[8,256,384]{2,1,0:T(8,128)(2,1)} async-done(((bf16[8,256,384]{2,1,0:T(8,128)(2,1)}), bf16[8,256,384]{2,1,0:T(8,128)(2,1)}, u32[]{:S(2)}, u32[]{:S(2)}) %all-to-all-start) | async-done | bytes 1572896 | tf_op jit(solution)/shard_map/all_to_all | solution.py:289
  90.9 0.0 collective-permute-done.other_any
  90.9 3.2 %forward.1.q_ref = f32[256,640]{1,0:T(8,128)S(1)} custom-call(s32[1]{0:T(128)} %bitcast.core_ref, bf16[8,256,384]{2,1,0:T(8,128)(2,1)} %all-to-all-done.x_any, f32[8,2,1,384]{3,2,1,0:T(1,128)S(1)} %bitcast.15, bf16[8,2,384,256]{3,2,1,0:T(8,128)(2,1)S(1)} %bitcast.12, bf16[8,384,256]{2,1,0:T(8,128)(2,1)} %collective-permute-done.other_any), custom_call_target="tpu_custom_call" | custom-call | tf_op jit(solution)/shard_map/forward/pallas_call | solution.py:104
  94.1 2.7 %collective-permute-start.3 = (f32[256,640]{1,0:T(8,128)S(1)}, f32[256,640]{1,0:T(8,128)S(1)}, u32[]{:S(2)}, u32[]{:S(2)}) collective-permute-start(f32[256,640]{1,0:T(8,128)S(1)} %forward.1.q_ref), channel_id=1, source_target_pairs={{0,1},{1,0},{2,3},{3,2},{4,5},{5,4},{6,7},{7,6},{8,9},{9,8},{10,11... | collective-permute-start | bytes 1966088 | tf_op jit(solution)/shard_map/ppermute | solution.py:321
  96.8 1.7 %collective-permute-done.3.got_ref = f32[256,640]{1,0:T(8,128)S(1)} collective-permute-done((f32[256,640]{1,0:T(8,128)S(1)}, f32[256,640]{1,0:T(8,128)S(1)}, u32[]{:S(2)}, u32[]{:S(2)}) %collective-permute-start.3) | collective-permute-done | bytes 655392 | tf_op jit(solution)/shard_map/ppermute | solution.py:321
  98.5 3.7 %backward.1 = (bf16[8,264,384]{2,1,0:T(8,128)(2,1)S(1)}, f32[256,128]{1,0:T(8,128)S(1)}) custom-call(s32[1]{0:T(128)} %bitcast.core_ref, f32[256,640]{1,0:T(8,128)S(1)} %forward.1.q_ref, f32[256,640]{1,0:T(8,128)S(1)} %collective-permute-done.3.got_ref, bf16[256,256]{1,0:T(8,128)(2,1)S(1)} %copy-done.2, bf16[256,256]{1,0:T(8,128)(2,1)S(1)} %collective-permute-done.1.upo_ref, ...), custom_call_target="tpu_custom_call" | custom-call | tf_op jit(solution)/shard_map/backward/pallas_call | solution.py:188
  102.2 0.0 copy-start.1
  102.2 27.5 %all_to_all.15.back_ref = bf16[8,264,384]{2,1,0:T(8,128)(2,1)S(1)} all-to-all(bf16[8,264,384]{2,1,0:T(8,128)(2,1)S(1)} %get-tuple-element.18), channel_id=1, replica_groups={{0,2,4,6,8,10,12,14},{1,3,5,7,9,11,13,15},{16,18,20,22,24,26,28,30},{17..., dimensions={0} | all-to-all | bytes 3244032 | tf_op jit(solution)/shard_map/all_to_all | solution.py:323
  129.7 0.0 copy-done.1
  129.7 0.8 finish.1
  130.5 38.2 %all_to_all.16.got_ref = bf16[32,56,128]{2,1,0:T(8,128)(2,1)S(1)} all-to-all(bf16[32,56,128]{2,1,0:T(8,128)(2,1)S(1)} %finish.1), channel_id=1, replica_groups=mesh['dp'=32,'tensor'=16] {'dp'}, dimensions={0} | all-to-all | bytes 917504 | tf_op jit(solution)/shard_map/all_to_all | solution.py:325
  168.7 1.2 land.1
  (8 shorter events, 0.1 us)
Async XLA Ops:
  0.0 11.6 %copy-start = (bf16[6144,256]{1,0:T(8,128)(2,1)S(1)}, bf16[6144,256]{1,0:T(8,128)(2,1)}, u32[]{:S(2)}) copy-start(bf16[6144,256]{1,0:T(8,128)(2,1)} %param.8) | copy-start | bytes 9437188
  0.0 11.6 %copy-start.3 = (f32[6144]{0:T(1024)S(1)}, f32[6144]{0:T(1024)}, u32[]{:S(2)}) copy-start(f32[6144]{0:T(1024)} %param.10) | copy-start | bytes 73732
  0.0 12.6 %copy-start.4 = (f32[256]{0:T(256)S(1)}, f32[256]{0:T(256)}, u32[]{:S(2)}) copy-start(f32[256]{0:T(256)} %param.9) | copy-start | bytes 3076
  2.8 88.0 %collective-permute-start = (bf16[8,384,256]{2,1,0:T(8,128)(2,1)}, bf16[8,384,256]{2,1,0:T(8,128)(2,1)}, u32[]{:S(2)}, u32[]{:S(2)}) collective-permute-start(bf16[8,384,256]{2,1,0:T(8,128)(2,1)} %dynamic-slice_bitcast_fusion), channel_id=1, source_target_pairs={{0,1},{1,0},{2,3},{3,2},{4,5},{5,4},{6,7},{7,6},{8,9},{9,8},{10,11... | collective-permute-start | bytes 4718600 | tf_op jit(solution)/shard_map/ppermute | solution.py:293
  12.6 55.2 %copy-start.2 = (bf16[256,256]{1,0:T(8,128)(2,1)S(1)}, bf16[256,256]{1,0:T(8,128)(2,1)}, u32[]{:S(2)}) copy-start(bf16[256,256]{1,0:T(8,128)(2,1)} %up_ref.1) | copy-start | bytes 393220
  12.6 57.7 %copy-start.5 = (s32[256]{0:T(256)S(1)}, s32[256]{0:T(256)}, u32[]{:S(2)}) copy-start(s32[256]{0:T(256)} %param.11) | copy-start | bytes 3076
  12.7 59.5 %collective-permute-start.2 = (f32[3,256]{1,0:T(4,128)S(1)}, f32[3,256]{1,0:T(4,128)S(1)}, u32[]{:S(2)}, u32[]{:S(2)}) collective-permute-start(f32[3,256]{1,0:T(4,128)S(1)} %pad_maximum_fusion.vec_ref), channel_id=1, source_target_pairs={{0,1},{1,0},{2,3},{3,2},{4,5},{5,4},{6,7},{7,6},{8,9},{9,8},{10,11... | collective-permute-start | bytes 9224 | tf_op jit(solution)/shard_map/ppermute | solution.py:298
  63.5 27.3 %all-to-all-start = ((bf16[8,256,384]{2,1,0:T(8,128)(2,1)}), bf16[8,256,384]{2,1,0:T(8,128)(2,1)}, u32[]{:S(2)}, u32[]{:S(2)}) async-start(bf16[8,256,384]{2,1,0:T(8,128)(2,1)} %spread.1), calls=%async_computation | async-start | bytes 3145728 | tf_op jit(solution)/shard_map/all_to_all | solution.py:289
  67.9 4.3 %collective-permute-start.1 = (bf16[256,256]{1,0:T(8,128)(2,1)S(1)}, bf16[256,256]{1,0:T(8,128)(2,1)S(1)}, u32[]{:S(2)}, u32[]{:S(2)}) collective-permute-start(bf16[256,256]{1,0:T(8,128)(2,1)S(1)} %copy-done.2), channel_id=1, source_target_pairs={{0,1},{1,0},{2,3},{3,2},{4,5},{5,4},{6,7},{7,6},{8,9},{9,8},{10,11... | collective-permute-start | bytes 393224 | tf_op jit(solution)/shard_map/ppermute | solution.py:294
  94.1 4.4 %collective-permute-start.3 = (f32[256,640]{1,0:T(8,128)S(1)}, f32[256,640]{1,0:T(8,128)S(1)}, u32[]{:S(2)}, u32[]{:S(2)}) collective-permute-start(f32[256,640]{1,0:T(8,128)S(1)} %forward.1.q_ref), channel_id=1, source_target_pairs={{0,1},{1,0},{2,3},{3,2},{4,5},{5,4},{6,7},{7,6},{8,9},{9,8},{10,11... | collective-permute-start | bytes 1966088 | tf_op jit(solution)/shard_map/ppermute | solution.py:321
  102.2 27.5 %copy-start.1 = (bf16[256,384]{1,0:T(8,128)(2,1)S(1)}, bf16[256,384]{1,0:T(8,128)(2,1)}, u32[]{:S(2)}) copy-start(bf16[256,384]{1,0:T(8,128)(2,1)} %x_ref.1) | copy-start | bytes 589828

commit v6 on v5

--- a/solution.py
+++ b/solution.py
@@ -28,12 +28,29 @@
 SCALAR = pl.BlockSpec(memory_space=pltpu.SMEM)
 
 
-def spread_kernel(x_any, o_any, sem):
-    copies = [pltpu.make_async_copy(x_any, o_any.at[b], sem.at[b]) for b in range(o_any.shape[0])]
-    for copy in copies:
+def spread_kernel(x_any, o_any, x_ref, in_sem, out_sem):
+    blocks, rows, _ = o_any.shape
+    parts = in_sem.shape[0]
+    step = rows // parts
+    loads, stores = [], []
+    for p in range(parts):
+        span = pl.ds(p * step, step)
+        loads.append(pltpu.make_async_copy(x_any.at[span], x_ref.at[span], in_sem.at[p]))
+        stores.append(
+            [
+                pltpu.make_async_copy(x_ref.at[span], o_any.at[b, span], out_sem.at[p, b])
+                for b in range(blocks)
+            ]
+        )
+    for copy in loads:
         copy.start()
-    for copy in copies:
-        copy.wait()
+    for p in range(parts):
+        loads[p].wait()
+        for copy in stores[p]:
+            copy.start()
+    for part in stores:
+        for copy in part:
+            copy.wait()
 
 
 def spread(x, blocks):
@@ -42,7 +59,11 @@
         in_specs=[ANYWHERE],
         out_specs=ANYWHERE,
         out_shape=pltpu.HBM((blocks,) + x.shape, x.dtype),
-        scratch_shapes=[pltpu.SemaphoreType.DMA((blocks,))],
+        scratch_shapes=[
+            pltpu.VMEM(x.shape, x.dtype),
+            pltpu.SemaphoreType.DMA((2,)),
+            pltpu.SemaphoreType.DMA((2, blocks)),
+        ],
         compiler_params=PARAMS,
         name="spread",
     )(pltpu.with_memory_space_constraint(x, pltpu.HBM))
@@ -65,6 +86,7 @@
 ):
     blocks, rows, feats = x_ref.shape
     width = weight_ref.shape[2]
+    half = blocks // 2
     core = core_ref[0]
     x_copies = [pltpu.make_async_copy(x_any.at[b], x_ref.at[b], x_sem.at[b]) for b in range(blocks)]
     w_copies = weight_copies(core, weight_any, other_any, weight_ref, w_sem, o_sem)
@@ -87,9 +109,16 @@
         rows_ref[:, b * feats : (b + 1) * feats] = (moved * gain_ref[b, core]).astype(bf16)
         for copy in w_copies[b]:
             copy.wait()
-    q_ref[:, :width] = jnp.dot(
-        rows_ref[...], weight_ref[...].reshape(blocks * feats, width), preferred_element_type=f32
-    )
+        if b % half == half - 1:
+            term = jnp.dot(
+                rows_ref[:, (b + 1 - half) * feats : (b + 1) * feats],
+                weight_ref[b + 1 - half : b + 1].reshape(half * feats, width),
+                preferred_element_type=f32,
+            )
+            if b < half:
+                q_ref[:, :width] = term
+            else:
+                q_ref[:, :width] += term
     shift = jnp.sum(total, axis=1, keepdims=True) / (blocks * feats)
     spread = jnp.sum(square, axis=1, keepdims=True) / (blocks * feats) - shift * shift
     lane = lax.broadcasted_iota(jnp.int32, (rows, 128), 1)
@@ -225,7 +254,9 @@
     placed = placed.reshape(owners, CAPACITY, feats)
     for k in range(feats // 128):
         send_ref[:, k * CAPACITY : (k + 1) * CAPACITY, :] = placed[:, :, k * 128 : (k + 1) * 128]
-    send_ref[:, feats // 128 * CAPACITY :, :] = jnp.broadcast_to(slot_ref[...][:, None, :], (owners, 8, 128))
+    send_ref[:, feats // 128 * CAPACITY :, :] = jnp.broadcast_to(
+        slot_ref[...][:, None, :], (owners, 2, 128)
+    )
 
 
 def finish(back, x, st, gain, target, slot):
@@ -234,7 +265,7 @@
         finish_kernel,
         in_specs=in_vmem(6),
         out_specs=in_vmem(1)[0],
-        out_shape=pltpu.VMEM((owners, x.shape[1] // 128 * CAPACITY + 8, 128), bf16),
+        out_shape=pltpu.VMEM((owners, x.shape[1] // 128 * CAPACITY + 2, 128), bf16),
         compiler_params=PARAMS,
         name="finish",
     )(*held(back, x, st, gain, target, slot))

time: 172 us -> 125 us (0.73)
  Pallas kernels: 57.7 us -> 11.1 us
    pallas_call x1, Pallas kernels: 48.8 us -> 2.24 us  [spread(): pl.pallas_call(spread_kernel, in_specs=[ANYWHERE], out_specs=ANYWHERE, ou...]
  transfers between devices with their start and end apart: 5 -> 5, of which waited for: 2 -> 2; matrix products, arithmetic and copies ran while one was open for 2% -> 2% of each run, Pallas kernels for 29% -> 2%
where the time goes in v6:
time: 125 us; the launch traced here: 123 us
  blocking collectives  65.8 us (53%)
  waiting for transfers between devices  20.4 us (16%)
  starting transfers between devices  20.2 us (16%)
  Pallas kernels  11.1 us (9%)
  local copies, waits for them, and re-layouts  2.87 us (2%)
  other arithmetic  2.79 us (2%)
    all_to_all x1, blocking collectives, per_device(): lax.all_to_all(send, 'dp', split_axis=0, concat_axis=0, tiled=True)  38.4 us
    all_to_all x1, blocking collectives, per_device(): lax.all_to_all(parts, 'tensor', 0, 0, axis_index_groups=classes, tiled=True)  27.4 us
    all_to_all x1, waiting for transfers between devices, per_device(): lax.all_to_all(sent, 'tensor', 0, 0, axis_index_groups=classes, tiled=True)  18.7 us
    ppermute x1, starting transfers between devices, per_device(): other = lax.ppermute(cut, 'tensor', swap)  8.74 us
    all_to_all x1, starting transfers between devices, per_device(): lax.all_to_all(sent, 'tensor', 0, 0, axis_index_groups=classes, tiled=True)  4.3 us
    pallas_call x1, Pallas kernels, backward(): pl.pallas_call(backward_kernel, in_specs=[SCALAR] + in_vmem(6) + [ANYWHER...  3.68 us
    pallas_call x1, Pallas kernels, forward(): pl.pallas_call(forward_kernel, in_specs=[SCALAR, ANYWHERE] + in_vmem(1) +...  3.2 us
    squeeze x1, local copies, waits for them, and re-layouts, per_device(): cut = lax.dynamic_index_in_dim(pairs, 1 - core, 1, False)  2.82 us
  transfers between devices with their start and end apart: 5, of which 2 were waited for; matrix products, arithmetic and copies ran while one was open for 2% of the time, Pallas kernels for 2%

profile of v6, /device:TPU:1, one launch (start us, length us, event | category | flops | bytes accessed | tf_op | source)
XLA Modules:
  0.0 123.4 jit_solution(2046957704975203998)
XLA Ops:
  0.0 0.0 copy-start
  0.0 0.0 copy-start.3
  0.0 0.0 copy-start.4
  0.0 2.8 %dynamic-slice_bitcast_fusion = bf16[8,384,256]{2,1,0:T(8,128)(2,1)} fusion(bf16[8,2,384,256]{3,2,1,0:T(8,128)(2,1)} %bitcast.10, s32[]{:T(128)S(6)} %select_n.31), kind=kLoop, calls=%fused_computation.2 | loop fusion | bytes 3145732 | tf_op jit(solution)/shard_map/jit(dynamic_index_in_dim)/squeeze | solution.py:323
  2.8 8.7 %collective-permute-start = (bf16[8,384,256]{2,1,0:T(8,128)(2,1)}, bf16[8,384,256]{2,1,0:T(8,128)(2,1)}, u32[]{:S(2)}, u32[]{:S(2)}) collective-permute-start(bf16[8,384,256]{2,1,0:T(8,128)(2,1)} %dynamic-slice_bitcast_fusion), channel_id=1, source_target_pairs={{0,1},{1,0},{2,3},{3,2},{4,5},{5,4},{6,7},{7,6},{8,9},{9,8},{10,11... | collective-permute-start | bytes 4718600 | tf_op jit(solution)/shard_map/ppermute | solution.py:324
  11.6 0.0 copy-done.3
  11.6 0.0 copy-done
  11.6 1.0 multiply_reduce_fusion
  12.6 0.0 copy-start.2
  12.6 0.0 copy-start.5
  12.6 0.0 copy-done.4
  12.7 2.1 %collective-permute-start.2 = (f32[3,256]{1,0:T(4,128)S(1)}, f32[3,256]{1,0:T(4,128)S(1)}, u32[]{:S(2)}, u32[]{:S(2)}) collective-permute-start(f32[3,256]{1,0:T(4,128)S(1)} %pad_maximum_fusion.vec_ref), channel_id=1, source_target_pairs={{0,1},{1,0},{2,3},{3,2},{4,5},{5,4},{6,7},{7,6},{8,9},{9,8},{10,11... | collective-permute-start | bytes 9224 | tf_op jit(solution)/shard_map/ppermute | solution.py:329
  14.7 2.2 %spread.1 = bf16[8,256,384]{2,1,0:T(8,128)(2,1)} custom-call(bf16[256,384]{1,0:T(8,128)(2,1)} %x_ref.1), custom_call_target="tpu_custom_call" | custom-call | tf_op jit(solution)/shard_map/spread/pallas_call | solution.py:57
  17.0 4.3 %all-to-all-start = ((bf16[8,256,384]{2,1,0:T(8,128)(2,1)}), bf16[8,256,384]{2,1,0:T(8,128)(2,1)}, u32[]{:S(2)}, u32[]{:S(2)}) async-start(bf16[8,256,384]{2,1,0:T(8,128)(2,1)} %spread.1), calls=%async_computation | async-start | bytes 3145728 | tf_op jit(solution)/shard_map/all_to_all | solution.py:320
  21.3 0.0 copy-done.2
  21.3 2.4 %collective-permute-start.1 = (bf16[256,256]{1,0:T(8,128)(2,1)S(1)}, bf16[256,256]{1,0:T(8,128)(2,1)S(1)}, u32[]{:S(2)}, u32[]{:S(2)}) collective-permute-start(bf16[256,256]{1,0:T(8,128)(2,1)S(1)} %copy-done.2), channel_id=1, source_target_pairs={{0,1},{1,0},{2,3},{3,2},{4,5},{5,4},{6,7},{7,6},{8,9},{9,8},{10,11... | collective-permute-start | bytes 393224 | tf_op jit(solution)/shard_map/ppermute | solution.py:325
  23.7 0.0 copy-done.5
  23.8 0.2 convert_reduce_fusion
  23.9 0.1 iota_add_fusion
  24.0 1.5 %select_reduce_fusion = s32[32,128]{1,0:T(8,128)S(1)} fusion(s32[256]{0:T(256)S(1)} %get-tuple-element.24, s32[256]{0:T(256)S(1)} %multiply_add_fusion, s32[32,128]{1,0:T(8,128)S(1)} %iota_add_fusion, pred[128]{0:T(512)(128)(4,1)S(1)} %iota_compare_fusion.1), kind=kLoop, calls=%fused_computation.1 | loop fusion | flops 4190208 | bytes 34944 | tf_op jit(solution)/shard_map/reduce_sum | solution.py:344
  25.6 0.0 collective-permute-done.2.veco_ref
  25.6 0.0 collective-permute-done.1.upo_ref
  25.6 18.7 %all-to-all-done.x_any = bf16[8,256,384]{2,1,0:T(8,128)(2,1)} async-done(((bf16[8,256,384]{2,1,0:T(8,128)(2,1)}), bf16[8,256,384]{2,1,0:T(8,128)(2,1)}, u32[]{:S(2)}, u32[]{:S(2)}) %all-to-all-start) | async-done | bytes 1572896 | tf_op jit(solution)/shard_map/all_to_all | solution.py:320
  44.3 0.0 collective-permute-done.other_any
  44.3 3.2 %forward.1.q_ref = f32[256,640]{1,0:T(8,128)S(1)} custom-call(s32[1]{0:T(128)} %bitcast.core_ref, bf16[8,256,384]{2,1,0:T(8,128)(2,1)} %all-to-all-done.x_any, f32[8,2,1,384]{3,2,1,0:T(1,128)S(1)} %bitcast.15, bf16[8,2,384,256]{3,2,1,0:T(8,128)(2,1)S(1)} %bitcast.12, bf16[8,384,256]{2,1,0:T(8,128)(2,1)} %collective-permute-done.other_any), custom_call_target="tpu_custom_call" | custom-call | tf_op jit(solution)/shard_map/forward/pallas_call | solution.py:133
  47.5 2.7 %collective-permute-start.3 = (f32[256,640]{1,0:T(8,128)S(1)}, f32[256,640]{1,0:T(8,128)S(1)}, u32[]{:S(2)}, u32[]{:S(2)}) collective-permute-start(f32[256,640]{1,0:T(8,128)S(1)} %forward.1.q_ref), channel_id=1, source_target_pairs={{0,1},{1,0},{2,3},{3,2},{4,5},{5,4},{6,7},{7,6},{8,9},{9,8},{10,11... | collective-permute-start | bytes 1966088 | tf_op jit(solution)/shard_map/ppermute | solution.py:352
  50.2 1.7 %collective-permute-done.3.got_ref = f32[256,640]{1,0:T(8,128)S(1)} collective-permute-done((f32[256,640]{1,0:T(8,128)S(1)}, f32[256,640]{1,0:T(8,128)S(1)}, u32[]{:S(2)}, u32[]{:S(2)}) %collective-permute-start.3) | collective-permute-done | bytes 655392 | tf_op jit(solution)/shard_map/ppermute | solution.py:352
  51.9 3.7 %backward.1 = (bf16[8,264,384]{2,1,0:T(8,128)(2,1)S(1)}, f32[256,128]{1,0:T(8,128)S(1)}) custom-call(s32[1]{0:T(128)} %bitcast.core_ref, f32[256,640]{1,0:T(8,128)S(1)} %forward.1.q_ref, f32[256,640]{1,0:T(8,128)S(1)} %collective-permute-done.3.got_ref, bf16[256,256]{1,0:T(8,128)(2,1)S(1)} %copy-done.2, bf16[256,256]{1,0:T(8,128)(2,1)S(1)} %collective-permute-done.1.upo_ref, ...), custom_call_target="tpu_custom_call" | custom-call | tf_op jit(solution)/shard_map/backward/pallas_call | solution.py:217
  55.6 0.0 copy-start.1
  55.6 27.4 %all_to_all.15.back_ref = bf16[8,264,384]{2,1,0:T(8,128)(2,1)S(1)} all-to-all(bf16[8,264,384]{2,1,0:T(8,128)(2,1)S(1)} %get-tuple-element.18), channel_id=1, replica_groups={{0,2,4,6,8,10,12,14},{1,3,5,7,9,11,13,15},{16,18,20,22,24,26,28,30},{17..., dimensions={0} | all-to-all | bytes 3244032 | tf_op jit(solution)/shard_map/all_to_all | solution.py:354
  83.0 0.0 copy-done.1
  83.1 0.8 finish.1
  83.9 38.4 %all_to_all.16.got_ref = bf16[32,50,128]{2,1,0:T(8,128)(2,1)S(1)} all-to-all(bf16[32,50,128]{2,1,0:T(8,128)(2,1)S(1)} %finish.1), channel_id=1, replica_groups=mesh['dp'=32,'tensor'=16] {'dp'}, dimensions={0} | all-to-all | bytes 819200 | tf_op jit(solution)/shard_map/all_to_all | solution.py:356
  122.2 1.2 land.1
  (8 shorter events, 0.1 us)
Async XLA Ops:
  0.0 11.6 %copy-start = (bf16[6144,256]{1,0:T(8,128)(2,1)S(1)}, bf16[6144,256]{1,0:T(8,128)(2,1)}, u32[]{:S(2)}) copy-start(bf16[6144,256]{1,0:T(8,128)(2,1)} %param.8) | copy-start | bytes 9437188
  0.0 11.6 %copy-start.3 = (f32[6144]{0:T(1024)S(1)}, f32[6144]{0:T(1024)}, u32[]{:S(2)}) copy-start(f32[6144]{0:T(1024)} %param.10) | copy-start | bytes 73732
  0.0 12.6 %copy-start.4 = (f32[256]{0:T(256)S(1)}, f32[256]{0:T(256)}, u32[]{:S(2)}) copy-start(f32[256]{0:T(256)} %param.9) | copy-start | bytes 3076
  2.8 41.5 %collective-permute-start = (bf16[8,384,256]{2,1,0:T(8,128)(2,1)}, bf16[8,384,256]{2,1,0:T(8,128)(2,1)}, u32[]{:S(2)}, u32[]{:S(2)}) collective-permute-start(bf16[8,384,256]{2,1,0:T(8,128)(2,1)} %dynamic-slice_bitcast_fusion), channel_id=1, source_target_pairs={{0,1},{1,0},{2,3},{3,2},{4,5},{5,4},{6,7},{7,6},{8,9},{9,8},{10,11... | collective-permute-start | bytes 4718600 | tf_op jit(solution)/shard_map/ppermute | solution.py:324
  12.6 8.7 %copy-start.2 = (bf16[256,256]{1,0:T(8,128)(2,1)S(1)}, bf16[256,256]{1,0:T(8,128)(2,1)}, u32[]{:S(2)}) copy-start(bf16[256,256]{1,0:T(8,128)(2,1)} %up_ref.1) | copy-start | bytes 393220
  12.6 11.1 %copy-start.5 = (s32[256]{0:T(256)S(1)}, s32[256]{0:T(256)}, u32[]{:S(2)}) copy-start(s32[256]{0:T(256)} %param.11) | copy-start | bytes 3076
  12.7 12.9 %collective-permute-start.2 = (f32[3,256]{1,0:T(4,128)S(1)}, f32[3,256]{1,0:T(4,128)S(1)}, u32[]{:S(2)}, u32[]{:S(2)}) collective-permute-start(f32[3,256]{1,0:T(4,128)S(1)} %pad_maximum_fusion.vec_ref), channel_id=1, source_target_pairs={{0,1},{1,0},{2,3},{3,2},{4,5},{5,4},{6,7},{7,6},{8,9},{9,8},{10,11... | collective-permute-start | bytes 9224 | tf_op jit(solution)/shard_map/ppermute | solution.py:329
  17.0 27.3 %all-to-all-start = ((bf16[8,256,384]{2,1,0:T(8,128)(2,1)}), bf16[8,256,384]{2,1,0:T(8,128)(2,1)}, u32[]{:S(2)}, u32[]{:S(2)}) async-start(bf16[8,256,384]{2,1,0:T(8,128)(2,1)} %spread.1), calls=%async_computation | async-start | bytes 3145728 | tf_op jit(solution)/shard_map/all_to_all | solution.py:320
  21.3 4.3 %collective-permute-start.1 = (bf16[256,256]{1,0:T(8,128)(2,1)S(1)}, bf16[256,256]{1,0:T(8,128)(2,1)S(1)}, u32[]{:S(2)}, u32[]{:S(2)}) collective-permute-start(bf16[256,256]{1,0:T(8,128)(2,1)S(1)} %copy-done.2), channel_id=1, source_target_pairs={{0,1},{1,0},{2,3},{3,2},{4,5},{5,4},{6,7},{7,6},{8,9},{9,8},{10,11... | collective-permute-start | bytes 393224 | tf_op jit(solution)/shard_map/ppermute | solution.py:325
  47.5 4.4 %collective-permute-start.3 = (f32[256,640]{1,0:T(8,128)S(1)}, f32[256,640]{1,0:T(8,128)S(1)}, u32[]{:S(2)}, u32[]{:S(2)}) collective-permute-start(f32[256,640]{1,0:T(8,128)S(1)} %forward.1.q_ref), channel_id=1, source_target_pairs={{0,1},{1,0},{2,3},{3,2},{4,5},{5,4},{6,7},{7,6},{8,9},{9,8},{10,11... | collective-permute-start | bytes 1966088 | tf_op jit(solution)/shard_map/ppermute | solution.py:352
  55.6 27.5 %copy-start.1 = (bf16[256,384]{1,0:T(8,128)(2,1)S(1)}, bf16[256,384]{1,0:T(8,128)(2,1)}, u32[]{:S(2)}) copy-start(bf16[256,384]{1,0:T(8,128)(2,1)} %x_ref.1) | copy-start | bytes 589828

commit v7 on v6

--- a/solution.py
+++ b/solution.py
@@ -10,6 +10,7 @@
 f32, bf16 = jnp.float32, jnp.bfloat16
 PAD = 8
 CAPACITY = 16
+EARLY = 2
 NT = (((1,), (1,)), ((), ()))
 
 
@@ -158,17 +159,20 @@
     veco_ref,
     weight_any,
     other_any,
-    p_ref,
+    p_any,
     st_ref,
     weight_ref,
+    p_ref,
     w_sem,
     o_sem,
+    p_sem,
 ):
     blocks, feats, width = weight_ref.shape
     width = width // 2
     rows = q_ref.shape[0]
     core = core_ref[0]
     w_copies = weight_copies(core, weight_any, other_any, weight_ref, w_sem, o_sem)
+    p_copies = [pltpu.make_async_copy(p_ref.at[b], p_any.at[b], p_sem.at[b]) for b in range(blocks)]
     for pair in w_copies:
         for copy in pair:
             copy.start()
@@ -209,6 +213,9 @@
             copy.wait()
         p_ref[b, :rows] = lax.dot_general(both, weight_ref[b], NT, preferred_element_type=f32).astype(bf16)
         p_ref[b, rows:] = tail
+        p_copies[b].start()
+    for copy in p_copies:
+        copy.wait()
 
 
 def backward(core, q, got, up, upo, vec, veco, weight, other):
@@ -217,13 +224,15 @@
     return pl.pallas_call(
         backward_kernel,
         in_specs=[SCALAR] + in_vmem(6) + [ANYWHERE, ANYWHERE],
-        out_specs=in_vmem(2),
+        out_specs=[ANYWHERE] + in_vmem(1),
         out_shape=[
-            pltpu.VMEM((blocks, rows + PAD, feats), bf16),
+            pltpu.HBM((blocks, rows + PAD, feats), bf16),
             pltpu.VMEM((rows, 128), f32),
         ],
         scratch_shapes=[
             pltpu.VMEM((blocks, feats, 2 * width), bf16),
+            pltpu.VMEM((blocks, rows + PAD, feats), bf16),
+            pltpu.SemaphoreType.DMA((blocks,)),
             pltpu.SemaphoreType.DMA((blocks,)),
             pltpu.SemaphoreType.DMA((blocks,)),
         ],
@@ -232,7 +241,9 @@
     )(core, q, got, up, upo, vec, veco, weight, other)
 
 
-def finish_kernel(back_ref, x_ref, st_ref, gain_ref, target_ref, slot_ref, send_ref):
+def finish_kernel(back_ref, x_any, st_ref, gain_ref, target_ref, send_ref, x_ref, sem):
+    fetch = pltpu.make_async_copy(x_any, x_ref, sem)
+    fetch.start()
     blocks = back_ref.shape[0]
     rows, feats = x_ref.shape
     owners = send_ref.shape[0]
@@ -244,6 +255,7 @@
     first = sums[:, 0:1] + sums[:, 1:2]
     second = sums[:, 2:3] + sums[:, 3:4]
     mean, inv_std = st_ref[:, 0:1], st_ref[:, 1:2]
+    fetch.wait()
     unit = (x_ref[...].astype(f32) - mean) * inv_std
     grad = (inv_std * (total[:rows] * gain_ref[...] - first - unit * second)).astype(bf16)
     slots = owners * CAPACITY
@@ -254,55 +266,56 @@
     placed = placed.reshape(owners, CAPACITY, feats)
     for k in range(feats // 128):
         send_ref[:, k * CAPACITY : (k + 1) * CAPACITY, :] = placed[:, :, k * 128 : (k + 1) * 128]
-    send_ref[:, feats // 128 * CAPACITY :, :] = jnp.broadcast_to(
-        slot_ref[...][:, None, :], (owners, 2, 128)
-    )
-
-
-def finish(back, x, st, gain, target, slot):
-    owners = slot.shape[0]
+
+
+def finish(back, x, st, gain, target, owners):
     return pl.pallas_call(
         finish_kernel,
-        in_specs=in_vmem(6),
+        in_specs=in_vmem(1) + [ANYWHERE] + in_vmem(3),
         out_specs=in_vmem(1)[0],
-        out_shape=pltpu.VMEM((owners, x.shape[1] // 128 * CAPACITY + 2, 128), bf16),
+        scratch_shapes=[pltpu.VMEM(x.shape, x.dtype), pltpu.SemaphoreType.DMA],
+        out_shape=pltpu.VMEM((owners, x.shape[1] // 128 * CAPACITY, 128), bf16),
         compiler_params=PARAMS,
         name="finish",
-    )(*held(back, x, st, gain, target, slot))
-
-
-def landing_kernel(got_ref, o_ref):
+    )(*held(back), pltpu.with_memory_space_constraint(x, pltpu.HBM), *held(st, gain, target))
+
+
+def landing_kernel(got_ref, slot_ref, o_ref):
     rows, feats = o_ref.shape
-    owners = got_ref.shape[0]
-    slots = owners * CAPACITY
-    pieces = feats // 128
-    held_slots = got_ref[:, pieces * CAPACITY, :].astype(bf16)
-    spread = lax.broadcasted_iota(jnp.int32, (128, slots), 0) == (
-        lax.broadcasted_iota(jnp.int32, (128, slots), 1) % CAPACITY
-    )
-    every = jnp.dot(held_slots, jnp.where(spread, 1.0, 0.0).astype(bf16), preferred_element_type=f32)
-    own = lax.broadcasted_iota(jnp.int32, (owners, slots), 0) == (
-        lax.broadcasted_iota(jnp.int32, (owners, slots), 1) // CAPACITY
-    )
-    slot = jnp.sum(jnp.where(own, every, 0.0), axis=0, keepdims=True).astype(jnp.int32)
-    landing = lax.broadcasted_iota(jnp.int32, (rows, slots), 0) == slot
+    slots = slot_ref.shape[1]
+    landing = lax.broadcasted_iota(jnp.int32, (rows, slots), 0) == slot_ref[...]
     landing = jnp.where(landing, 1.0, 0.0).astype(bf16)
-    for k in range(pieces):
+    for k in range(feats // 128):
         piece = got_ref[:, k * CAPACITY : (k + 1) * CAPACITY, :].reshape(slots, 128)
         o_ref[:, k * 128 : (k + 1) * 128] = jnp.dot(
             landing, piece, preferred_element_type=f32
         ).astype(bf16)
 
 
-def land(got, rows, feats):
+def land(got, slot, rows, feats):
     return pl.pallas_call(
         landing_kernel,
-        in_specs=in_vmem(1),
+        in_specs=in_vmem(2),
         out_specs=in_vmem(1)[0],
         out_shape=jax.ShapeDtypeStruct((rows, feats), bf16),
         compiler_params=PARAMS,
         name="land",
-    )(*held(got))
+    )(*held(got, slot))
+
+
+def arriving_slots(listed, rows):
+    owners = listed.shape[0]
+    me = lax.axis_index("dp")
+    ids = jnp.arange(rows, dtype=jnp.int32)
+    mine = listed // rows == me
+    below = (ids[:, None] < ids[None, :]).astype(bf16)
+    rank = jnp.dot(mine.astype(bf16), below, preferred_element_type=f32).astype(jnp.int32)
+    places = jnp.arange(CAPACITY, dtype=jnp.int32)[None, :, None]
+    match = mine[:, None, :] & (rank[:, None, :] == places)
+    slot = jnp.sum(jnp.where(match, listed[:, None, :] % rows + 1, 0), axis=2) - 1
+    index = jnp.arange(owners, dtype=jnp.int32)
+    source = (me - index[:, None]) % owners == index[None, :]
+    return jnp.sum(jnp.where(source[:, :, None], slot[None], 0), axis=1).reshape(1, -1)
 
 
 def per_device(inputs, upstream, proj_weight, proj_bias, norm_gain, home_rows):
@@ -329,7 +342,6 @@
     veco = lax.ppermute(vec, "tensor", swap)
 
     owner_of = home_rows // rows
-    home_slot = home_rows % rows
     order_ids = jnp.arange(rows, dtype=jnp.int32)
     earlier = jnp.sum(
         ((owner_of[:, None] == owner_of[None, :]) & (order_ids[:, None] > order_ids[None, :])).astype(
@@ -338,23 +350,32 @@
         axis=1,
     )
     target = owner_of * CAPACITY + earlier
-    lanes = jnp.arange(128, dtype=jnp.int32)
-    held_at = (jnp.arange(owners, dtype=jnp.int32)[:, None] * CAPACITY + lanes[None, :])[:, :, None]
-    match = (held_at == target[None, None, :]) & (lanes < CAPACITY)[None, :, None]
-    slot = jnp.sum(jnp.where(match, home_slot[None, None, :] + 1, 0), axis=2) - 1
-    slot = slot.astype(f32).astype(bf16)
+
+    def doubled(listed, step):
+        hop = [(d, (d + 2**step) % owners) for d in range(owners)]
+        return jnp.concatenate([listed, lax.ppermute(listed, "dp", hop)], axis=0)
+
+    steps = owners.bit_length() - 1
+    listed = home_rows[None]
+    for step in range(EARLY):
+        listed = doubled(listed, step)
 
     own_gain = lax.dynamic_index_in_dim(norm_gain.reshape(n_tensor, 1, feats), me, 0, False)
-    half, other, upo, veco, slot, target, own_gain = lax.optimization_barrier(
-        (half, other, upo, veco, slot, target, own_gain)
+    half, other, upo, veco, listed, target, own_gain = lax.optimization_barrier(
+        (half, other, upo, veco, listed, target, own_gain)
     )
     q = forward(core_arr, half, gains, pairs, other)
     got = lax.ppermute(q, "tensor", swap)
     parts, st = backward(core_arr, q, got, upstream, upo, vec, veco, pairs, other)
+    parts, listed = lax.optimization_barrier((parts, listed))
     back = lax.all_to_all(parts, "tensor", 0, 0, axis_index_groups=classes, tiled=True)
-    send = finish(back, inputs, st, own_gain, target[None, :], slot)
+    for step in range(EARLY, steps):
+        listed = doubled(listed, step)
+    slot = arriving_slots(listed, rows)
+    back, slot = lax.optimization_barrier((back, slot))
+    send = finish(back, inputs, st, own_gain, target[None, :], owners)
     arrived = lax.all_to_all(send, "dp", split_axis=0, concat_axis=0, tiled=True)
-    return land(arrived, rows, feats)
+    return land(arrived, slot, rows, feats)
 
 
 def solution(mesh):

time: 125 us -> 130 us (1.040)
  blocking collectives: 65.8 us -> 36.7 us
  starting transfers between devices: 20.2 us -> 48.8 us
  other arithmetic: 2.79 us -> 5.98 us
  Pallas kernels: 11.1 us -> 12.8 us
    all_to_all x1 -> x0, blocking collectives: 27.4 us -> none  [per_device(): lax.all_to_all(parts, 'tensor', 0, 0, axis_index_groups=classes, tiled=True)]
    ppermute x0 -> x5, starting transfers between devices: none -> 23.4 us  [doubled(): return jnp.concatenate([listed, lax.ppermute(listed, 'dp', hop)], axis=0)]
    ppermute x0 -> x5, waiting for transfers between devices: none -> 15.5 us  [doubled(): return jnp.concatenate([listed, lax.ppermute(listed, 'dp', hop)], axis=0)]
    all_to_all x1, waiting for transfers between devices: 18.7 us -> 3.94 us  [per_device(): lax.all_to_all(sent, 'tensor', 0, 0, axis_index_groups=classes, tiled=True)]
    all_to_all x0 -> x1, starting transfers between devices: none -> 4.99 us  [per_device(): lax.all_to_all(parts, 'tensor', 0, 0, axis_index_groups=classes, tiled=True)]
    concatenate x0 -> x4, other arithmetic: none -> 2 us  [doubled(): return jnp.concatenate([listed, lax.ppermute(listed, 'dp', hop)], axis=0)]
    all_to_all x1, blocking collectives: 38.4 us -> 36.7 us  [per_device(): lax.all_to_all(send, 'dp', split_axis=0, concat_axis=0, tiled=True)]
  transfers between devices with their start and end apart: 5 -> 11, of which waited for: 2 -> 6; matrix products, arithmetic and copies ran while one was open for 2% -> 5% of each run, Pallas kernels for 2% -> 2%
where the time goes in v7:
time: 130 us; the launch traced here: 129 us
  starting transfers between devices  48.8 us (38%)
  blocking collectives  36.7 us (28%)
  waiting for transfers between devices  21.1 us (16%)
  Pallas kernels  12.8 us (10%)
  other arithmetic  5.98 us (5%)
  local copies, waits for them, and re-layouts  2.87 us (2%)
    all_to_all x1, blocking collectives, per_device(): lax.all_to_all(send, 'dp', split_axis=0, concat_axis=0, tiled=True)  36.7 us
    ppermute x5, starting transfers between devices, doubled(): return jnp.concatenate([listed, lax.ppermute(listed, 'dp', hop)], axis=0)  23.4 us
    ppermute x5, waiting for transfers between devices, doubled(): return jnp.concatenate([listed, lax.ppermute(listed, 'dp', hop)], axis=0)  15.5 us
    ppermute x1, starting transfers between devices, per_device(): other = lax.ppermute(cut, 'tensor', swap)  8.74 us
    all_to_all x1, starting transfers between devices, per_device(): lax.all_to_all(parts, 'tensor', 0, 0, axis_index_groups=classes, tiled=True)  4.99 us
    all_to_all x1, starting transfers between devices, per_device(): lax.all_to_all(sent, 'tensor', 0, 0, axis_index_groups=classes, tiled=True)  4.57 us
    pallas_call x1, Pallas kernels, backward(): pl.pallas_call(backward_kernel, in_specs=[SCALAR] + in_vmem(6) + [ANYWHER...  4.47 us
    all_to_all x1, waiting for transfers between devices, per_device(): lax.all_to_all(sent, 'tensor', 0, 0, axis_index_groups=classes, tiled=True)  3.94 us
  transfers between devices with their start and end apart: 11, of which 6 were waited for; matrix products, arithmetic and copies ran while one was open for 5% of the time, Pallas kernels for 2%

profile of v7, /device:TPU:1, one launch (start us, length us, event | category | flops | bytes accessed | tf_op | source)
XLA Modules:
  0.0 128.8 jit_solution(4342785325715938806)
XLA Ops:
  0.0 2.7 %dynamic-slice_bitcast_fusion = bf16[8,384,256]{2,1,0:T(8,128)(2,1)} fusion(bf16[8,2,384,256]{3,2,1,0:T(8,128)(2,1)} %bitcast.12, s32[]{:T(128)S(6)} %select_n.60), kind=kLoop, calls=%fused_computation.1 | loop fusion | bytes 3145732 | tf_op jit(solution)/shard_map/jit(dynamic_index_in_dim)/squeeze | solution.py:336
  2.7 8.7 %collective-permute-start = (bf16[8,384,256]{2,1,0:T(8,128)(2,1)}, bf16[8,384,256]{2,1,0:T(8,128)(2,1)}, u32[]{:S(2)}, u32[]{:S(2)}) collective-permute-start(bf16[8,384,256]{2,1,0:T(8,128)(2,1)} %dynamic-slice_bitcast_fusion), channel_id=1, source_target_pairs={{0,1},{1,0},{2,3},{3,2},{4,5},{5,4},{6,7},{7,6},{8,9},{9,8},{10,11... | collective-permute-start | bytes 4718600 | tf_op jit(solution)/shard_map/ppermute | solution.py:337
  11.4 0.0 copy-start.2
  11.4 2.2 %spread.1 = bf16[8,256,384]{2,1,0:T(8,128)(2,1)} custom-call(bf16[256,384]{1,0:T(8,128)(2,1)} %x_any.3), custom_call_target="tpu_custom_call" | custom-call | tf_op jit(solution)/shard_map/spread/pallas_call | solution.py:58
  13.7 0.0 copy-start.3
  13.7 0.0 copy-start
  13.7 4.6 %all-to-all-start = ((bf16[8,256,384]{2,1,0:T(8,128)(2,1)}), bf16[8,256,384]{2,1,0:T(8,128)(2,1)}, u32[]{:S(2)}, u32[]{:S(2)}) async-start(bf16[8,256,384]{2,1,0:T(8,128)(2,1)} %spread.1), calls=%async_computation | async-start | bytes 3145728 | tf_op jit(solution)/shard_map/all_to_all | solution.py:333
  18.3 0.0 copy-start.4
  18.3 0.0 copy-start.1
  18.3 0.0 copy-done.3
  18.3 2.1 %collective-permute-start.3 = (s32[1,256]{1,0:T(1,128)S(1)}, s32[1,256]{1,0:T(1,128)S(1)}, u32[]{:S(2)}, u32[]{:S(2)}) collective-permute-start(s32[1,256]{1,0:T(1,128)S(1)} %bitcast.19), channel_id=1, source_target_pairs={{0,16},{16,32},{32,48},{48,64},{64,80},{80,96},{96,112},{112,128},... | collective-permute-start | bytes 3080 | tf_op jit(solution)/shard_map/ppermute | solution.py:356
  20.4 0.0 copy-done.2
  20.4 0.0 copy-done
  20.4 1.0 multiply_reduce_fusion
  21.4 0.0 copy-done.4
  21.4 1.9 %collective-permute-start.2 = (f32[3,256]{1,0:T(4,128)S(1)}, f32[3,256]{1,0:T(4,128)S(1)}, u32[]{:S(2)}, u32[]{:S(2)}) collective-permute-start(f32[3,256]{1,0:T(4,128)S(1)} %pad_maximum_fusion.vec_ref), channel_id=1, source_target_pairs={{0,1},{1,0},{2,3},{3,2},{4,5},{5,4},{6,7},{7,6},{8,9},{9,8},{10,11... | collective-permute-start | bytes 9224 | tf_op jit(solution)/shard_map/ppermute | solution.py:342
  23.4 0.0 copy-done.1
  23.4 2.4 %collective-permute-start.1 = (bf16[256,256]{1,0:T(8,128)(2,1)S(1)}, bf16[256,256]{1,0:T(8,128)(2,1)S(1)}, u32[]{:S(2)}, u32[]{:S(2)}) collective-permute-start(bf16[256,256]{1,0:T(8,128)(2,1)S(1)} %copy-done.1), channel_id=1, source_target_pairs={{0,1},{1,0},{2,3},{3,2},{4,5},{5,4},{6,7},{7,6},{8,9},{9,8},{10,11... | collective-permute-start | bytes 393224 | tf_op jit(solution)/shard_map/ppermute | solution.py:338
  25.8 0.2 convert_reduce_fusion
  26.0 3.4 %collective-permute-done.3 = s32[1,256]{1,0:T(1,128)S(1)} collective-permute-done((s32[1,256]{1,0:T(1,128)S(1)}, s32[1,256]{1,0:T(1,128)S(1)}, u32[]{:S(2)}, u32[]{:S(2)}) %collective-permute-start.3) | collective-permute-done | bytes 1056 | tf_op jit(solution)/shard_map/ppermute | solution.py:356
  29.4 1.9 %collective-permute-start.4 = (s32[2,256]{1,0:T(2,128)S(1)}, s32[2,256]{1,0:T(2,128)S(1)}, u32[]{:S(2)}, u32[]{:S(2)}) collective-permute-start(s32[2,256]{1,0:T(2,128)S(1)} %pad_add_fusion.4), channel_id=1, source_target_pairs={{0,32},{16,48},{32,64},{48,80},{64,96},{80,112},{96,128},{112,144}... | collective-permute-start | bytes 6152 | tf_op jit(solution)/shard_map/ppermute | solution.py:356
  31.3 5.4 %collective-permute-done.4 = s32[2,256]{1,0:T(2,128)S(1)} collective-permute-done((s32[2,256]{1,0:T(2,128)S(1)}, s32[2,256]{1,0:T(2,128)S(1)}, u32[]{:S(2)}, u32[]{:S(2)}) %collective-permute-start.4) | collective-permute-done | bytes 2080 | tf_op jit(solution)/shard_map/ppermute | solution.py:356
  36.7 0.6 pad_add_fusion.3
  37.3 0.0 collective-permute-done.2.veco_ref
  37.3 0.0 collective-permute-done.1.upo_ref
  37.3 3.9 %all-to-all-done.x_any = bf16[8,256,384]{2,1,0:T(8,128)(2,1)} async-done(((bf16[8,256,384]{2,1,0:T(8,128)(2,1)}), bf16[8,256,384]{2,1,0:T(8,128)(2,1)}, u32[]{:S(2)}, u32[]{:S(2)}) %all-to-all-start) | async-done | bytes 1572896 | tf_op jit(solution)/shard_map/all_to_all | solution.py:333
  41.3 0.0 collective-permute-done.other_any
  41.3 3.2 %forward.1.q_ref = f32[256,640]{1,0:T(8,128)S(1)} custom-call(s32[1]{0:T(128)} %bitcast.core_ref, bf16[8,256,384]{2,1,0:T(8,128)(2,1)} %all-to-all-done.x_any, f32[8,2,1,384]{3,2,1,0:T(1,128)S(1)} %bitcast.17, bf16[8,2,384,256]{3,2,1,0:T(8,128)(2,1)S(1)} %bitcast.14, bf16[8,384,256]{2,1,0:T(8,128)(2,1)} %collective-permute-done.other_any), custom_call_target="tpu_custom_call" | custom-call | tf_op jit(solution)/shard_map/forward/pallas_call | solution.py:134
  44.5 2.7 %collective-permute-start.5 = (f32[256,640]{1,0:T(8,128)S(1)}, f32[256,640]{1,0:T(8,128)S(1)}, u32[]{:S(2)}, u32[]{:S(2)}) collective-permute-start(f32[256,640]{1,0:T(8,128)S(1)} %forward.1.q_ref), channel_id=1, source_target_pairs={{0,1},{1,0},{2,3},{3,2},{4,5},{5,4},{6,7},{7,6},{8,9},{9,8},{10,11... | collective-permute-start | bytes 1966088 | tf_op jit(solution)/shard_map/ppermute | solution.py:368
  47.2 1.7 %collective-permute-done.5.got_ref = f32[256,640]{1,0:T(8,128)S(1)} collective-permute-done((f32[256,640]{1,0:T(8,128)S(1)}, f32[256,640]{1,0:T(8,128)S(1)}, u32[]{:S(2)}, u32[]{:S(2)}) %collective-permute-start.5) | collective-permute-done | bytes 655392 | tf_op jit(solution)/shard_map/ppermute | solution.py:368
  48.9 4.5 %backward.1 = (bf16[8,264,384]{2,1,0:T(8,128)(2,1)}, f32[256,128]{1,0:T(8,128)S(1)}) custom-call(s32[1]{0:T(128)} %bitcast.core_ref, f32[256,640]{1,0:T(8,128)S(1)} %forward.1.q_ref, f32[256,640]{1,0:T(8,128)S(1)} %collective-permute-done.5.got_ref, bf16[256,256]{1,0:T(8,128)(2,1)S(1)} %copy-done.1, bf16[256,256]{1,0:T(8,128)(2,1)S(1)} %collective-permute-done.1.upo_ref, ...), custom_call_target="tpu_custom_call" | custom-call | tf_op jit(solution)/shard_map/backward/pallas_call | solution.py:224
  53.4 5.9 %collective-permute-start.6 = (s32[4,256]{1,0:T(4,128)}, s32[4,256]{1,0:T(4,128)S(1)}, u32[]{:S(2)}, u32[]{:S(2)}) collective-permute-start(s32[4,256]{1,0:T(4,128)} %pad_add_fusion.3), channel_id=1, source_target_pairs={{0,64},{16,80},{32,96},{48,112},{64,128},{80,144},{96,160},{112,17... | collective-permute-start | bytes 12296 | tf_op jit(solution)/shard_map/ppermute | solution.py:356
  59.3 5.0 %all-to-all-start.1 = ((bf16[8,264,384]{2,1,0:T(8,128)(2,1)}), bf16[8,264,384]{2,1,0:T(8,128)(2,1)S(1)}, u32[]{:S(2)}, u32[]{:S(2)}) async-start(bf16[8,264,384]{2,1,0:T(8,128)(2,1)} %get-tuple-element.24), calls=%async_computation.1 | async-start | bytes 3244032 | tf_op jit(solution)/shard_map/all_to_all | solution.py:371
  64.3 0.0 collective-permute-done.6
  64.3 0.7 pad_add_fusion.2
  65.0 10.6 %collective-permute-start.7 = (s32[8,256]{1,0:T(8,128)S(1)}, s32[8,256]{1,0:T(8,128)S(1)}, u32[]{:S(2)}, u32[]{:S(2)}) collective-permute-start(s32[8,256]{1,0:T(8,128)S(1)} %pad_add_fusion.2), channel_id=1, source_target_pairs={{0,128},{16,144},{32,160},{48,176},{64,192},{80,208},{96,224},{112... | collective-permute-start | bytes 24584 | tf_op jit(solution)/shard_map/ppermute | solution.py:356
  75.7 3.9 %collective-permute-done.7 = s32[8,256]{1,0:T(8,128)S(1)} collective-permute-done((s32[8,256]{1,0:T(8,128)S(1)}, s32[8,256]{1,0:T(8,128)S(1)}, u32[]{:S(2)}, u32[]{:S(2)}) %collective-permute-start.7) | collective-permute-done | bytes 8224 | tf_op jit(solution)/shard_map/ppermute | solution.py:356
  79.6 0.7 pad_add_fusion.1
  80.3 3.0 %collective-permute-start.8 = (s32[16,256]{1,0:T(8,128)S(1)}, s32[16,256]{1,0:T(8,128)S(1)}, u32[]{:S(2)}, u32[]{:S(2)}) collective-permute-start(s32[16,256]{1,0:T(8,128)S(1)} %pad_add_fusion.1), channel_id=1, source_target_pairs={{0,256},{16,272},{32,288},{48,304},{64,320},{80,336},{96,352},{112... | collective-permute-start | bytes 49160 | tf_op jit(solution)/shard_map/ppermute | solution.py:356
  83.3 0.1 iota_compare_fusion.4
  83.3 2.8 %collective-permute-done.8 = s32[16,256]{1,0:T(8,128)S(1)} collective-permute-done((s32[16,256]{1,0:T(8,128)S(1)}, s32[16,256]{1,0:T(8,128)S(1)}, u32[]{:S(2)}, u32[]{:S(2)}) %collective-permute-start.8) | collective-permute-done | bytes 16416 | tf_op jit(solution)/shard_map/ppermute | solution.py:356
  86.1 0.7 fusion.2
  86.8 0.7 fusion.3
  87.6 0.2 convolution_convert_fusion
  87.7 0.6 select_reduce_fusion
  88.3 0.1 copy.8
  88.4 0.6 select_reduce_fusion.1
  89.0 0.1 reshape.280.slot_ref
  89.1 0.0 all-to-all-done.1.back_ref
  89.1 1.8 %finish.1 = bf16[32,48,128]{2,1,0:T(8,128)(2,1)S(1)} custom-call(bf16[8,264,384]{2,1,0:T(8,128)(2,1)S(1)} %all-to-all-done.1.back_ref, bf16[256,384]{1,0:T(8,128)(2,1)} %x_any.3, f32[256,128]{1,0:T(8,128)S(1)} %get-tuple-element.27.st_ref, f32[1,384]{1,0:T(1,128)S(1)} %dynamic-slice_bitcast_fusion.1.gain_ref, s32[1,256]{1,0:T(1,128)S(1)} %bitcast.18), custom_call_target="tpu_custom_call" | custom-call | tf_op jit(solution)/shard_map/finish/pallas_call | solution.py:272
  91.0 36.7 %all_to_all.15.got_ref = bf16[32,48,128]{2,1,0:T(8,128)(2,1)S(1)} all-to-all(bf16[32,48,128]{2,1,0:T(8,128)(2,1)S(1)} %finish.1), channel_id=1, replica_groups=mesh['dp'=32,'tensor'=16] {'dp'}, dimensions={0} | all-to-all | bytes 786432 | tf_op jit(solution)/shard_map/all_to_all | solution.py:377
  127.7 1.1 land.1
  (8 shorter events, 0.1 us)
Async XLA Ops:
  2.7 38.6 %collective-permute-start = (bf16[8,384,256]{2,1,0:T(8,128)(2,1)}, bf16[8,384,256]{2,1,0:T(8,128)(2,1)}, u32[]{:S(2)}, u32[]{:S(2)}) collective-permute-start(bf16[8,384,256]{2,1,0:T(8,128)(2,1)} %dynamic-slice_bitcast_fusion), channel_id=1, source_target_pairs={{0,1},{1,0},{2,3},{3,2},{4,5},{5,4},{6,7},{7,6},{8,9},{9,8},{10,11... | collective-permute-start | bytes 4718600 | tf_op jit(solution)/shard_map/ppermute | solution.py:337
  11.4 9.0 %copy-start.2 = (f32[6144]{0:T(1024)S(1)}, f32[6144]{0:T(1024)}, u32[]{:S(2)}) copy-start(f32[6144]{0:T(1024)} %param.10) | copy-start | bytes 73732
  13.7 4.6 %copy-start.3 = (s32[256]{0:T(256)S(1)}, s32[256]{0:T(256)}, u32[]{:S(2)}) copy-start(s32[256]{0:T(256)} %param.11) | copy-start | bytes 3076
  13.7 6.7 %copy-start = (bf16[6144,256]{1,0:T(8,128)(2,1)S(1)}, bf16[6144,256]{1,0:T(8,128)(2,1)}, u32[]{:S(2)}) copy-start(bf16[6144,256]{1,0:T(8,128)(2,1)} %param.8) | copy-start | bytes 9437188
  13.7 27.6 %all-to-all-start = ((bf16[8,256,384]{2,1,0:T(8,128)(2,1)}), bf16[8,256,384]{2,1,0:T(8,128)(2,1)}, u32[]{:S(2)}, u32[]{:S(2)}) async-start(bf16[8,256,384]{2,1,0:T(8,128)(2,1)} %spread.1), calls=%async_computation | async-start | bytes 3145728 | tf_op jit(solution)/shard_map/all_to_all | solution.py:333
  18.3 3.1 %copy-start.4 = (f32[256]{0:T(256)S(1)}, f32[256]{0:T(256)}, u32[]{:S(2)}) copy-start(f32[256]{0:T(256)} %param.9) | copy-start | bytes 3076
  18.3 5.1 %copy-start.1 = (bf16[256,256]{1,0:T(8,128)(2,1)S(1)}, bf16[256,256]{1,0:T(8,128)(2,1)}, u32[]{:S(2)}) copy-start(bf16[256,256]{1,0:T(8,128)(2,1)} %up_ref.1) | copy-start | bytes 393220
  18.3 11.1 %collective-permute-start.3 = (s32[1,256]{1,0:T(1,128)S(1)}, s32[1,256]{1,0:T(1,128)S(1)}, u32[]{:S(2)}, u32[]{:S(2)}) collective-permute-start(s32[1,256]{1,0:T(1,128)S(1)} %bitcast.19), channel_id=1, source_target_pairs={{0,16},{16,32},{32,48},{48,64},{64,80},{80,96},{96,112},{112,128},... | collective-permute-start | bytes 3080 | tf_op jit(solution)/shard_map/ppermute | solution.py:356
  21.4 15.9 %collective-permute-start.2 = (f32[3,256]{1,0:T(4,128)S(1)}, f32[3,256]{1,0:T(4,128)S(1)}, u32[]{:S(2)}, u32[]{:S(2)}) collective-permute-start(f32[3,256]{1,0:T(4,128)S(1)} %pad_maximum_fusion.vec_ref), channel_id=1, source_target_pairs={{0,1},{1,0},{2,3},{3,2},{4,5},{5,4},{6,7},{7,6},{8,9},{9,8},{10,11... | collective-permute-start | bytes 9224 | tf_op jit(solution)/shard_map/ppermute | solution.py:342
  23.4 14.0 %collective-permute-start.1 = (bf16[256,256]{1,0:T(8,128)(2,1)S(1)}, bf16[256,256]{1,0:T(8,128)(2,1)S(1)}, u32[]{:S(2)}, u32[]{:S(2)}) collective-permute-start(bf16[256,256]{1,0:T(8,128)(2,1)S(1)} %copy-done.1), channel_id=1, source_target_pairs={{0,1},{1,0},{2,3},{3,2},{4,5},{5,4},{6,7},{7,6},{8,9},{9,8},{10,11... | collective-permute-start | bytes 393224 | tf_op jit(solution)/shard_map/ppermute | solution.py:338
  29.4 7.3 %collective-permute-start.4 = (s32[2,256]{1,0:T(2,128)S(1)}, s32[2,256]{1,0:T(2,128)S(1)}, u32[]{:S(2)}, u32[]{:S(2)}) collective-permute-start(s32[2,256]{1,0:T(2,128)S(1)} %pad_add_fusion.4), channel_id=1, source_target_pairs={{0,32},{16,48},{32,64},{48,80},{64,96},{80,112},{96,128},{112,144}... | collective-permute-start | bytes 6152 | tf_op jit(solution)/shard_map/ppermute | solution.py:356
  44.5 4.4 %collective-permute-start.5 = (f32[256,640]{1,0:T(8,128)S(1)}, f32[256,640]{1,0:T(8,128)S(1)}, u32[]{:S(2)}, u32[]{:S(2)}) collective-permute-start(f32[256,640]{1,0:T(8,128)S(1)} %forward.1.q_ref), channel_id=1, source_target_pairs={{0,1},{1,0},{2,3},{3,2},{4,5},{5,4},{6,7},{7,6},{8,9},{9,8},{10,11... | collective-permute-start | bytes 1966088 | tf_op jit(solution)/shard_map/ppermute | solution.py:368
  53.4 10.9 %collective-permute-start.6 = (s32[4,256]{1,0:T(4,128)}, s32[4,256]{1,0:T(4,128)S(1)}, u32[]{:S(2)}, u32[]{:S(2)}) collective-permute-start(s32[4,256]{1,0:T(4,128)} %pad_add_fusion.3), channel_id=1, source_target_pairs={{0,64},{16,80},{32,96},{48,112},{64,128},{80,144},{96,160},{112,17... | collective-permute-start | bytes 12296 | tf_op jit(solution)/shard_map/ppermute | solution.py:356
  59.3 29.8 %all-to-all-start.1 = ((bf16[8,264,384]{2,1,0:T(8,128)(2,1)}), bf16[8,264,384]{2,1,0:T(8,128)(2,1)S(1)}, u32[]{:S(2)}, u32[]{:S(2)}) async-start(bf16[8,264,384]{2,1,0:T(8,128)(2,1)} %get-tuple-element.24), calls=%async_computation.1 | async-start | bytes 3244032 | tf_op jit(solution)/shard_map/all_to_all | solution.py:371
  65.0 14.6 %collective-permute-start.7 = (s32[8,256]{1,0:T(8,128)S(1)}, s32[8,256]{1,0:T(8,128)S(1)}, u32[]{:S(2)}, u32[]{:S(2)}) collective-permute-start(s32[8,256]{1,0:T(8,128)S(1)} %pad_add_fusion.2), channel_id=1, source_target_pairs={{0,128},{16,144},{32,160},{48,176},{64,192},{80,208},{96,224},{112... | collective-permute-start | bytes 24584 | tf_op jit(solution)/shard_map/ppermute | solution.py:356
  80.3 5.8 %collective-permute-start.8 = (s32[16,256]{1,0:T(8,128)S(1)}, s32[16,256]{1,0:T(8,128)S(1)}, u32[]{:S(2)}, u32[]{:S(2)}) collective-permute-start(s32[16,256]{1,0:T(8,128)S(1)} %pad_add_fusion.1), channel_id=1, source_target_pairs={{0,256},{16,272},{32,288},{48,304},{64,320},{80,336},{96,352},{112... | collective-permute-start | bytes 49160 | tf_op jit(solution)/shard_map/ppermute | solution.py:356

commit v8 on v7

--- a/solution.py
+++ b/solution.py
@@ -10,7 +10,7 @@
 f32, bf16 = jnp.float32, jnp.bfloat16
 PAD = 8
 CAPACITY = 16
-EARLY = 2
+EARLY = 3
 NT = (((1,), (1,)), ((), ()))
 
 
@@ -20,6 +20,10 @@
 
 def held(*arrays):
     return [pltpu.with_memory_space_constraint(a, pltpu.VMEM) for a in arrays]
+
+
+def far(*arrays):
+    return [pltpu.with_memory_space_constraint(a, pltpu.HBM) for a in arrays]
 
 
 PARAMS = pltpu.CompilerParams(vmem_limit_bytes=16 * 1024 * 1024)
@@ -135,7 +139,7 @@
         forward_kernel,
         in_specs=[SCALAR, ANYWHERE] + in_vmem(1) + [ANYWHERE, ANYWHERE],
         out_specs=in_vmem(1)[0],
-        out_shape=jax.ShapeDtypeStruct((rows, 2 * width + 128), f32),
+        out_shape=pltpu.VMEM((rows, 2 * width + 128), f32),
         scratch_shapes=[
             pltpu.VMEM(x.shape, bf16),
             pltpu.VMEM((blocks, feats, 2 * width), bf16),
@@ -146,7 +150,7 @@
         ],
         compiler_params=PARAMS,
         name="forward",
-    )(core, x, gain, weight, other)
+    )(core, x, gain, *far(weight), other)
 
 
 def backward_kernel(
@@ -238,12 +242,10 @@
         ],
         compiler_params=PARAMS,
         name="backward",
-    )(core, q, got, up, upo, vec, veco, weight, other)
-
-
-def finish_kernel(back_ref, x_any, st_ref, gain_ref, target_ref, send_ref, x_ref, sem):
-    fetch = pltpu.make_async_copy(x_any, x_ref, sem)
-    fetch.start()
+    )(core, q, got, up, upo, vec, veco, *far(weight), other)
+
+
+def finish_kernel(back_ref, x_ref, st_ref, gain_ref, target_ref, send_ref):
     blocks = back_ref.shape[0]
     rows, feats = x_ref.shape
     owners = send_ref.shape[0]
@@ -255,7 +257,6 @@
     first = sums[:, 0:1] + sums[:, 1:2]
     second = sums[:, 2:3] + sums[:, 3:4]
     mean, inv_std = st_ref[:, 0:1], st_ref[:, 1:2]
-    fetch.wait()
     unit = (x_ref[...].astype(f32) - mean) * inv_std
     grad = (inv_std * (total[:rows] * gain_ref[...] - first - unit * second)).astype(bf16)
     slots = owners * CAPACITY
@@ -271,13 +272,12 @@
 def finish(back, x, st, gain, target, owners):
     return pl.pallas_call(
         finish_kernel,
-        in_specs=in_vmem(1) + [ANYWHERE] + in_vmem(3),
+        in_specs=in_vmem(5),
         out_specs=in_vmem(1)[0],
-        scratch_shapes=[pltpu.VMEM(x.shape, x.dtype), pltpu.SemaphoreType.DMA],
         out_shape=pltpu.VMEM((owners, x.shape[1] // 128 * CAPACITY, 128), bf16),
         compiler_params=PARAMS,
         name="finish",
-    )(*held(back), pltpu.with_memory_space_constraint(x, pltpu.HBM), *held(st, gain, target))
+    )(*held(back, x, st, gain, target))
 
 
 def landing_kernel(got_ref, slot_ref, o_ref):

time: 130 us -> 139 us (1.069)
  waiting for transfers between devices: 21.1 us -> 32.3 us
  blocking collectives: 36.7 us -> 30.9 us
  Pallas kernels: 12.8 us -> 14.8 us
    all_to_all x1, waiting for transfers between devices: 0.01 us -> 16.2 us  [per_device(): lax.all_to_all(parts, 'tensor', 0, 0, axis_index_groups=classes, tiled=True)]
    all_to_all x1, blocking collectives: 36.7 us -> 30.9 us  [per_device(): lax.all_to_all(send, 'dp', split_axis=0, concat_axis=0, tiled=True)]
    all_to_all x1, waiting for transfers between devices: 3.94 us -> 0.01 us  [per_device(): lax.all_to_all(sent, 'tensor', 0, 0, axis_index_groups=classes, tiled=True)]
    ppermute x5, starting transfers between devices: 23.4 us -> 20.9 us  [doubled(): return jnp.concatenate([listed, lax.ppermute(listed, 'dp', hop)], axis=0)]
    all_to_all x1, starting transfers between devices: 4.99 us -> 7.05 us  [per_device(): lax.all_to_all(parts, 'tensor', 0, 0, axis_index_groups=classes, tiled=True)]
    pallas_call x1, Pallas kernels: 3.2 us -> 5.2 us  [forward(): pl.pallas_call(forward_kernel, in_specs=[SCALAR, ANYWHERE] + in_vmem(1) +...]
    ppermute x1, starting transfers between devices: 2.74 us -> 4.45 us  [per_device(): got = lax.ppermute(q, 'tensor', swap)]
    reduce_sum x1, other arithmetic: 0.99 us -> 2.43 us  [per_device(): jnp.sum(norm_gain.reshape(chips, 2, feats, 1) * pairs.astype(f32), axis=(...]
  transfers between devices with their start and end apart: 11 -> 11, of which waited for: 6 -> 5; matrix products, arithmetic and copies ran while one was open for 5% -> 5% of each run, Pallas kernels for 2% -> 2%
where the time goes in v8:
time: 139 us; the launch traced here: 137 us
  starting transfers between devices  49 us (35%)
  waiting for transfers between devices  32.3 us (23%)
  blocking collectives  30.9 us (22%)
  Pallas kernels  14.8 us (11%)
  other arithmetic  5.94 us (4%)
  local copies, waits for them, and re-layouts  3.59 us (3%)
    all_to_all x1, blocking collectives, per_device(): lax.all_to_all(send, 'dp', split_axis=0, concat_axis=0, tiled=True)  30.9 us
    ppermute x5, starting transfers between devices, doubled(): return jnp.concatenate([listed, lax.ppermute(listed, 'dp', hop)], axis=0)  20.9 us
    all_to_all x1, waiting for transfers between devices, per_device(): lax.all_to_all(parts, 'tensor', 0, 0, axis_index_groups=classes, tiled=True)  16.2 us
    ppermute x5, waiting for transfers between devices, doubled(): return jnp.concatenate([listed, lax.ppermute(listed, 'dp', hop)], axis=0)  14.8 us
    ppermute x1, starting transfers between devices, per_device(): other = lax.ppermute(cut, 'tensor', swap)  8.73 us
    all_to_all x1, starting transfers between devices, per_device(): lax.all_to_all(parts, 'tensor', 0, 0, axis_index_groups=classes, tiled=True)  7.05 us
    pallas_call x1, Pallas kernels, backward(): pl.pallas_call(backward_kernel, in_specs=[SCALAR] + in_vmem(6) + [ANYWHER...  5.53 us
    pallas_call x1, Pallas kernels, forward(): pl.pallas_call(forward_kernel, in_specs=[SCALAR, ANYWHERE] + in_vmem(1) +...  5.2 us
  transfers between devices with their start and end apart: 11, of which 5 were waited for; matrix products, arithmetic and copies ran while one was open for 5% of the time, Pallas kernels for 2%

profile of v8, /device:TPU:1, one launch (start us, length us, event | category | flops | bytes accessed | tf_op | source)
XLA Modules:
  0.0 137.0 jit_solution(12964036769440676889)
XLA Ops:
  0.0 0.0 copy-start.3
  0.0 2.7 %dynamic-slice_bitcast_fusion = bf16[8,384,256]{2,1,0:T(8,128)(2,1)} fusion(bf16[8,2,384,256]{3,2,1,0:T(8,128)(2,1)} %bitcast.15, s32[]{:T(128)S(6)} %select_n.60), kind=kLoop, calls=%fused_computation.1 | loop fusion | bytes 3145732 | tf_op jit(solution)/shard_map/jit(dynamic_index_in_dim)/squeeze | solution.py:336
  2.7 8.7 %collective-permute-start = (bf16[8,384,256]{2,1,0:T(8,128)(2,1)}, bf16[8,384,256]{2,1,0:T(8,128)(2,1)S(1)}, u32[]{:S(2)}, u32[]{:S(2)}) collective-permute-start(bf16[8,384,256]{2,1,0:T(8,128)(2,1)} %dynamic-slice_bitcast_fusion), channel_id=1, source_target_pairs={{0,1},{1,0},{2,3},{3,2},{4,5},{5,4},{6,7},{7,6},{8,9},{9,8},{10,11... | collective-permute-start | bytes 4718600 | tf_op jit(solution)/shard_map/ppermute | solution.py:337
  11.4 0.0 copy-done.3
  11.4 1.9 %collective-permute-start.3 = (s32[1,256]{1,0:T(1,128)S(1)}, s32[1,256]{1,0:T(1,128)S(1)}, u32[]{:S(2)}, u32[]{:S(2)}) collective-permute-start(s32[1,256]{1,0:T(1,128)S(1)} %bitcast.19), channel_id=1, source_target_pairs={{0,16},{16,32},{32,48},{48,64},{64,80},{80,96},{96,112},{112,128},... | collective-permute-start | bytes 3080 | tf_op jit(solution)/shard_map/ppermute | solution.py:356
  13.4 2.2 %spread.1 = bf16[8,256,384]{2,1,0:T(8,128)(2,1)} custom-call(bf16[256,384]{1,0:T(8,128)(2,1)} %x_ref.1), custom_call_target="tpu_custom_call" | custom-call | tf_op jit(solution)/shard_map/spread/pallas_call | solution.py:62
  15.6 0.0 copy-start.2
  15.6 3.6 %all-to-all-start = ((bf16[8,256,384]{2,1,0:T(8,128)(2,1)}), bf16[8,256,384]{2,1,0:T(8,128)(2,1)S(1)}, u32[]{:S(2)}, u32[]{:S(2)}) async-start(bf16[8,256,384]{2,1,0:T(8,128)(2,1)} %spread.1), calls=%async_computation | async-start | bytes 3145728 | tf_op jit(solution)/shard_map/all_to_all | solution.py:333
  19.2 0.0 copy-done.2
  19.2 0.0 copy-start.5
  19.2 0.0 copy-start.1
  19.2 2.4 %multiply_reduce_fusion = f32[2,256]{1,0:T(2,128)S(1)} fusion(bf16[8,2,384,256]{3,2,1,0:T(8,128)(2,1)} %bitcast.16, f32[8,2,384]{2,1,0:T(2,128)S(1)} %mul.16), kind=kLoop, calls=%fused_computation | loop fusion | flops 4718080 | bytes 3172352 | tf_op jit(solution)/shard_map/reduce_sum | solution.py:340
  21.7 0.0 copy-done.5
  21.7 1.9 %collective-permute-start.2 = (f32[3,256]{1,0:T(4,128)S(1)}, f32[3,256]{1,0:T(4,128)S(1)}, u32[]{:S(2)}, u32[]{:S(2)}) collective-permute-start(f32[3,256]{1,0:T(4,128)S(1)} %pad_maximum_fusion.vec_ref), channel_id=1, source_target_pairs={{0,1},{1,0},{2,3},{3,2},{4,5},{5,4},{6,7},{7,6},{8,9},{9,8},{10,11... | collective-permute-start | bytes 9224 | tf_op jit(solution)/shard_map/ppermute | solution.py:342
  23.6 0.0 copy-done.1
  23.6 2.4 %collective-permute-start.1 = (bf16[256,256]{1,0:T(8,128)(2,1)S(1)}, bf16[256,256]{1,0:T(8,128)(2,1)S(1)}, u32[]{:S(2)}, u32[]{:S(2)}) collective-permute-start(bf16[256,256]{1,0:T(8,128)(2,1)S(1)} %copy-done.1), channel_id=1, source_target_pairs={{0,1},{1,0},{2,3},{3,2},{4,5},{5,4},{6,7},{7,6},{8,9},{9,8},{10,11... | collective-permute-start | bytes 393224 | tf_op jit(solution)/shard_map/ppermute | solution.py:338
  26.1 0.2 convert_reduce_fusion
  26.2 0.0 collective-permute-done.3
  26.3 4.3 %collective-permute-start.4 = (s32[2,256]{1,0:T(2,128)S(1)}, s32[2,256]{1,0:T(2,128)S(1)}, u32[]{:S(2)}, u32[]{:S(2)}) collective-permute-start(s32[2,256]{1,0:T(2,128)S(1)} %pad_add_fusion.3), channel_id=1, source_target_pairs={{0,32},{16,48},{32,64},{48,80},{64,96},{80,112},{96,128},{112,144}... | collective-permute-start | bytes 6152 | tf_op jit(solution)/shard_map/ppermute | solution.py:356
  30.6 6.8 %collective-permute-done.4 = s32[2,256]{1,0:T(2,128)S(1)} collective-permute-done((s32[2,256]{1,0:T(2,128)S(1)}, s32[2,256]{1,0:T(2,128)S(1)}, u32[]{:S(2)}, u32[]{:S(2)}) %collective-permute-start.4) | collective-permute-done | bytes 2080 | tf_op jit(solution)/shard_map/ppermute | solution.py:356
  37.5 3.8 %collective-permute-start.5 = (s32[4,256]{1,0:T(4,128)S(1)}, s32[4,256]{1,0:T(4,128)S(1)}, u32[]{:S(2)}, u32[]{:S(2)}) collective-permute-start(s32[4,256]{1,0:T(4,128)S(1)} %pad_add_fusion.2), channel_id=1, source_target_pairs={{0,64},{16,80},{32,96},{48,112},{64,128},{80,144},{96,160},{112,17... | collective-permute-start | bytes 12296 | tf_op jit(solution)/shard_map/ppermute | solution.py:356
  41.3 5.3 %collective-permute-done.5 = s32[4,256]{1,0:T(4,128)S(1)} collective-permute-done((s32[4,256]{1,0:T(4,128)S(1)}, s32[4,256]{1,0:T(4,128)S(1)}, u32[]{:S(2)}, u32[]{:S(2)}) %collective-permute-start.5) | collective-permute-done | bytes 4128 | tf_op jit(solution)/shard_map/ppermute | solution.py:356
  46.6 0.6 pad_add_fusion.1
  47.2 0.0 collective-permute-done.2.veco_ref
  47.2 0.0 collective-permute-done.1.upo_ref
  47.2 0.0 all-to-all-done.x_any
  47.2 0.0 collective-permute-done.other_any
  47.2 5.2 %forward.1.q_ref = f32[256,640]{1,0:T(8,128)} custom-call(s32[1]{0:T(128)} %bitcast.core_ref, bf16[8,256,384]{2,1,0:T(8,128)(2,1)S(1)} %all-to-all-done.x_any, f32[8,2,1,384]{3,2,1,0:T(1,128)S(1)} %bitcast.13, bf16[8,2,384,256]{3,2,1,0:T(8,128)(2,1)} %bitcast.17, bf16[8,384,256]{2,1,0:T(8,128)(2,1)S(1)} %collective-permute-done.other_any), custom_call_target="tpu_custom_call" | custom-call | tf_op jit(solution)/shard_map/forward/pallas_call | solution.py:138
  52.5 4.4 %collective-permute-start.6 = (f32[256,640]{1,0:T(8,128)}, f32[256,640]{1,0:T(8,128)S(1)}, u32[]{:S(2)}, u32[]{:S(2)}) collective-permute-start(f32[256,640]{1,0:T(8,128)} %forward.1.q_ref), channel_id=1, source_target_pairs={{0,1},{1,0},{2,3},{3,2},{4,5},{5,4},{6,7},{7,6},{8,9},{9,8},{10,11... | collective-permute-start | bytes 1966088 | tf_op jit(solution)/shard_map/ppermute | solution.py:368
  56.9 0.7 iota_compare_fusion.4
  57.6 1.2 collective-permute-done.6.got_ref
  58.8 5.5 %backward.1 = (bf16[8,264,384]{2,1,0:T(8,128)(2,1)}, f32[256,128]{1,0:T(8,128)S(1)}) custom-call(s32[1]{0:T(128)} %bitcast.core_ref, f32[256,640]{1,0:T(8,128)} %forward.1.q_ref, f32[256,640]{1,0:T(8,128)S(1)} %collective-permute-done.6.got_ref, bf16[256,256]{1,0:T(8,128)(2,1)S(1)} %copy-done.1, bf16[256,256]{1,0:T(8,128)(2,1)S(1)} %collective-permute-done.1.upo_ref, ...), custom_call_target="tpu_custom_call" | custom-call | tf_op jit(solution)/shard_map/backward/pallas_call | solution.py:228
  64.4 8.6 %collective-permute-start.7 = (s32[8,256]{1,0:T(8,128)}, s32[8,256]{1,0:T(8,128)S(1)}, u32[]{:S(2)}, u32[]{:S(2)}) collective-permute-start(s32[8,256]{1,0:T(8,128)} %pad_add_fusion.1), channel_id=1, source_target_pairs={{0,128},{16,144},{32,160},{48,176},{64,192},{80,208},{96,224},{112... | collective-permute-start | bytes 24584 | tf_op jit(solution)/shard_map/ppermute | solution.py:356
  72.9 0.7 constant_dynamic-update-slice_fusion.2
  73.6 0.0 copy-start.4
  73.6 0.0 copy-start
  73.7 7.0 %all-to-all-start.1 = ((bf16[8,264,384]{2,1,0:T(8,128)(2,1)}), bf16[8,264,384]{2,1,0:T(8,128)(2,1)S(1)}, u32[]{:S(2)}, u32[]{:S(2)}) async-start(bf16[8,264,384]{2,1,0:T(8,128)(2,1)} %get-tuple-element.24), calls=%async_computation.1 | async-start | bytes 3244032 | tf_op jit(solution)/shard_map/all_to_all | solution.py:371
  80.7 0.0 collective-permute-done.7
  80.7 0.7 pad_add_fusion
  81.4 2.3 %collective-permute-start.8 = (s32[16,256]{1,0:T(8,128)S(1)}, s32[16,256]{1,0:T(8,128)S(1)}, u32[]{:S(2)}, u32[]{:S(2)}) collective-permute-start(s32[16,256]{1,0:T(8,128)S(1)} %pad_add_fusion), channel_id=1, source_target_pairs={{0,256},{16,272},{32,288},{48,304},{64,320},{80,336},{96,352},{112... | collective-permute-start | bytes 49160 | tf_op jit(solution)/shard_map/ppermute | solution.py:356
  83.7 2.6 %collective-permute-done.8 = s32[16,256]{1,0:T(8,128)S(1)} collective-permute-done((s32[16,256]{1,0:T(8,128)S(1)}, s32[16,256]{1,0:T(8,128)S(1)}, u32[]{:S(2)}, u32[]{:S(2)}) %collective-permute-start.8) | collective-permute-done | bytes 16416 | tf_op jit(solution)/shard_map/ppermute | solution.py:356
  86.4 0.2 convolution_convert_fusion
  86.6 0.6 select_reduce_fusion
  87.2 0.1 copy.8
  87.3 0.0 copy-done.4
  87.3 0.6 select_reduce_fusion.1
  87.9 0.1 reshape.236.slot_ref
  88.0 16.2 %all-to-all-done.1.back_ref = bf16[8,264,384]{2,1,0:T(8,128)(2,1)S(1)} async-done(((bf16[8,264,384]{2,1,0:T(8,128)(2,1)}), bf16[8,264,384]{2,1,0:T(8,128)(2,1)S(1)}, u32[]{:S(2)}, u32[]{:S(2)}) %all-to-all-start.1) | async-done | bytes 1622048 | tf_op jit(solution)/shard_map/all_to_all | solution.py:371
  104.2 0.0 copy-done
  104.2 0.8 finish.1
  105.0 30.9 %all_to_all.15.got_ref = bf16[32,48,128]{2,1,0:T(8,128)(2,1)S(1)} all-to-all(bf16[32,48,128]{2,1,0:T(8,128)(2,1)S(1)} %finish.1), channel_id=1, replica_groups=mesh['dp'=32,'tensor'=16] {'dp'}, dimensions={0} | all-to-all | bytes 786432 | tf_op jit(solution)/shard_map/all_to_all | solution.py:377
  135.9 1.1 land.1
  (13 shorter events, 0.2 us)
Async XLA Ops:
  0.0 11.4 %copy-start.3 = (s32[256]{0:T(256)S(1)}, s32[256]{0:T(256)}, u32[]{:S(2)}) copy-start(s32[256]{0:T(256)} %param.11) | copy-start | bytes 3076
  2.7 44.6 %collective-permute-start = (bf16[8,384,256]{2,1,0:T(8,128)(2,1)}, bf16[8,384,256]{2,1,0:T(8,128)(2,1)S(1)}, u32[]{:S(2)}, u32[]{:S(2)}) collective-permute-start(bf16[8,384,256]{2,1,0:T(8,128)(2,1)} %dynamic-slice_bitcast_fusion), channel_id=1, source_target_pairs={{0,1},{1,0},{2,3},{3,2},{4,5},{5,4},{6,7},{7,6},{8,9},{9,8},{10,11... | collective-permute-start | bytes 4718600 | tf_op jit(solution)/shard_map/ppermute | solution.py:337
  11.4 14.8 %collective-permute-start.3 = (s32[1,256]{1,0:T(1,128)S(1)}, s32[1,256]{1,0:T(1,128)S(1)}, u32[]{:S(2)}, u32[]{:S(2)}) collective-permute-start(s32[1,256]{1,0:T(1,128)S(1)} %bitcast.19), channel_id=1, source_target_pairs={{0,16},{16,32},{32,48},{48,64},{64,80},{80,96},{96,112},{112,128},... | collective-permute-start | bytes 3080 | tf_op jit(solution)/shard_map/ppermute | solution.py:356
  15.6 3.6 %copy-start.2 = (f32[6144]{0:T(1024)S(1)}, f32[6144]{0:T(1024)}, u32[]{:S(2)}) copy-start(f32[6144]{0:T(1024)} %param.10) | copy-start | bytes 73732
  15.6 31.6 %all-to-all-start = ((bf16[8,256,384]{2,1,0:T(8,128)(2,1)}), bf16[8,256,384]{2,1,0:T(8,128)(2,1)S(1)}, u32[]{:S(2)}, u32[]{:S(2)}) async-start(bf16[8,256,384]{2,1,0:T(8,128)(2,1)} %spread.1), calls=%async_computation | async-start | bytes 3145728 | tf_op jit(solution)/shard_map/all_to_all | solution.py:333
  19.2 2.5 %copy-start.5 = (f32[256]{0:T(256)S(1)}, f32[256]{0:T(256)}, u32[]{:S(2)}) copy-start(f32[256]{0:T(256)} %param.9) | copy-start | bytes 3076
  19.2 4.4 %copy-start.1 = (bf16[256,256]{1,0:T(8,128)(2,1)S(1)}, bf16[256,256]{1,0:T(8,128)(2,1)}, u32[]{:S(2)}) copy-start(bf16[256,256]{1,0:T(8,128)(2,1)} %up_ref.1) | copy-start | bytes 393220
  21.7 25.5 %collective-permute-start.2 = (f32[3,256]{1,0:T(4,128)S(1)}, f32[3,256]{1,0:T(4,128)S(1)}, u32[]{:S(2)}, u32[]{:S(2)}) collective-permute-start(f32[3,256]{1,0:T(4,128)S(1)} %pad_maximum_fusion.vec_ref), channel_id=1, source_target_pairs={{0,1},{1,0},{2,3},{3,2},{4,5},{5,4},{6,7},{7,6},{8,9},{9,8},{10,11... | collective-permute-start | bytes 9224 | tf_op jit(solution)/shard_map/ppermute | solution.py:342
  23.6 23.6 %collective-permute-start.1 = (bf16[256,256]{1,0:T(8,128)(2,1)S(1)}, bf16[256,256]{1,0:T(8,128)(2,1)S(1)}, u32[]{:S(2)}, u32[]{:S(2)}) collective-permute-start(bf16[256,256]{1,0:T(8,128)(2,1)S(1)} %copy-done.1), channel_id=1, source_target_pairs={{0,1},{1,0},{2,3},{3,2},{4,5},{5,4},{6,7},{7,6},{8,9},{9,8},{10,11... | collective-permute-start | bytes 393224 | tf_op jit(solution)/shard_map/ppermute | solution.py:338
  26.3 11.2 %collective-permute-start.4 = (s32[2,256]{1,0:T(2,128)S(1)}, s32[2,256]{1,0:T(2,128)S(1)}, u32[]{:S(2)}, u32[]{:S(2)}) collective-permute-start(s32[2,256]{1,0:T(2,128)S(1)} %pad_add_fusion.3), channel_id=1, source_target_pairs={{0,32},{16,48},{32,64},{48,80},{64,96},{80,112},{96,128},{112,144}... | collective-permute-start | bytes 6152 | tf_op jit(solution)/shard_map/ppermute | solution.py:356
  37.5 9.2 %collective-permute-start.5 = (s32[4,256]{1,0:T(4,128)S(1)}, s32[4,256]{1,0:T(4,128)S(1)}, u32[]{:S(2)}, u32[]{:S(2)}) collective-permute-start(s32[4,256]{1,0:T(4,128)S(1)} %pad_add_fusion.2), channel_id=1, source_target_pairs={{0,64},{16,80},{32,96},{48,112},{64,128},{80,144},{96,160},{112,17... | collective-permute-start | bytes 12296 | tf_op jit(solution)/shard_map/ppermute | solution.py:356
  52.5 6.4 %collective-permute-start.6 = (f32[256,640]{1,0:T(8,128)}, f32[256,640]{1,0:T(8,128)S(1)}, u32[]{:S(2)}, u32[]{:S(2)}) collective-permute-start(f32[256,640]{1,0:T(8,128)} %forward.1.q_ref), channel_id=1, source_target_pairs={{0,1},{1,0},{2,3},{3,2},{4,5},{5,4},{6,7},{7,6},{8,9},{9,8},{10,11... | collective-permute-start | bytes 1966088 | tf_op jit(solution)/shard_map/ppermute | solution.py:368
  64.4 16.3 %collective-permute-start.7 = (s32[8,256]{1,0:T(8,128)}, s32[8,256]{1,0:T(8,128)S(1)}, u32[]{:S(2)}, u32[]{:S(2)}) collective-permute-start(s32[8,256]{1,0:T(8,128)} %pad_add_fusion.1), channel_id=1, source_target_pairs={{0,128},{16,144},{32,160},{48,176},{64,192},{80,208},{96,224},{112... | collective-permute-start | bytes 24584 | tf_op jit(solution)/shard_map/ppermute | solution.py:356
  73.6 13.6 %copy-start.4 = (pred[32,32]{1,0:T(8,128)(4,1)S(1)}, pred[32,32]{1,0:T(8,128)(4,1)}, u32[]{:S(2)}) copy-start(pred[32,32]{1,0:T(8,128)(4,1)} %iota_compare_fusion.4) | copy-start | bytes 3076
  73.6 30.6 %copy-start = (bf16[256,384]{1,0:T(8,128)(2,1)S(1)}, bf16[256,384]{1,0:T(8,128)(2,1)}, u32[]{:S(2)}) copy-start(bf16[256,384]{1,0:T(8,128)(2,1)} %x_ref.1) | copy-start | bytes 589828
  73.7 30.6 %all-to-all-start.1 = ((bf16[8,264,384]{2,1,0:T(8,128)(2,1)}), bf16[8,264,384]{2,1,0:T(8,128)(2,1)S(1)}, u32[]{:S(2)}, u32[]{:S(2)}) async-start(bf16[8,264,384]{2,1,0:T(8,128)(2,1)} %get-tuple-element.24), calls=%async_computation.1 | async-start | bytes 3244032 | tf_op jit(solution)/shard_map/all_to_all | solution.py:371
  81.4 4.9 %collective-permute-start.8 = (s32[16,256]{1,0:T(8,128)S(1)}, s32[16,256]{1,0:T(8,128)S(1)}, u32[]{:S(2)}, u32[]{:S(2)}) collective-permute-start(s32[16,256]{1,0:T(8,128)S(1)} %pad_add_fusion), channel_id=1, source_target_pairs={{0,256},{16,272},{32,288},{48,304},{64,320},{80,336},{96,352},{112... | collective-permute-start | bytes 49160 | tf_op jit(solution)/shard_map/ppermute | solution.py:356
